TPU v7x, 32 devices: a whole 2x2x4 slice. The times are simulated.
32 devices in a mesh: gx: 4 (over x, core), gy: 8 (over z, y).
Axes of the slice: x: 2, y: 2, z: 4, core: 2. Of those that a mesh axis runs over, the one named last changes fastest.
Arguments:
- rock_type: int32 [64, 256, 512], P('gx', 'gy'), may hold values from 0 to 7
- rock_perm: float32 [8], replicated, may hold values from 0.05 to 0.5
- rock_poro: float32 [8], replicated, may hold values from 0.1 to 0.35
- base_flux: float32 [64, 256, 512], P('gx', 'gy'), may hold values from 0.5 to 2
- initial_pressure: float32 [64, 256, 512], P('gx', 'gy'), may hold values from -6 to 6
- old_saturation: float32 [64, 256, 512], P('gx', 'gy'), may hold values from 0 to 1
- well_cells: int32 [3, 128], replicated, may hold values from 0 to 511, as said below
- well_rates: float32 [128], replicated, may hold values from -2 to 2
Outputs:
- pressure: float32 [64, 256, 512], P('gx', 'gy')
- saturation: float32 [64, 256, 512], P('gx', 'gy')
Inputs may be any that keep to these rules, and one draw needn't show every extreme that they name: `well_cells`: row 0 holds first coordinates below 64, row 1 second coordinates below 256, row 2 third coordinates below 512. The first well lies in the last cell of the grid and the second in the first cell; wells may share a cell.
All inputs are finite; a program needn't handle non-finite values.
Results may differ from a plain program's by a relative error of at most 0.0003.
Values sent between devices are 32-bit elements; how exact they have to be, the bound alone decides.
No kernel may reach another device: no remote copies, remote signals or barrier semaphores. Data moves between devices by JAX's collectives and lax.ppermute only.
A program may use at most 64 MiB of HBM per device.

v0:
```python
import jax
import jax.numpy as jnp
from jax import lax
from jax.sharding import PartitionSpec as P

PASSES = 4
NEWTON = 3


MOBILITY = 0.5
OMEGA = 0.8
VOLUME = 4.0
COMPRESS = 0.5


def padded(block, sides, width):
    for axis, dim in sides:
        count = lax.axis_size(axis)
        forward = [(i, i + 1) for i in range(count - 1)]
        backward = [(target, source) for source, target in forward]
        low = lax.ppermute(
            lax.slice_in_dim(block, block.shape[dim] - width, None, axis=dim), axis, forward
        )
        high = lax.ppermute(lax.slice_in_dim(block, 0, width, axis=dim), axis, backward)
        block = jnp.concatenate([low, block, high], axis=dim)
    return block


def passed_along(value, axis, by):
    length = lax.axis_size(axis)
    pairs = [(i, i + by) for i in range(length) if 0 <= i + by < length]
    return lax.ppermute(value, axis, pairs)


def fraction(water):
    denom = water * water + MOBILITY * (1.0 - water) ** 2
    return water * water / denom


def fraction_slope(water):
    denom = water * water + MOBILITY * (1.0 - water) ** 2
    return 2.0 * MOBILITY * water * (1.0 - water) / (denom * denom)


def transmit(left, right):
    total = left + right
    return 2.0 * left * right / jnp.where(total > 0, total, 1.0)


def along_depth(field):
    deeper = jnp.pad(field[:, :, 1:], ((0, 0), (0, 0), (0, 1)))
    shallower = jnp.pad(field[:, :, :-1], ((0, 0), (0, 0), (1, 0)))
    return (deeper, shallower)


def links(perm_ext):
    center = perm_ext[1:-1, 1:-1]
    deeper, shallower = along_depth(center)
    return (
        transmit(center, perm_ext[2:, 1:-1]),
        transmit(center, perm_ext[:-2, 1:-1]),
        transmit(center, perm_ext[1:-1, 2:]),
        transmit(center, perm_ext[1:-1, :-2]),
        transmit(center, deeper),
        transmit(center, shallower),
    )


def jacobi(press_ext, perm_ext, storage, source):
    east, west, north, south, below, above = links(perm_ext)
    center = press_ext[1:-1, 1:-1]
    deeper, shallower = along_depth(center)
    flow = (
        east * (center - press_ext[2:, 1:-1])
        + west * (center - press_ext[:-2, 1:-1])
        + north * (center - press_ext[1:-1, 2:])
        + south * (center - press_ext[1:-1, :-2])
        + below * (center - deeper)
        + above * (center - shallower)
    )
    outside = jnp.where(perm_ext[1:-1, 1:-1] > 0, 0.0, 1.0)
    diagonal = storage + east + west + north + south + below + above + outside
    return center + OMEGA * (source - storage * center - flow) / diagonal


def upwind(flux, own, other):
    return jnp.maximum(flux, 0.0) * own + jnp.minimum(flux, 0.0) * other


def water_terms(press_ext, perm_ext, frac_old, frac_side, base_flux, rates_field):
    east, west, north, south, below, above = links(perm_ext)
    center = press_ext[1:-1, 1:-1]
    deeper, shallower = along_depth(center)
    frac_deep, frac_shallow = along_depth(frac_old)
    through = jnp.maximum(base_flux + east * (center - press_ext[2:, 1:-1]), 0.0)
    leaving = (
        upwind(north * (center - press_ext[1:-1, 2:]), frac_old, frac_side[:, 2:])
        + upwind(south * (center - press_ext[1:-1, :-2]), frac_old, frac_side[:, :-2])
        + upwind(below * (center - deeper), frac_old, frac_deep)
        + upwind(above * (center - shallower), frac_old, frac_shallow)
    )
    explicit = jnp.maximum(rates_field, 0.0) + jnp.minimum(rates_field, 0.0) * frac_old - leaving
    return (through, explicit)


def sweep(inflow, volume, through, explicit, old_sat):

    def advance(incoming, items):
        vol_row, flux_row, extra_row, start_row = items
        water = start_row
        for _ in range(NEWTON):
            misfit = (
                vol_row * (water - start_row) + flux_row * fraction(water) - incoming - extra_row
            )
            water = jnp.clip(
                water - misfit / (vol_row + flux_row * fraction_slope(water)), 0.0, 1.0
            )
        return (flux_row * fraction(water), water)

    outgoing, saturation = lax.scan(advance, inflow, (volume, through, explicit, old_sat))
    return (saturation, outgoing)


def lookup(rock_type, table):
    result = jnp.zeros(rock_type.shape, table.dtype)
    for kind in range(table.shape[0]):
        result = jnp.where(rock_type == kind, table[kind], result)
    return result


def well_field(well_cells, well_rates, shape, anchor_x, anchor_y):
    local_x = well_cells[0] - anchor_x
    local_y = well_cells[1] - anchor_y
    local_z = well_cells[2]
    inside = (
        (local_x >= 0)
        & (local_x < shape[0])
        & (local_y >= 0)
        & (local_y < shape[1])
        & (local_z >= 0)
        & (local_z < shape[2])
    )
    count = shape[0] * shape[1] * shape[2]
    flat = jnp.where(inside, (local_x * shape[1] + local_y) * shape[2] + local_z, count)
    return (
        jnp.zeros((count,), well_rates.dtype).at[flat].add(well_rates, mode="drop").reshape(shape)
    )


def shards(
    rock_type,
    rock_perm,
    rock_poro,
    base_flux,
    initial_pressure,
    old_saturation,
    well_cells,
    well_rates,
):
    shape = rock_type.shape
    depth_cells = shape[2]
    rank_x = lax.axis_index("gx")
    anchor_x = rank_x * shape[0]
    anchor_y = lax.axis_index("gy") * shape[1]
    perm = lookup(rock_type, rock_perm)
    volume = VOLUME * lookup(rock_type, rock_poro)
    storage = COMPRESS * volume
    rates_field = well_field(well_cells, well_rates, shape, anchor_x, anchor_y)
    source = storage * initial_pressure + rates_field
    pressure = initial_pressure
    perm_ext = padded(perm, (("gx", 0), ("gy", 1)), 1)
    for _ in range(PASSES):
        press_ext = padded(pressure, (("gx", 0), ("gy", 1)), 1)
        pressure = jacobi(press_ext, perm_ext, storage, source)
    side_ext = padded(pressure, (("gy", 1),), 1)
    next_layer = passed_along(pressure[:1], "gx", -1)
    next_wide = jnp.pad(next_layer, ((0, 0), (1, 1), (0, 0)))
    press_ext = jnp.concatenate([jnp.zeros_like(next_wide), side_ext, next_wide], axis=0)
    frac_old = fraction(old_saturation)
    frac_side = padded(frac_old, (("gy", 1),), 1)
    through, explicit = water_terms(
        press_ext, perm_ext, frac_old, frac_side, base_flux, rates_field
    )
    inlet = base_flux[0]
    upstream_end = rank_x == 0
    width = min(128, depth_cells)
    count = depth_cells // width

    def turn(step, carry):
        current, arriving = carry
        offset = step - rank_x
        active = (offset >= 0) & (offset < count)
        start = jnp.clip(offset, 0, count - 1) * width

        def pick(field):
            return lax.dynamic_slice_in_dim(field, start, width, 2)

        inflow = jnp.where(upstream_end, lax.dynamic_slice_in_dim(inlet, start, width, 1), arriving)
        fresh, outgoing = sweep(
            inflow, pick(volume), pick(through), pick(explicit), pick(old_saturation)
        )
        kept = pick(current)
        current = lax.dynamic_update_slice_in_dim(current, jnp.where(active, fresh, kept), start, 2)
        arriving = passed_along(outgoing, "gx", 1)
        return (current, arriving)

    empty = jnp.zeros((shape[1], width), old_saturation.dtype)
    saturation, _ = lax.fori_loop(0, lax.axis_size("gx") + count - 1, turn, (old_saturation, empty))
    return (pressure, saturation)


def solution(mesh):
    return jax.shard_map(
        shards,
        mesh=mesh,
        in_specs=(
            P("gx", "gy", None),
            P(),
            P(),
            P("gx", "gy", None),
            P("gx", "gy", None),
            P("gx", "gy", None),
            P(),
            P(),
        ),
        out_specs=(P("gx", "gy", None), P("gx", "gy", None)),
        check_vma=False,
    )
```

profile of v0, /device:TPU:14, one launch (start us, length us, event | category | flops | bytes accessed | tf_op | source)
XLA Modules:
  0.0 217.9 jit_solution(17249930125373245590)
XLA Ops:
  3.9 9.0 %broadcast_multiply_fusion = (f32[16,32,512]{2,1,0:T(8,128)}, f32[16,32,512]{2,1,0:T(8,128)}, pred[16,32,512]{2,1,0:T(8,128)(4,1)S(1)}, pred[16,32,512]{2,1,0:T(...) fusion(f32[]{:T(128)} %bitcast.12, f32[]{:T(128)} %bitcast.11, ...), kind=kLoop, calls=%fused_computation.214 | loop fusion | flops 4456448 | bytes 5242912 | tf_op jit(solution)/shard_map/mul | solution.py:166
  12.9 5.8 %select_select_fusion = f32[16,32,512]{2,1,0:T(8,128)S(1)} fusion(pred[16,32,512]{2,1,0:T(8,128)(4,1)S(1)} %get-tuple-element.255, pred[16,32,512]{2,1,0:T(8,128)(4,1)S(1)} %get-tuple-element.254, pred[16,32,512]{2,1,0:T(8,128)(4,1)S(1)} %get-tuple-element.253, pred[16,32,512]{2,1,0:T(8,128)(4,1)S(1)} %get-tuple-element.252, ...), kind=kLoop, calls=%fused_computation.210 | loop fusion | flops 2097152 | bytes 3145760 | tf_op jit(solution)/shard_map/jit(_where)/select_n | solution.py:127
  18.7 1.9 collective-permute-start.1
  20.6 2.4 %collective-permute-start.3 = (f32[1,32,512]{2,1,0:T(8,128)S(1)}, f32[1,32,512]{2,1,0:T(8,128)S(1)}, u32[]{:S(2)}, u32[]{:S(2)}) collective-permute-start(f32[1,32,512]{2,1,0:T(8,128)S(1)} %get-tuple-element.297), channel_id=1, source_target_pairs={{0,8},{8,16},{16,24},{1,9},{9,17},{17,25},{2,10},{10,18},{18,26},{... | collective-permute-start | bytes 196616 | tf_op jit(solution)/shard_map/ppermute | solution.py:21
  25.6 3.8 %collective-permute-start.2 = (f32[1,32,512]{2,1,0:T(8,128)}, f32[1,32,512]{2,1,0:T(8,128)}, u32[]{:S(2)}, u32[]{:S(2)}) collective-permute-start(f32[1,32,512]{2,1,0:T(8,128)} %get-tuple-element.300), channel_id=1, source_target_pairs={{8,0},{16,8},{24,16},{9,1},{17,9},{25,17},{10,2},{18,10},{26,18},{... | collective-permute-start | bytes 196616 | tf_op jit(solution)/shard_map/ppermute | solution.py:24
  29.4 2.6 %fusion.149 = (f32[16,32,511]{2,1,0:T(8,128)}, f32[16,32,511]{2,1,0:T(8,128)}, f32[16,32,511]{2,1,0:T(8,128)}, f32[16,32,511]{2,1,0:T(8,128)}) fusion(f32[16,32,512]{2,1,0:T(8,128)S(1)} %select_select_fusion, f32[16,32,512]{2,1,0:T(8,128)S(1)} %copy-done), kind=kLoop, calls=%fused_computation.256 | loop fusion | bytes 8372224 | tf_op jit(solution)/shard_map/slice | solution.py:52
  34.0 2.4 %collective-permute-start.5 = (f32[18,1,512]{2,1,0:T(1,128)}, f32[18,1,512]{2,1,0:T(1,128)S(1)}, u32[]{:S(2)}, u32[]{:S(2)}) collective-permute-start(f32[18,1,512]{2,1,0:T(1,128)} %get-tuple-element.270), channel_id=1, source_target_pairs={{1,0},{2,1},{3,2},{4,3},{5,4},{6,5},{7,6},{9,8},{10,9},{11,10},{12... | collective-permute-start | bytes 110600 | tf_op jit(solution)/shard_map/ppermute | solution.py:24
  36.4 4.3 %collective-permute-start.7 = (f32[18,1,512]{2,1,0:T(1,128)}, f32[18,1,512]{2,1,0:T(1,128)S(1)}, u32[]{:S(2)}, u32[]{:S(2)}) collective-permute-start(f32[18,1,512]{2,1,0:T(1,128)} %get-tuple-element.271), channel_id=1, source_target_pairs={{0,1},{1,2},{2,3},{3,4},{4,5},{5,6},{6,7},{8,9},{9,10},{10,11},{11... | collective-permute-start | bytes 110600 | tf_op jit(solution)/shard_map/ppermute | solution.py:21
  44.5 4.8 %collective-permute-start.8 = (f32[18,1,512]{2,1,0:T(1,128)}, f32[18,1,512]{2,1,0:T(1,128)S(1)}, u32[]{:S(2)}, u32[]{:S(2)}) collective-permute-start(f32[18,1,512]{2,1,0:T(1,128)} %get-tuple-element.273), channel_id=1, source_target_pairs={{0,1},{1,2},{2,3},{3,4},{4,5},{5,6},{6,7},{8,9},{9,10},{10,11},{11... | collective-permute-start | bytes 110600 | tf_op jit(solution)/shard_map/ppermute | solution.py:21
  49.8 2.5 %scatter_custom_fusion = f32[262144]{0:T(1024)} fusion(s32[128]{0:T(128)} %fusion.134, f32[128]{0:T(128)} %param.19, f32[]{:T(128)} %constant.108.clone.1), kind=kCustom, calls=%fused_computation.215 | custom fusion | flops 128 | bytes 1049088 | tf_op jit(solution)/shard_map/scatter-add | solution.py:146
  54.4 6.7 %fusion.114 = (f32[16,32,512]{2,1,0:T(8,128)S(1)}, f32[16,32,512]{2,1,0:T(8,128)S(1)}, f32[16,32,512]{2,1,0:T(8,128)S(1)}, pred[16,32,512]{2,1,0:T(8,128)(4,1)S(1)}) fusion(f32[16,32,512]{2,1,0:T(8,128)S(1)} %copy-done, f32[18,32,512]{2,1,0:T(8,128)} %copy-done.18, f32[18,1,512]{2,1,0:T(1,128)} %copy-done.28, f32[18,1,512]{2,1,0:T(1,128)} %copy-done.27, ...), kind=kLoop, calls=%fused_computation.181 | loop fusion | flops 20185088 | bytes 13377536 | tf_op jit(solution)/shard_map/add | solution.py:83
  61.1 1.9 collective-permute-start.10
  63.1 3.6 %collective-permute-start.9 = (f32[1,32,512]{2,1,0:T(8,128)S(1)}, f32[1,32,512]{2,1,0:T(8,128)S(1)}, u32[]{:S(2)}, u32[]{:S(2)}) collective-permute-start(f32[1,32,512]{2,1,0:T(8,128)S(1)} %get-tuple-element.293), channel_id=1, source_target_pairs={{8,0},{16,8},{24,16},{9,1},{17,9},{25,17},{10,2},{18,10},{26,18},{... | collective-permute-start | bytes 196616 | tf_op jit(solution)/shard_map/ppermute | solution.py:24
  69.3 4.8 %collective-permute-start.25 = (f32[16,1,512]{2,1,0:T(1,128)}, f32[16,1,512]{2,1,0:T(1,128)}, u32[]{:S(2)}, u32[]{:S(2)}) collective-permute-start(f32[16,1,512]{2,1,0:T(1,128)} %get-tuple-element.279), channel_id=1, source_target_pairs={{0,1},{1,2},{2,3},{3,4},{4,5},{5,6},{6,7},{8,9},{9,10},{10,11},{11... | collective-permute-start | bytes 98312 | tf_op jit(solution)/shard_map/ppermute | solution.py:21
  74.2 1.9 collective-permute-start.11
  76.2 5.0 %collective-permute-start.12 = (f32[18,1,512]{2,1,0:T(1,128)S(1)}, f32[18,1,512]{2,1,0:T(1,128)S(1)}, u32[]{:S(2)}, u32[]{:S(2)}) collective-permute-start(f32[18,1,512]{2,1,0:T(1,128)S(1)} %get-tuple-element.269), channel_id=1, source_target_pairs={{0,1},{1,2},{2,3},{3,4},{4,5},{5,6},{6,7},{8,9},{9,10},{10,11},{11... | collective-permute-start | bytes 110600 | tf_op jit(solution)/shard_map/ppermute | solution.py:21
  82.8 3.0 %fusion.97 = f32[16,32,512]{2,1,0:T(8,128)S(1)} fusion(f32[16,32,512]{2,1,0:T(8,128)S(1)} %get-tuple-element.256, f32[18,1,512]{2,1,0:T(1,128)S(1)} %collective-permute-done.12, f32[1,32,512]{2,1,0:T(8,128)S(1)} %collective-permute-done.9, f32[1,32,512]{2,1,0:T(8,128)S(1)} %collective-permute-done.10, f32[18,1,512]{2,1,0:T(1,128)S(1)} %collective-permute-done.11, ...), kind=kLoop, calls=%fused_computation.156 | loop fusion | flops 18612224 | bytes 11153408 | tf_op jit(solution)/shard_map/add | solution.py:83
  85.8 1.9 collective-permute-start.13
  87.7 2.4 %collective-permute-start.14 = (f32[1,32,512]{2,1,0:T(8,128)S(1)}, f32[1,32,512]{2,1,0:T(8,128)S(1)}, u32[]{:S(2)}, u32[]{:S(2)}) collective-permute-start(f32[1,32,512]{2,1,0:T(8,128)S(1)} %get-tuple-element.288), channel_id=1, source_target_pairs={{0,8},{8,16},{16,24},{1,9},{9,17},{17,25},{2,10},{10,18},{18,26},{... | collective-permute-start | bytes 196616 | tf_op jit(solution)/shard_map/ppermute | solution.py:21
  93.3 4.2 %collective-permute-start.15 = (f32[18,1,512]{2,1,0:T(1,128)S(1)}, f32[18,1,512]{2,1,0:T(1,128)S(1)}, u32[]{:S(2)}, u32[]{:S(2)}) collective-permute-start(f32[18,1,512]{2,1,0:T(1,128)S(1)} %get-tuple-element.266), channel_id=1, source_target_pairs={{1,0},{2,1},{3,2},{4,3},{5,4},{6,5},{7,6},{9,8},{10,9},{11,10},{12... | collective-permute-start | bytes 110600 | tf_op jit(solution)/shard_map/ppermute | solution.py:24
  97.5 3.1 %collective-permute-start.16 = (f32[18,1,512]{2,1,0:T(1,128)S(1)}, f32[18,1,512]{2,1,0:T(1,128)S(1)}, u32[]{:S(2)}, u32[]{:S(2)}) collective-permute-start(f32[18,1,512]{2,1,0:T(1,128)S(1)} %get-tuple-element.267), channel_id=1, source_target_pairs={{0,1},{1,2},{2,3},{3,4},{4,5},{5,6},{6,7},{8,9},{9,10},{10,11},{11... | collective-permute-start | bytes 110600 | tf_op jit(solution)/shard_map/ppermute | solution.py:21
  101.0 2.3 %collective-permute-done.16 = f32[18,1,512]{2,1,0:T(1,128)S(1)} collective-permute-done((f32[18,1,512]{2,1,0:T(1,128)S(1)}, f32[18,1,512]{2,1,0:T(1,128)S(1)}, u32[]{:S(2)}, u32[]{:S(2)}) %collective-permute-start.16) | collective-permute-done | bytes 36896 | tf_op jit(solution)/shard_map/ppermute | solution.py:21
  103.4 3.0 %fusion.80 = f32[16,32,512]{2,1,0:T(8,128)S(1)} fusion(f32[16,32,512]{2,1,0:T(8,128)S(1)} %fusion.97, f32[18,1,512]{2,1,0:T(1,128)S(1)} %collective-permute-done.16, f32[1,32,512]{2,1,0:T(8,128)S(1)} %collective-permute-done.13, f32[1,32,512]{2,1,0:T(8,128)S(1)} %collective-permute-done.14, f32[18,1,512]{2,1,0:T(1,128)S(1)} %collective-permute-done.15, ...), kind=kLoop, calls=%fused_computation.131 | loop fusion | flops 18612224 | bytes 11153408 | tf_op jit(solution)/shard_map/add | solution.py:83
  110.0 3.0 %collective-permute-start.18 = (f32[1,32,512]{2,1,0:T(8,128)}, f32[1,32,512]{2,1,0:T(8,128)}, u32[]{:S(2)}, u32[]{:S(2)}) collective-permute-start(f32[1,32,512]{2,1,0:T(8,128)} %get-tuple-element.284), channel_id=1, source_target_pairs={{0,8},{8,16},{16,24},{1,9},{9,17},{17,25},{2,10},{10,18},{18,26},{... | collective-permute-start | bytes 196616 | tf_op jit(solution)/shard_map/ppermute | solution.py:21
  117.1 2.8 %collective-permute-start.19 = (f32[18,1,512]{2,1,0:T(1,128)S(1)}, f32[18,1,512]{2,1,0:T(1,128)S(1)}, u32[]{:S(2)}, u32[]{:S(2)}) collective-permute-start(f32[18,1,512]{2,1,0:T(1,128)S(1)} %get-tuple-element.264), channel_id=1, source_target_pairs={{1,0},{2,1},{3,2},{4,3},{5,4},{6,5},{7,6},{9,8},{10,9},{11,10},{12... | collective-permute-start | bytes 110600 | tf_op jit(solution)/shard_map/ppermute | solution.py:24
  119.9 4.2 %collective-permute-start.20 = (f32[18,1,512]{2,1,0:T(1,128)S(1)}, f32[18,1,512]{2,1,0:T(1,128)S(1)}, u32[]{:S(2)}, u32[]{:S(2)}) collective-permute-start(f32[18,1,512]{2,1,0:T(1,128)S(1)} %get-tuple-element.265), channel_id=1, source_target_pairs={{0,1},{1,2},{2,3},{3,4},{4,5},{5,6},{6,7},{8,9},{9,10},{10,11},{11... | collective-permute-start | bytes 110600 | tf_op jit(solution)/shard_map/ppermute | solution.py:21
  126.1 3.8 %fusion.63 = f32[16,32,512]{2,1,0:T(8,128)S(1)} fusion(f32[16,32,512]{2,1,0:T(8,128)S(1)} %copy-done.3, f32[18,1,512]{2,1,0:T(1,128)S(1)} %collective-permute-done.20, f32[1,32,512]{2,1,0:T(8,128)} %collective-permute-done.17, f32[1,32,512]{2,1,0:T(8,128)} %collective-permute-done.18, f32[18,1,512]{2,1,0:T(1,128)S(1)} %collective-permute-done.19, ...), kind=kLoop, calls=%fused_computation.106 | loop fusion | flops 18612224 | bytes 11153408 | tf_op jit(solution)/shard_map/add | solution.py:83
  130.0 4.8 %collective-permute-start.21 = (f32[16,1,512]{2,1,0:T(1,128)S(1)}, f32[16,1,512]{2,1,0:T(1,128)S(1)}, u32[]{:S(2)}, u32[]{:S(2)}) collective-permute-start(f32[16,1,512]{2,1,0:T(1,128)S(1)} %get-tuple-element.280), channel_id=1, source_target_pairs={{0,1},{1,2},{2,3},{3,4},{4,5},{5,6},{6,7},{8,9},{9,10},{10,11},{11... | collective-permute-start | bytes 98312 | tf_op jit(solution)/shard_map/ppermute | solution.py:21
  134.8 2.2 %collective-permute-start.22 = (f32[16,1,512]{2,1,0:T(1,128)S(1)}, f32[16,1,512]{2,1,0:T(1,128)S(1)}, u32[]{:S(2)}, u32[]{:S(2)}) collective-permute-start(f32[16,1,512]{2,1,0:T(1,128)S(1)} %get-tuple-element.281), channel_id=1, source_target_pairs={{1,0},{2,1},{3,2},{4,3},{5,4},{6,5},{7,6},{9,8},{10,9},{11,10},{12... | collective-permute-start | bytes 98312 | tf_op jit(solution)/shard_map/ppermute | solution.py:24
  137.4 1.9 collective-permute-start.23
  139.4 2.4 %collective-permute-done.22 = f32[16,1,512]{2,1,0:T(1,128)S(1)} collective-permute-done((f32[16,1,512]{2,1,0:T(1,128)S(1)}, f32[16,1,512]{2,1,0:T(1,128)S(1)}, u32[]{:S(2)}, u32[]{:S(2)}) %collective-permute-start.22) | collective-permute-done | bytes 32800 | tf_op jit(solution)/shard_map/ppermute | solution.py:24
  141.8 5.1 %fusion.43 = f32[16,32,512]{2,1,0:T(8,128)} fusion(f32[16,32,512]{2,1,0:T(8,128)S(1)} %copy-done.11, f32[16,1,512]{2,1,0:T(1,128)} %collective-permute-done.25, f32[16,1,512]{2,1,0:T(1,128)} %collective-permute-done.24, f32[16,32,511]{2,1,0:T(8,128)S(1)} %copy-done.17, f32[16,32,512]{2,1,0:T(8,128)S(1)} %copy-done.7, f32[16,32,512]{2,1,0:T(8,128)S(1)} %fusion.63, ...), kind=kLoop, calls=%fused_computation.78 | loop fusion | flops 14942208 | bytes 11862016 | tf_op jit(solution)/shard_map/sub | solution.py:102
  148.2 68.8 %while.44 = (s32[]{:T(128)}, f32[16,32,512]{2,1,0:T(8,128)S(1)}, f32[32,128]{1,0:T(8,128)S(1)}, s32[]{:T(128)}, pred[]{:T(512)}, /*index=5*/f32[32,512]{1,0:T(8,...) while((s32[]{:T(128)}, f32[16,32,512]{2,1,0:T(8,128)S(1)}, ...), condition=%wide.region_4.5_spmd, body=%wide.region_1.4_spmd.sunk | while | flops 344078 | bytes 3162595 | solution.py:208
  151.0 1.9 while.45
  153.0 1.9 collective-permute-start
  155.0 3.0 %collective-permute-done = f32[32,128]{1,0:T(8,128)S(1)} collective-permute-done((f32[32,128]{1,0:T(8,128)S(1)}, f32[32,128]{1,0:T(8,128)S(1)}, u32[]{:S(2)}, u32[]{:S(2)}) %collective-permute-start) | collective-permute-done | bytes 16416 | tf_op jit(solution)/shard_map/while/body/eval_jaxpr/ppermute | solution.py:32
  160.8 1.9 while.45
  164.8 3.0 %collective-permute-done = f32[32,128]{1,0:T(8,128)S(1)} collective-permute-done((f32[32,128]{1,0:T(8,128)S(1)}, f32[32,128]{1,0:T(8,128)S(1)}, u32[]{:S(2)}, u32[]{:S(2)}) %collective-permute-start) | collective-permute-done | bytes 16416 | tf_op jit(solution)/shard_map/while/body/eval_jaxpr/ppermute | solution.py:32
  170.6 1.9 while.45
  174.6 3.0 %collective-permute-done = f32[32,128]{1,0:T(8,128)S(1)} collective-permute-done((f32[32,128]{1,0:T(8,128)S(1)}, f32[32,128]{1,0:T(8,128)S(1)}, u32[]{:S(2)}, u32[]{:S(2)}) %collective-permute-start) | collective-permute-done | bytes 16416 | tf_op jit(solution)/shard_map/while/body/eval_jaxpr/ppermute | solution.py:32
  180.5 1.9 while.45
  184.4 3.0 %collective-permute-done = f32[32,128]{1,0:T(8,128)S(1)} collective-permute-done((f32[32,128]{1,0:T(8,128)S(1)}, f32[32,128]{1,0:T(8,128)S(1)}, u32[]{:S(2)}, u32[]{:S(2)}) %collective-permute-start) | collective-permute-done | bytes 16416 | tf_op jit(solution)/shard_map/while/body/eval_jaxpr/ppermute | solution.py:32
  190.3 1.9 while.45
  194.3 3.0 %collective-permute-done = f32[32,128]{1,0:T(8,128)S(1)} collective-permute-done((f32[32,128]{1,0:T(8,128)S(1)}, f32[32,128]{1,0:T(8,128)S(1)}, u32[]{:S(2)}, u32[]{:S(2)}) %collective-permute-start) | collective-permute-done | bytes 16416 | tf_op jit(solution)/shard_map/while/body/eval_jaxpr/ppermute | solution.py:32
  200.1 1.9 while.45
  204.1 3.0 %collective-permute-done = f32[32,128]{1,0:T(8,128)S(1)} collective-permute-done((f32[32,128]{1,0:T(8,128)S(1)}, f32[32,128]{1,0:T(8,128)S(1)}, u32[]{:S(2)}, u32[]{:S(2)}) %collective-permute-start) | collective-permute-done | bytes 16416 | tf_op jit(solution)/shard_map/while/body/eval_jaxpr/ppermute | solution.py:32
  210.0 1.9 while.45
  213.9 3.0 %collective-permute-done = f32[32,128]{1,0:T(8,128)S(1)} collective-permute-done((f32[32,128]{1,0:T(8,128)S(1)}, f32[32,128]{1,0:T(8,128)S(1)}, u32[]{:S(2)}, u32[]{:S(2)}) %collective-permute-start) | collective-permute-done | bytes 16416 | tf_op jit(solution)/shard_map/while/body/eval_jaxpr/ppermute | solution.py:32
  (382 shorter events, 76.1 us)
Async XLA Ops:
  12.9 10.2 %copy-start = (f32[16,32,512]{2,1,0:T(8,128)S(1)}, f32[16,32,512]{2,1,0:T(8,128)}, u32[]{:S(2)}) copy-start(f32[16,32,512]{2,1,0:T(8,128)} %param.16) | copy-start | bytes 3145732
  18.7 14.6 %collective-permute-start.1 = (f32[1,32,512]{2,1,0:T(8,128)S(1)}, f32[1,32,512]{2,1,0:T(8,128)S(1)}, u32[]{:S(2)}, u32[]{:S(2)}) collective-permute-start(f32[1,32,512]{2,1,0:T(8,128)S(1)} %get-tuple-element.296), channel_id=1, source_target_pairs={{8,0},{16,8},{24,16},{9,1},{17,9},{25,17},{10,2},{18,10},{26,18},{... | collective-permute-start | bytes 196616 | tf_op jit(solution)/shard_map/ppermute | solution.py:24
  20.6 12.7 %collective-permute-start.3 = (f32[1,32,512]{2,1,0:T(8,128)S(1)}, f32[1,32,512]{2,1,0:T(8,128)S(1)}, u32[]{:S(2)}, u32[]{:S(2)}) collective-permute-start(f32[1,32,512]{2,1,0:T(8,128)S(1)} %get-tuple-element.297), channel_id=1, source_target_pairs={{0,8},{8,16},{16,24},{1,9},{9,17},{17,25},{2,10},{10,18},{18,26},{... | collective-permute-start | bytes 196616 | tf_op jit(solution)/shard_map/ppermute | solution.py:21
  23.7 17.0 %collective-permute-start.4 = (f32[1,32,512]{2,1,0:T(8,128)S(1)}, f32[1,32,512]{2,1,0:T(8,128)S(1)}, u32[]{:S(2)}, u32[]{:S(2)}) collective-permute-start(f32[1,32,512]{2,1,0:T(8,128)S(1)} %get-tuple-element.301), channel_id=1, source_target_pairs={{0,8},{8,16},{16,24},{1,9},{9,17},{17,25},{2,10},{10,18},{18,26},{... | collective-permute-start | bytes 196616 | tf_op jit(solution)/shard_map/ppermute | solution.py:21
  25.6 6.4 %copy-start.12 = (f32[16,32,512]{2,1,0:T(8,128)S(1)}, f32[16,32,512]{2,1,0:T(8,128)}, u32[]{:S(2)}) copy-start(f32[16,32,512]{2,1,0:T(8,128)} %param.17) | copy-start | bytes 3145732
  25.6 15.3 %collective-permute-start.2 = (f32[1,32,512]{2,1,0:T(8,128)}, f32[1,32,512]{2,1,0:T(8,128)}, u32[]{:S(2)}, u32[]{:S(2)}) collective-permute-start(f32[1,32,512]{2,1,0:T(8,128)} %get-tuple-element.300), channel_id=1, source_target_pairs={{8,0},{16,8},{24,16},{9,1},{17,9},{25,17},{10,2},{18,10},{26,18},{... | collective-permute-start | bytes 196616 | tf_op jit(solution)/shard_map/ppermute | solution.py:24
  34.0 19.7 %collective-permute-start.5 = (f32[18,1,512]{2,1,0:T(1,128)}, f32[18,1,512]{2,1,0:T(1,128)S(1)}, u32[]{:S(2)}, u32[]{:S(2)}) collective-permute-start(f32[18,1,512]{2,1,0:T(1,128)} %get-tuple-element.270), channel_id=1, source_target_pairs={{1,0},{2,1},{3,2},{4,3},{5,4},{6,5},{7,6},{9,8},{10,9},{11,10},{12... | collective-permute-start | bytes 110600 | tf_op jit(solution)/shard_map/ppermute | solution.py:24
  36.4 17.3 %collective-permute-start.7 = (f32[18,1,512]{2,1,0:T(1,128)}, f32[18,1,512]{2,1,0:T(1,128)S(1)}, u32[]{:S(2)}, u32[]{:S(2)}) collective-permute-start(f32[18,1,512]{2,1,0:T(1,128)} %get-tuple-element.271), channel_id=1, source_target_pairs={{0,1},{1,2},{2,3},{3,4},{4,5},{5,6},{6,7},{8,9},{9,10},{10,11},{11... | collective-permute-start | bytes 110600 | tf_op jit(solution)/shard_map/ppermute | solution.py:21
  40.8 8.5 %copy-start.29 = (s32[3,128]{1,0:T(4,128)S(1)}, s32[3,128]{1,0:T(4,128)}, u32[]{:S(2)}) copy-start(s32[3,128]{1,0:T(4,128)} %param.18) | copy-start | bytes 4612
  41.7 8.1 %copy-start.18 = (f32[18,32,512]{2,1,0:T(8,128)}, f32[18,32,512]{2,1,0:T(8,128)S(1)}, u32[]{:S(2)}) copy-start(f32[18,32,512]{2,1,0:T(8,128)S(1)} %constant_dynamic-update-slice_fusion) | copy-start | bytes 3538948
  42.5 11.2 %collective-permute-start.6 = (f32[18,1,512]{2,1,0:T(1,128)}, f32[18,1,512]{2,1,0:T(1,128)S(1)}, u32[]{:S(2)}, u32[]{:S(2)}) collective-permute-start(f32[18,1,512]{2,1,0:T(1,128)} %get-tuple-element.272), channel_id=1, source_target_pairs={{1,0},{2,1},{3,2},{4,3},{5,4},{6,5},{7,6},{9,8},{10,9},{11,10},{12... | collective-permute-start | bytes 110600 | tf_op jit(solution)/shard_map/ppermute | solution.py:24
  44.5 9.3 %collective-permute-start.8 = (f32[18,1,512]{2,1,0:T(1,128)}, f32[18,1,512]{2,1,0:T(1,128)S(1)}, u32[]{:S(2)}, u32[]{:S(2)}) collective-permute-start(f32[18,1,512]{2,1,0:T(1,128)} %get-tuple-element.273), channel_id=1, source_target_pairs={{0,1},{1,2},{2,3},{3,4},{4,5},{5,6},{6,7},{8,9},{9,10},{10,11},{11... | collective-permute-start | bytes 110600 | tf_op jit(solution)/shard_map/ppermute | solution.py:21
  54.4 12.3 %copy-start.10 = (f32[16,32,512]{2,1,0:T(8,128)S(1)}, f32[16,32,512]{2,1,0:T(8,128)}, u32[]{:S(2)}) copy-start(f32[16,32,512]{2,1,0:T(8,128)} %add_divide_fusion.1) | copy-start | bytes 3145732
  61.1 42.3 %copy-start.4 = (f32[16,32,512]{2,1,0:T(8,128)}, f32[16,32,512]{2,1,0:T(8,128)S(1)}, u32[]{:S(2)}) copy-start(f32[16,32,512]{2,1,0:T(8,128)S(1)} %get-tuple-element.257) | copy-start | bytes 3145732
  61.1 42.3 %copy-start.6 = (f32[16,32,512]{2,1,0:T(8,128)}, f32[16,32,512]{2,1,0:T(8,128)S(1)}, u32[]{:S(2)}) copy-start(f32[16,32,512]{2,1,0:T(8,128)S(1)} %get-tuple-element.258) | copy-start | bytes 3145732
  61.1 13.0 %collective-permute-start.10 = (f32[1,32,512]{2,1,0:T(8,128)S(1)}, f32[1,32,512]{2,1,0:T(8,128)S(1)}, u32[]{:S(2)}, u32[]{:S(2)}) collective-permute-start(f32[1,32,512]{2,1,0:T(8,128)S(1)} %get-tuple-element.292), channel_id=1, source_target_pairs={{0,8},{8,16},{16,24},{1,9},{9,17},{17,25},{2,10},{10,18},{18,26},{... | collective-permute-start | bytes 196616 | tf_op jit(solution)/shard_map/ppermute | solution.py:21
  63.1 11.1 %collective-permute-start.9 = (f32[1,32,512]{2,1,0:T(8,128)S(1)}, f32[1,32,512]{2,1,0:T(8,128)S(1)}, u32[]{:S(2)}, u32[]{:S(2)}) collective-permute-start(f32[1,32,512]{2,1,0:T(8,128)S(1)} %get-tuple-element.293), channel_id=1, source_target_pairs={{8,0},{16,8},{24,16},{9,1},{17,9},{25,17},{10,2},{18,10},{26,18},{... | collective-permute-start | bytes 196616 | tf_op jit(solution)/shard_map/ppermute | solution.py:24
  67.4 71.9 %collective-permute-start.24 = (f32[16,1,512]{2,1,0:T(1,128)}, f32[16,1,512]{2,1,0:T(1,128)}, u32[]{:S(2)}, u32[]{:S(2)}) collective-permute-start(f32[16,1,512]{2,1,0:T(1,128)} %get-tuple-element.278), channel_id=1, source_target_pairs={{1,0},{2,1},{3,2},{4,3},{5,4},{6,5},{7,6},{9,8},{10,9},{11,10},{12... | collective-permute-start | bytes 98312 | tf_op jit(solution)/shard_map/ppermute | solution.py:24
  69.3 70.0 %collective-permute-start.25 = (f32[16,1,512]{2,1,0:T(1,128)}, f32[16,1,512]{2,1,0:T(1,128)}, u32[]{:S(2)}, u32[]{:S(2)}) collective-permute-start(f32[16,1,512]{2,1,0:T(1,128)} %get-tuple-element.279), channel_id=1, source_target_pairs={{0,1},{1,2},{2,3},{3,4},{4,5},{5,6},{6,7},{8,9},{9,10},{10,11},{11... | collective-permute-start | bytes 98312 | tf_op jit(solution)/shard_map/ppermute | solution.py:21
  74.2 7.3 %collective-permute-start.11 = (f32[18,1,512]{2,1,0:T(1,128)S(1)}, f32[18,1,512]{2,1,0:T(1,128)S(1)}, u32[]{:S(2)}, u32[]{:S(2)}) collective-permute-start(f32[18,1,512]{2,1,0:T(1,128)S(1)} %get-tuple-element.268), channel_id=1, source_target_pairs={{1,0},{2,1},{3,2},{4,3},{5,4},{6,5},{7,6},{9,8},{10,9},{11,10},{12... | collective-permute-start | bytes 110600 | tf_op jit(solution)/shard_map/ppermute | solution.py:24
  76.2 6.6 %copy-start.8 = (f32[16,32,512]{2,1,0:T(8,128)S(1)}, f32[16,32,512]{2,1,0:T(8,128)}, u32[]{:S(2)}) copy-start(f32[16,32,512]{2,1,0:T(8,128)} %get-tuple-element.247) | copy-start | bytes 3145732
  76.2 6.6 %copy-start.21 = (f32[18,1,512]{2,1,0:T(1,128)S(1)}, f32[18,1,512]{2,1,0:T(1,128)}, u32[]{:S(2)}) copy-start(f32[18,1,512]{2,1,0:T(1,128)} %copy-done.20) | copy-start | bytes 110596
  76.2 6.6 %copy-start.24 = (f32[18,1,512]{2,1,0:T(1,128)S(1)}, f32[18,1,512]{2,1,0:T(1,128)}, u32[]{:S(2)}) copy-start(f32[18,1,512]{2,1,0:T(1,128)} %copy-done.23) | copy-start | bytes 110596
  76.2 6.6 %collective-permute-start.12 = (f32[18,1,512]{2,1,0:T(1,128)S(1)}, f32[18,1,512]{2,1,0:T(1,128)S(1)}, u32[]{:S(2)}, u32[]{:S(2)}) collective-permute-start(f32[18,1,512]{2,1,0:T(1,128)S(1)} %get-tuple-element.269), channel_id=1, source_target_pairs={{0,1},{1,2},{2,3},{3,4},{4,5},{5,6},{6,7},{8,9},{9,10},{10,11},{11... | collective-permute-start | bytes 110600 | tf_op jit(solution)/shard_map/ppermute | solution.py:21
  85.8 6.1 %collective-permute-start.13 = (f32[1,32,512]{2,1,0:T(8,128)S(1)}, f32[1,32,512]{2,1,0:T(8,128)S(1)}, u32[]{:S(2)}, u32[]{:S(2)}) collective-permute-start(f32[1,32,512]{2,1,0:T(8,128)S(1)} %get-tuple-element.289), channel_id=1, source_target_pairs={{8,0},{16,8},{24,16},{9,1},{17,9},{25,17},{10,2},{18,10},{26,18},{... | collective-permute-start | bytes 196616 | tf_op jit(solution)/shard_map/ppermute | solution.py:24
  87.7 5.6 %collective-permute-start.14 = (f32[1,32,512]{2,1,0:T(8,128)S(1)}, f32[1,32,512]{2,1,0:T(8,128)S(1)}, u32[]{:S(2)}, u32[]{:S(2)}) collective-permute-start(f32[1,32,512]{2,1,0:T(8,128)S(1)} %get-tuple-element.288), channel_id=1, source_target_pairs={{0,8},{8,16},{16,24},{1,9},{9,17},{17,25},{2,10},{10,18},{18,26},{... | collective-permute-start | bytes 196616 | tf_op jit(solution)/shard_map/ppermute | solution.py:21
  93.3 7.7 %collective-permute-start.15 = (f32[18,1,512]{2,1,0:T(1,128)S(1)}, f32[18,1,512]{2,1,0:T(1,128)S(1)}, u32[]{:S(2)}, u32[]{:S(2)}) collective-permute-start(f32[18,1,512]{2,1,0:T(1,128)S(1)} %get-tuple-element.266), channel_id=1, source_target_pairs={{1,0},{2,1},{3,2},{4,3},{5,4},{6,5},{7,6},{9,8},{10,9},{11,10},{12... | collective-permute-start | bytes 110600 | tf_op jit(solution)/shard_map/ppermute | solution.py:24
  97.5 5.9 %collective-permute-start.16 = (f32[18,1,512]{2,1,0:T(1,128)S(1)}, f32[18,1,512]{2,1,0:T(1,128)S(1)}, u32[]{:S(2)}, u32[]{:S(2)}) collective-permute-start(f32[18,1,512]{2,1,0:T(1,128)S(1)} %get-tuple-element.267), channel_id=1, source_target_pairs={{0,1},{1,2},{2,3},{3,4},{4,5},{5,6},{6,7},{8,9},{9,10},{10,11},{11... | collective-permute-start | bytes 110600 | tf_op jit(solution)/shard_map/ppermute | solution.py:21
  103.4 11.2 %copy-start.13 = (f32[16,32,512]{2,1,0:T(8,128)S(1)}, f32[16,32,512]{2,1,0:T(8,128)}, u32[]{:S(2)}) copy-start(f32[16,32,512]{2,1,0:T(8,128)} %param.17) | copy-start | bytes 3145732
  108.1 7.4 %collective-permute-start.17 = (f32[1,32,512]{2,1,0:T(8,128)}, f32[1,32,512]{2,1,0:T(8,128)}, u32[]{:S(2)}, u32[]{:S(2)}) collective-permute-start(f32[1,32,512]{2,1,0:T(8,128)} %get-tuple-element.285), channel_id=1, source_target_pairs={{8,0},{16,8},{24,16},{9,1},{17,9},{25,17},{10,2},{18,10},{26,18},{... | collective-permute-start | bytes 196616 | tf_op jit(solution)/shard_map/ppermute | solution.py:24
  110.0 5.9 %collective-permute-start.18 = (f32[1,32,512]{2,1,0:T(8,128)}, f32[1,32,512]{2,1,0:T(8,128)}, u32[]{:S(2)}, u32[]{:S(2)}) collective-permute-start(f32[1,32,512]{2,1,0:T(8,128)} %get-tuple-element.284), channel_id=1, source_target_pairs={{0,8},{8,16},{16,24},{1,9},{9,17},{17,25},{2,10},{10,18},{18,26},{... | collective-permute-start | bytes 196616 | tf_op jit(solution)/shard_map/ppermute | solution.py:21
  115.5 8.6 %copy-start.3 = (f32[16,32,512]{2,1,0:T(8,128)S(1)}, f32[16,32,512]{2,1,0:T(8,128)}, u32[]{:S(2)}) copy-start(f32[16,32,512]{2,1,0:T(8,128)} %copy-done.2) | copy-start | bytes 3145732
  117.1 7.5 %collective-permute-start.19 = (f32[18,1,512]{2,1,0:T(1,128)S(1)}, f32[18,1,512]{2,1,0:T(1,128)S(1)}, u32[]{:S(2)}, u32[]{:S(2)}) collective-permute-start(f32[18,1,512]{2,1,0:T(1,128)S(1)} %get-tuple-element.264), channel_id=1, source_target_pairs={{1,0},{2,1},{3,2},{4,3},{5,4},{6,5},{7,6},{9,8},{10,9},{11,10},{12... | collective-permute-start | bytes 110600 | tf_op jit(solution)/shard_map/ppermute | solution.py:24
  119.9 6.1 %collective-permute-start.20 = (f32[18,1,512]{2,1,0:T(1,128)S(1)}, f32[18,1,512]{2,1,0:T(1,128)S(1)}, u32[]{:S(2)}, u32[]{:S(2)}) collective-permute-start(f32[18,1,512]{2,1,0:T(1,128)S(1)} %get-tuple-element.265), channel_id=1, source_target_pairs={{0,1},{1,2},{2,3},{3,4},{4,5},{5,6},{6,7},{8,9},{9,10},{10,11},{11... | collective-permute-start | bytes 110600 | tf_op jit(solution)/shard_map/ppermute | solution.py:21
  129.9 17.1 %copy-start.1 = (f32[16,32,512]{2,1,0:T(8,128)}, f32[16,32,512]{2,1,0:T(8,128)S(1)}, u32[]{:S(2)}) copy-start(f32[16,32,512]{2,1,0:T(8,128)S(1)} %fusion.63) | copy-start | bytes 3145732
  130.0 9.4 %collective-permute-start.21 = (f32[16,1,512]{2,1,0:T(1,128)S(1)}, f32[16,1,512]{2,1,0:T(1,128)S(1)}, u32[]{:S(2)}, u32[]{:S(2)}) collective-permute-start(f32[16,1,512]{2,1,0:T(1,128)S(1)} %get-tuple-element.280), channel_id=1, source_target_pairs={{0,1},{1,2},{2,3},{3,4},{4,5},{5,6},{6,7},{8,9},{9,10},{10,11},{11... | collective-permute-start | bytes 98312 | tf_op jit(solution)/shard_map/ppermute | solution.py:21
  134.8 7.0 %copy-start.11 = (f32[16,32,512]{2,1,0:T(8,128)S(1)}, f32[16,32,512]{2,1,0:T(8,128)}, u32[]{:S(2)}) copy-start(f32[16,32,512]{2,1,0:T(8,128)} %add_divide_fusion.1) | copy-start | bytes 3145732
  134.8 7.0 %copy-start.16 = (f32[16,32,511]{2,1,0:T(8,128)S(1)}, f32[16,32,511]{2,1,0:T(8,128)}, u32[]{:S(2)}) copy-start(f32[16,32,511]{2,1,0:T(8,128)} %get-tuple-element.276) | copy-start | bytes 3139588
  134.8 7.0 %copy-start.17 = (f32[16,32,511]{2,1,0:T(8,128)S(1)}, f32[16,32,511]{2,1,0:T(8,128)}, u32[]{:S(2)}) copy-start(f32[16,32,511]{2,1,0:T(8,128)} %get-tuple-element.277) | copy-start | bytes 3139588
  134.8 7.0 %collective-permute-start.22 = (f32[16,1,512]{2,1,0:T(1,128)S(1)}, f32[16,1,512]{2,1,0:T(1,128)S(1)}, u32[]{:S(2)}, u32[]{:S(2)}) collective-permute-start(f32[16,1,512]{2,1,0:T(1,128)S(1)} %get-tuple-element.281), channel_id=1, source_target_pairs={{1,0},{2,1},{3,2},{4,3},{5,4},{6,5},{7,6},{9,8},{10,9},{11,10},{12... | collective-permute-start | bytes 98312 | tf_op jit(solution)/shard_map/ppermute | solution.py:24
  137.4 9.6 %collective-permute-start.23 = (f32[1,32,512]{2,1,0:T(8,128)S(1)}, f32[1,32,512]{2,1,0:T(8,128)S(1)}, u32[]{:S(2)}, u32[]{:S(2)}) collective-permute-start(f32[1,32,512]{2,1,0:T(8,128)S(1)} %slice.403), channel_id=1, source_target_pairs={{8,0},{16,8},{24,16},{9,1},{17,9},{25,17},{10,2},{18,10},{26,18},{... | collective-permute-start | bytes 196616 | tf_op jit(solution)/shard_map/ppermute | solution.py:32
  153.0 5.1 %collective-permute-start = (f32[32,128]{1,0:T(8,128)S(1)}, f32[32,128]{1,0:T(8,128)S(1)}, u32[]{:S(2)}, u32[]{:S(2)}) collective-permute-start(f32[32,128]{1,0:T(8,128)S(1)} %get-tuple-element.443), channel_id=1, source_target_pairs={{0,8},{8,16},{16,24},{1,9},{9,17},{17,25},{2,10},{10,18},{18,26},{... | collective-permute-start | bytes 49160 | tf_op jit(solution)/shard_map/while/body/eval_jaxpr/ppermute | solution.py:32
  162.8 5.1 %collective-permute-start = (f32[32,128]{1,0:T(8,128)S(1)}, f32[32,128]{1,0:T(8,128)S(1)}, u32[]{:S(2)}, u32[]{:S(2)}) collective-permute-start(f32[32,128]{1,0:T(8,128)S(1)} %get-tuple-element.443), channel_id=1, source_target_pairs={{0,8},{8,16},{16,24},{1,9},{9,17},{17,25},{2,10},{10,18},{18,26},{... | collective-permute-start | bytes 49160 | tf_op jit(solution)/shard_map/while/body/eval_jaxpr/ppermute | solution.py:32
  172.6 5.1 %collective-permute-start = (f32[32,128]{1,0:T(8,128)S(1)}, f32[32,128]{1,0:T(8,128)S(1)}, u32[]{:S(2)}, u32[]{:S(2)}) collective-permute-start(f32[32,128]{1,0:T(8,128)S(1)} %get-tuple-element.443), channel_id=1, source_target_pairs={{0,8},{8,16},{16,24},{1,9},{9,17},{17,25},{2,10},{10,18},{18,26},{... | collective-permute-start | bytes 49160 | tf_op jit(solution)/shard_map/while/body/eval_jaxpr/ppermute | solution.py:32
  182.4 5.1 %collective-permute-start = (f32[32,128]{1,0:T(8,128)S(1)}, f32[32,128]{1,0:T(8,128)S(1)}, u32[]{:S(2)}, u32[]{:S(2)}) collective-permute-start(f32[32,128]{1,0:T(8,128)S(1)} %get-tuple-element.443), channel_id=1, source_target_pairs={{0,8},{8,16},{16,24},{1,9},{9,17},{17,25},{2,10},{10,18},{18,26},{... | collective-permute-start | bytes 49160 | tf_op jit(solution)/shard_map/while/body/eval_jaxpr/ppermute | solution.py:32
  192.3 5.1 %collective-permute-start = (f32[32,128]{1,0:T(8,128)S(1)}, f32[32,128]{1,0:T(8,128)S(1)}, u32[]{:S(2)}, u32[]{:S(2)}) collective-permute-start(f32[32,128]{1,0:T(8,128)S(1)} %get-tuple-element.443), channel_id=1, source_target_pairs={{0,8},{8,16},{16,24},{1,9},{9,17},{17,25},{2,10},{10,18},{18,26},{... | collective-permute-start | bytes 49160 | tf_op jit(solution)/shard_map/while/body/eval_jaxpr/ppermute | solution.py:32
  202.1 5.1 %collective-permute-start = (f32[32,128]{1,0:T(8,128)S(1)}, f32[32,128]{1,0:T(8,128)S(1)}, u32[]{:S(2)}, u32[]{:S(2)}) collective-permute-start(f32[32,128]{1,0:T(8,128)S(1)} %get-tuple-element.443), channel_id=1, source_target_pairs={{0,8},{8,16},{16,24},{1,9},{9,17},{17,25},{2,10},{10,18},{18,26},{... | collective-permute-start | bytes 49160 | tf_op jit(solution)/shard_map/while/body/eval_jaxpr/ppermute | solution.py:32
  211.9 5.1 %collective-permute-start = (f32[32,128]{1,0:T(8,128)S(1)}, f32[32,128]{1,0:T(8,128)S(1)}, u32[]{:S(2)}, u32[]{:S(2)}) collective-permute-start(f32[32,128]{1,0:T(8,128)S(1)} %get-tuple-element.443), channel_id=1, source_target_pairs={{0,8},{8,16},{16,24},{1,9},{9,17},{17,25},{2,10},{10,18},{18,26},{... | collective-permute-start | bytes 49160 | tf_op jit(solution)/shard_map/while/body/eval_jaxpr/ppermute | solution.py:32
  (14 other events, 42.6 us)
where the time goes:
time: 220 us; the launch traced here: 218 us
  starting transfers between devices  88.5 us (40%)
  other arithmetic  59.1 us (27%)
  local copies, waits for them, and re-layouts  34.7 us (16%)
  waiting for transfers between devices  30.7 us (14%)
  loops' own time  3.54 us (2%)
    ppermute x12, starting transfers between devices, padded(): lax.ppermute(lax.slice_in_dim(block, block.shape[dim] - width, None, axis...  42.7 us
    ppermute x12, starting transfers between devices, padded(): lax.ppermute(lax.slice_in_dim(block, 0, width, axis=dim), axis, backward)  30.5 us
    ppermute x8, waiting for transfers between devices, passed_along(): return lax.ppermute(value, axis, pairs)  21.3 us
    add x4, other arithmetic, jacobi(): return center + OMEGA * (source - storage * center - flow) / diagonal  16.5 us
    ppermute x8, starting transfers between devices, passed_along(): return lax.ppermute(value, axis, pairs)  15.4 us
    dynamic_slice x14, local copies, waits for them, and re-layouts, pick(): return lax.dynamic_slice_in_dim(field, start, width, 2)  14.5 us
    mul x1, other arithmetic, shards(): volume = VOLUME * lookup(rock_type, rock_poro)  9.03 us
    dynamic_update_slice x112, other arithmetic, sweep(): lax.scan(advance, inflow, (volume, through, explicit, old_sat))  8.65 us
  transfers between devices with their start and end apart: 32, of which 13 were waited for; matrix products, arithmetic and copies ran while one was open for 16% of the time, Pallas kernels for 0%

commit v1 on v0

v1 whole, which is shorter than its diff:
```python
import functools

import jax
import jax.numpy as jnp
from jax import lax
from jax.experimental import pallas as pl
from jax.experimental.pallas import tpu as pltpu
from jax.sharding import PartitionSpec as P

PASSES = 4
NEWTON = 3

MOBILITY = 0.5
OMEGA = 0.8
VOLUME = 4.0
COMPRESS = 0.5

LANES = 128
REACH = PASSES + 1
PAD = 8
ANY = pl.BlockSpec(memory_space=pl.ANY)
VMEM = pl.BlockSpec(memory_space=pltpu.VMEM)
SMEM = pl.BlockSpec(memory_space=pltpu.SMEM)


def swap_pairs(axis):
    count = lax.axis_size(axis)
    pairs = []
    for first in (0, 1):
        ups = [(i, i + 1) for i in range(first, count - 1, 2)]
        pairs.append(ups + [(j, i) for i, j in ups])
    return pairs


def swap(value_a, value_b, axis):
    pairs_a, pairs_b = swap_pairs(axis)
    return lax.ppermute(value_a, axis, pairs_a), lax.ppermute(value_b, axis, pairs_b)


def chunks_of(ref):
    return ref.shape[-1] // LANES


def fetch(source, target, sems, start):
    for c in range(target.shape[0]):
        copy = pltpu.make_async_copy(source.at[:, :, pl.ds(c * LANES, LANES)], target.at[c], sems.at[c])
        copy.start() if start else copy.wait()


def pack_kernel(p_ref, rock_ref, sat_ref, ya_ref, yb_ref, xa_ref, xb_ref, p, rock, sat, sems):
    chunks, nx, ny, _ = p.shape
    for i, (source, target) in enumerate(((p_ref, p), (rock_ref, rock), (sat_ref, sat))):
        fetch(source, target, sems.at[i], True)
    for i, (source, target) in enumerate(((p_ref, p), (rock_ref, rock), (sat_ref, sat))):
        fetch(source, target, sems.at[i], False)
    even_y = lax.rem(lax.axis_index("gy"), 2) == 0
    even_x = lax.rem(lax.axis_index("gx"), 2) == 0
    p2, rock2, sat2 = (f.reshape(chunks * nx * ny, LANES) for f in (p, rock, sat))
    rows = (2 * REACH + 1) * nx
    for out, high in ((ya_ref, even_y), (yb_ref, jnp.logical_not(even_y))):
        first = jnp.where(high, ny - REACH, 0)
        edge = jnp.where(high, ny - 1, 0)
        for c in range(chunks):
            base = c * nx * ny
            for j in range(REACH):
                out[pl.ds(c * rows + j * nx, nx), :] = p2[pl.ds(base + first + j, nx, stride=ny), :]
                kinds = rock2[pl.ds(base + first + j, nx, stride=ny), :]
                out[pl.ds(c * rows + (REACH + j) * nx, nx), :] = kinds.astype(jnp.float32) + 1.0
            out[pl.ds(c * rows + 2 * REACH * nx, nx), :] = sat2[pl.ds(base + edge, nx, stride=ny), :]
    for out, high in ((xa_ref, even_x), (xb_ref, jnp.logical_not(even_x))):
        first = jnp.where(high, nx - REACH, 0)
        for c in range(chunks):
            for j in range(REACH):
                out[j, :, pl.ds(c * LANES, LANES)] = p[c, first + j]
                out[REACH + j, :, pl.ds(c * LANES, LANES)] = rock[c, first + j].astype(jnp.float32) + 1.0


def pack(pressure, rock_type, saturation):
    nx, ny, nz = pressure.shape
    chunks = nz // LANES
    side = jax.ShapeDtypeStruct((chunks * (2 * REACH + 1) * nx, LANES), jnp.float32)
    end = jax.ShapeDtypeStruct((2 * REACH, ny, nz), jnp.float32)
    block = (chunks, nx, ny, LANES)
    return pl.pallas_call(
        pack_kernel,
        name="pack",
        out_shape=(side, side, end, end),
        in_specs=[ANY] * 3,
        out_specs=(VMEM,) * 4,
        scratch_shapes=[
            pltpu.VMEM(block, jnp.float32),
            pltpu.VMEM(block, jnp.int32),
            pltpu.VMEM(block, jnp.float32),
            pltpu.SemaphoreType.DMA((3, chunks)),
        ],
    )(pressure, rock_type, saturation)


def corner_kernel(nx, ya_ref, yb_ref, ca_ref, cb_ref):
    rows = (2 * REACH + 1) * nx
    chunks = ya_ref.shape[0] // rows
    even_y = lax.rem(lax.axis_index("gy"), 2) == 0
    even_x = lax.rem(lax.axis_index("gx"), 2) == 0
    for out, high in ((ca_ref, even_x), (cb_ref, jnp.logical_not(even_x))):
        layer = jnp.where(high, nx - PASSES, 0)
        for c in range(chunks):
            for kind in range(2):
                for i in range(PASSES):
                    for side in range(2):
                        start = c * rows + (kind * REACH + 1 - side) * nx + layer + i
                        from_a = ya_ref[pl.ds(start, PASSES, stride=nx), :]
                        from_b = yb_ref[pl.ds(start, PASSES, stride=nx), :]
                        mine = jnp.where(even_y, from_b, from_a) if side == 0 else jnp.where(even_y, from_a, from_b)
                        at = ((c * 2 + kind) * PASSES + i) * 2 + side
                        out[pl.ds(at * PASSES, PASSES), :] = mine


def corners(side_a, side_b, nx):
    chunks = side_a.shape[0] // ((2 * REACH + 1) * nx)
    shape = jax.ShapeDtypeStruct((chunks * 4 * PASSES * PASSES, LANES), jnp.float32)
    return pl.pallas_call(
        functools.partial(corner_kernel, nx),
        name="corners",
        out_shape=(shape, shape),
        in_specs=[VMEM] * 2,
        out_specs=(VMEM,) * 2,
    )(side_a, side_b)


def fraction(water):
    denom = water * water + MOBILITY * (1.0 - water) ** 2
    return water * water / denom


def transmit(left, right):
    return 2.0 * left * right / jnp.maximum(left + right, 1e-30)


def look_up(table, kinds):
    return jnp.take_along_axis(table, kinds, axis=1, mode="promise_in_bounds")


def deeper(values):
    turned = [pltpu.roll(v, LANES - 1, 1) for v in values]
    last = lax.broadcasted_iota(jnp.int32, turned[0].shape, 1) == LANES - 1
    return [jnp.where(last, turned[(c + 1) % len(values)], turned[c]) for c in range(len(values))]


def shallower(values):
    turned = [pltpu.roll(v, 1, 1) for v in values]
    first = lax.broadcasted_iota(jnp.int32, turned[0].shape, 1) == 0
    return [jnp.where(first, turned[c - 1], turned[c]) for c in range(len(values))]


def flow_kernel(
    p_ref, rock_ref, flux_ref, sat_ref, ya_ref, yb_ref, xa_ref, xb_ref, ca_ref, cb_ref, tables_ref, cells_ref, rates_ref,
    press_ref, prep_ref, inlet_ref,
    press, other, kinds, perms, rates, trans_x, trans_y, trans_z, scale, drive, rock, flux, sat, frac, sems,
):
    chunks, layers, pitch, _ = press.shape
    _, nx, ny, _ = rock.shape
    low, depth = PASSES, layers * pitch
    tiles = (ny + 2 * PASSES) // 8
    side_rows = (2 * REACH + 1) * nx
    rank_x, rank_y = lax.axis_index("gx"), lax.axis_index("gy")
    even_x, even_y = lax.rem(rank_x, 2) == 0, lax.rem(rank_y, 2) == 0
    flat = lambda f: f.reshape(chunks * f.shape[1] * f.shape[2], LANES)
    press2, other2, kinds2, perms2, rates2, frac2, rock2, flux2, sat2 = map(flat, (press, other, kinds, perms, rates, frac, rock, flux, sat))

    own_p = press.at[:, pl.ds(low, nx), pl.ds(PAD, ny), :]
    fetch(p_ref, own_p, sems.at[0], True)
    fetch(rock_ref, rock, sems.at[1], True)

    def ends(start, from_low, from_high):
        for c in range(chunks):
            lanes = pl.ds(c * LANES, LANES)
            for i, target in enumerate((press, kinds)):
                a = pltpu.make_async_copy(
                    from_low.at[pl.ds(i * REACH + REACH - low, low), :, lanes],
                    target.at[c, pl.ds(0, low), pl.ds(PAD, ny), :], sems.at[2 + i, c])
                b = pltpu.make_async_copy(
                    from_high.at[pl.ds(i * REACH, REACH), :, lanes],
                    target.at[c, pl.ds(low + nx, REACH), pl.ds(PAD, ny), :], sems.at[4 + i, c])
                for copy in (a, b):
                    copy.start() if start else copy.wait()

    @pl.when(even_x)
    def _():
        ends(True, xb_ref, xa_ref)

    @pl.when(jnp.logical_not(even_x))
    def _():
        ends(True, xa_ref, xb_ref)

    fetch(flux_ref, flux, sems.at[6], True)
    fetch(sat_ref, sat, sems.at[7], True)

    zero = jnp.zeros((8, LANES), jnp.float32)
    sub = lax.broadcasted_iota(jnp.int32, (8, LANES), 0)
    lane = lax.broadcasted_iota(jnp.int32, (8, LANES), 1)

    def clear(layer, _):
        for c in range(chunks):
            for t in range(pitch // 8):
                rates[c, layer, pl.ds(t * 8, 8), :] = zero
            for t in (0, pitch // 8 - 1):
                press[c, layer, pl.ds(t * 8, 8), :] = zero
                kinds[c, layer, pl.ds(t * 8, 8), :] = zero
        return 0

    lax.fori_loop(0, layers, clear, 0)

    def add_well(w, _):
        x = cells_ref[0, w] - rank_x * nx + low
        y = cells_ref[1, w] - rank_y * ny + PAD
        z = cells_ref[2, w]

        @pl.when((x >= 0) & (x < layers) & (y >= 0) & (y < pitch))
        def _():
            row = (lax.shift_right_logical(z, 7) * layers + x) * pitch + y
            tile = pl.multiple_of(lax.shift_left(lax.shift_right_logical(row, 3), 3), 8)
            here = (sub == row - tile) & (lane == lax.bitwise_and(z, LANES - 1))
            rates2[pl.ds(tile, 8), :] = rates2[pl.ds(tile, 8), :] + jnp.where(here, rates_ref[w], 0.0)

        return 0

    lax.fori_loop(0, cells_ref.shape[1], add_well, 0)

    for c in range(chunks):
        for j in range(REACH):
            for i, target in enumerate((press2, kinds2)):
                start = c * side_rows + (i * REACH + j) * nx
                a, b = ya_ref[pl.ds(start, nx), :], yb_ref[pl.ds(start, nx), :]
                at = c * depth + low * pitch + j
                target[pl.ds(at + PAD - REACH, nx, stride=pitch), :] = jnp.where(even_y, b, a)
                target[pl.ds(at + PAD + ny, nx, stride=pitch), :] = jnp.where(even_y, a, b)
        start = c * side_rows + 2 * REACH * nx
        a, b = fraction(ya_ref[pl.ds(start, nx), :]), fraction(yb_ref[pl.ds(start, nx), :])
        at = c * nx * pitch
        frac2[pl.ds(at + PAD - 1, nx, stride=pitch), :] = jnp.where(even_y, b, a)
        frac2[pl.ds(at + PAD + ny, nx, stride=pitch), :] = jnp.where(even_y, a, b)
        for i, target in enumerate((press2, kinds2)):
            for k in range(PASSES):
                for side in range(2):
                    start = (((c * 2 + i) * PASSES + k) * 2 + side) * PASSES
                    a, b = ca_ref[pl.ds(start, PASSES), :], cb_ref[pl.ds(start, PASSES), :]
                    row = PAD - PASSES if side == 0 else PAD + ny
                    at = c * depth + row
                    target[pl.ds(at + k * pitch, PASSES), :] = jnp.where(even_x, b, a)
                    target[pl.ds(at + (low + nx + k) * pitch, PASSES), :] = jnp.where(even_x, a, b)

    fetch(rock_ref, rock, sems.at[1], False)

    def encode(layer, _):
        for c in range(chunks):
            kinds[c, low + layer, pl.ds(PAD, ny), :] = rock[c, layer].astype(jnp.float32) + 1.0
        return 0

    lax.fori_loop(0, nx, encode, 0)
    fetch(p_ref, own_p, sems.at[0], False)
    ends(False, xa_ref, xb_ref)
    perm_table, store_table, volume_table = tables_ref[0], tables_ref[1], tables_ref[2]

    def look(layer, _):
        for c in range(chunks):
            for t in range(pitch // 8):
                kind = kinds[c, layer, pl.ds(t * 8, 8), :].astype(jnp.int32)
                perms[c, layer, pl.ds(t * 8, 8), :] = look_up(perm_table, kind)
        return 0

    lax.fori_loop(0, layers, look, 0)

    def rows_of(ref, layer, k):
        return [ref[pl.ds(c * depth + layer * pitch + PAD - PASSES + k, 8, stride=tiles), :] for c in range(chunks)]

    def tile_of(layer, k):
        return pl.ds(pl.multiple_of((layer * (tiles + 1) + k) * 8, 8), 8)

    def prepare(layer, _):
        perm = {k: rows_of(perms2, layer, k) for k in range(-1, tiles + 1)}
        for k in range(-1, tiles):
            for c in range(chunks):
                trans_y[c, tile_of(layer, k + 1), :] = transmit(perm[k][c], perm[k + 1][c])
        for k in range(tiles):
            ahead = rows_of(perms2, layer + 1, k)
            deep = deeper(perm[k])
            t_z = [transmit(perm[k][c], deep[c]) for c in range(chunks)]
            t_z[-1] = jnp.where(lane == LANES - 1, 0.0, t_z[-1])
            above = shallower(t_z)
            kind = rows_of(kinds2, layer, k)
            start = rows_of(press2, layer, k)
            rate = rows_of(rates2, layer, k)
            for c in range(chunks):
                t_x = transmit(perm[k][c], ahead[c])
                trans_x[c, tile_of(layer, k), :] = t_x
                trans_z[c, tile_of(layer, k), :] = t_z[c]
                t_w = trans_x[c, tile_of(jnp.maximum(layer - 1, 0), k), :]
                t_n, t_s = trans_y[c, tile_of(layer, k + 1), :], trans_y[c, tile_of(layer, k), :]
                store = look_up(store_table, kind[c].astype(jnp.int32))
                factor = OMEGA / (store + ((t_x + t_w) + (t_n + t_s) + (t_z[c] + above[c])))
                scale[c, tile_of(layer, k), :] = factor
                drive[c, tile_of(layer, k), :] = factor * (store * start[c] + rate[c])
        return 0

    lax.fori_loop(0, layers - 1, prepare, 0)

    def sweep_pass(source, target, number):
        def one(layer, _):
            now = {k: rows_of(source, layer, k) for k in range(-1, tiles + 1)}
            for k in range(tiles):
                here = now[k]
                t_z = [trans_z[c, tile_of(layer, k), :] for c in range(chunks)]
                deep = deeper(here)
                shallow = shallower([t_z[c] * here[c] for c in range(chunks)])
                east, west = rows_of(source, layer + 1, k), rows_of(source, layer - 1, k)
                for c in range(chunks):
                    total = (
                        (trans_x[c, tile_of(layer, k), :] * east[c] + trans_x[c, tile_of(layer - 1, k), :] * west[c])
                        + (trans_y[c, tile_of(layer, k + 1), :] * now[k + 1][c] + trans_y[c, tile_of(layer, k), :] * now[k - 1][c])
                        + (t_z[c] * deep[c] + shallow[c])
                    )
                    new = (1.0 - OMEGA) * here[c] + (drive[c, tile_of(layer, k), :] + scale[c, tile_of(layer, k), :] * total)
                    at = c * depth + layer * pitch + PAD - PASSES + k
                    target[pl.ds(at, 8, stride=tiles), :] = new
            return 0

        lax.fori_loop(number, layers - number, one, 0)

    for number in range(1, PASSES + 1):
        source, target = (press2, other2) if number % 2 else (other2, press2)
        sweep_pass(source, target, number)
    final, final2 = (press, press2) if PASSES % 2 == 0 else (other, other2)

    def send_out(start):
        for c in range(chunks):
            copy = pltpu.make_async_copy(
                final.at[c, pl.ds(low, nx), pl.ds(PAD, ny), :], press_ref.at[:, :, pl.ds(c * LANES, LANES)], sems.at[0, c]
            )
            copy.start() if start else copy.wait()

    send_out(True)
    fetch(flux_ref, flux, sems.at[6], False)
    fetch(sat_ref, sat, sems.at[7], False)
    for c in range(chunks):
        inlet_ref[pl.ds(c * ny, ny), :] = flux[c, 0]

    def old_fraction(layer, _):
        for c in range(chunks):
            frac[c, layer, pl.ds(PAD, ny), :] = fraction(sat[c, layer])
        return 0

    lax.fori_loop(0, nx, old_fraction, 0)
    step = ny // 8

    def upwind(flow, own, far):
        return jnp.maximum(flow, 0.0) * own + jnp.minimum(flow, 0.0) * far

    def fluxes(layer, _):
        def rows(ref, k, at=low, span=layers, pad=PAD, width=pitch):
            return [ref[pl.ds((c * span + layer + at) * width + pad + k, 8, stride=step), :] for c in range(chunks)]

        perm = {k: rows(perms2, k) for k in range(-1, step + 1)}
        here = {k: rows(final2, k) for k in range(-1, step + 1)}
        old = {k: rows(frac2, k, 0, nx) for k in range(-1, step + 1)}
        for k in range(step):
            deep = deeper(perm[k])
            t_z = [transmit(perm[k][c], deep[c]) for c in range(chunks)]
            t_z[-1] = jnp.where(lane == LANES - 1, 0.0, t_z[-1])
            below, old_below = deeper(here[k]), deeper(old[k])
            down = [upwind(t_z[c] * (here[k][c] - below[c]), old[k][c], old_below[c]) for c in range(chunks)]
            from_above = shallower(down)
            east, perm_east = rows(final2, k, low + 1), rows(perms2, k, low + 1)
            kind, rate = rows(kinds2, k), rows(rates2, k)
            imposed, water = rows(flux2, k, 0, nx, 0, ny), rows(sat2, k, 0, nx, 0, ny)
            for c in range(chunks):
                north = transmit(perm[k][c], perm[k + 1][c]) * (here[k][c] - here[k + 1][c])
                south = transmit(perm[k][c], perm[k - 1][c]) * (here[k][c] - here[k - 1][c])
                own = old[k][c]
                leaving = (upwind(north, own, old[k + 1][c]) + upwind(south, own, old[k - 1][c])) + (down[c] - from_above[c])
                explicit = jnp.maximum(rate[c], 0.0) + jnp.minimum(rate[c], 0.0) * own - leaving
                t_x = transmit(perm[k][c], perm_east[c])
                through = jnp.maximum(imposed[c] + t_x * (here[k][c] - east[c]), 0.0)
                s = water[c]
                volume = look_up(volume_table, kind[c].astype(jnp.int32))
                denom = s * s + MOBILITY * (1.0 - s) ** 2
                gain = 1.0 / (volume + through * (2.0 * MOBILITY * s * (1.0 - s) / (denom * denom)))
                first = s - (through * own - explicit) * gain
                for i, value in enumerate((first, gain, through, volume, volume * s + explicit)):
                    prep_ref[layer, pl.ds((i * chunks + c) * ny + k, 8, stride=step), :] = value
        return 0

    lax.fori_loop(0, nx, fluxes, 0)
    send_out(False)


def flow(pressure, rock_type, base_flux, saturation, sides, ends, ends_corner, tables, well_cells, well_rates):
    nx, ny, nz = pressure.shape
    chunks = nz // LANES
    layers, pitch = PASSES + nx + REACH, ny + 2 * PAD
    assert ny % 8 == 0 and nz % LANES == 0
    tiles = (ny + 2 * PASSES) // 8
    wide = pltpu.VMEM((chunks, layers, pitch, LANES), jnp.float32)
    packed = pltpu.VMEM((chunks, layers * (tiles + 1) * 8, LANES), jnp.float32)
    block = (chunks, nx, ny, LANES)
    return pl.pallas_call(
        flow_kernel,
        name="flow",
        out_shape=(
            jax.ShapeDtypeStruct(pressure.shape, jnp.float32),
            jax.ShapeDtypeStruct((nx, 5 * chunks * ny, LANES), jnp.float32),
            jax.ShapeDtypeStruct((chunks * ny, LANES), jnp.float32),
        ),
        in_specs=[ANY] * 4 + [VMEM] * 2 + [ANY] * 2 + [VMEM] * 2 + [VMEM, SMEM, SMEM],
        out_specs=(ANY, VMEM, VMEM),
        scratch_shapes=[wide] * 5 + [packed] * 5
        + [pltpu.VMEM(block, jnp.int32)] + [pltpu.VMEM(block, jnp.float32)] * 2
        + [pltpu.VMEM((chunks, nx, pitch, LANES), jnp.float32), pltpu.SemaphoreType.DMA((8, chunks))],
        compiler_params=pltpu.CompilerParams(vmem_limit_bytes=60 << 20),
    )(pressure, rock_type, base_flux, saturation, *sides, *ends, *ends_corner, tables, well_cells, well_rates)


def stage_kernel(stage, inflow_ref, prep_ref, *refs):
    sat_ref, out_ref, prep, sat, sems, out_sems = refs[-6:]
    nx, rows, _ = prep.shape
    plane = rows // 5
    chunks, _, ny, _ = sat.shape

    @pl.when(lax.axis_index("gx") == stage)
    def _():
        def bring(layer):
            return pltpu.make_async_copy(prep_ref.at[layer], prep.at[layer], sems.at[layer])

        def send(layer):
            return [
                pltpu.make_async_copy(sat.at[c, layer], sat_ref.at[layer, :, pl.ds(c * LANES, LANES)], out_sems.at[layer, c])
                for c in range(chunks)
            ]

        for layer in range(nx):
            bring(layer).start()

        def advance(layer, incoming):
            bring(layer).wait()
            first, gain, through, volume, held = (prep[layer, pl.ds(i * plane, plane), :] for i in range(5))
            known = held + incoming
            water = jnp.clip(first + gain * incoming, 0.0, 1.0)
            for _ in range(NEWTON - 1):
                dry = 1.0 - water
                square = water * water
                denom = square + MOBILITY * (dry * dry)
                top = denom * (denom * (volume * water - known) + through * square)
                bottom = denom * denom * volume + through * (2.0 * MOBILITY * (water * dry))
                water = jnp.clip(water - top / bottom, 0.0, 1.0)
            for c in range(chunks):
                sat[c, layer] = water[c * ny : (c + 1) * ny]
            for copy in send(layer):
                copy.start()
            return through * fraction(water)

        out_ref[...] = lax.fori_loop(0, nx, advance, inflow_ref[...])

        def finish(layer, _):
            for copy in send(layer):
                copy.wait()
            return 0

        lax.fori_loop(0, nx, finish, 0)


def run_stage(stage, inflow, prep, shape, saturation):
    nx, ny, nz = shape
    chunks = nz // LANES
    block = jax.ShapeDtypeStruct(shape, jnp.float32)
    return pl.pallas_call(
        functools.partial(stage_kernel, stage),
        name="stage",
        out_shape=(block, jax.ShapeDtypeStruct(inflow.shape, jnp.float32)),
        in_specs=[VMEM, ANY] + [ANY] * len(saturation),
        out_specs=(ANY, VMEM),
        input_output_aliases={2: 0} if saturation else {},
        scratch_shapes=[
            pltpu.VMEM(prep.shape, jnp.float32),
            pltpu.VMEM((chunks, nx, ny, LANES), jnp.float32),
            pltpu.SemaphoreType.DMA((nx,)),
            pltpu.SemaphoreType.DMA((nx, chunks)),
        ],
    )(inflow, prep, *saturation)


def shards(rock_type, rock_perm, rock_poro, base_flux, initial_pressure, old_saturation, well_cells, well_rates):
    nx = rock_type.shape[0]
    volume = VOLUME * rock_poro
    tables = jnp.stack([
        jnp.pad(rock_perm, (1, LANES - 1 - rock_perm.shape[0])),
        jnp.pad(COMPRESS * volume, (1, LANES - 1 - volume.shape[0]), constant_values=1.0),
        jnp.pad(volume, (1, LANES - 1 - volume.shape[0]), constant_values=1.0),
    ])
    tables = jnp.broadcast_to(tables[:, None, :], (3, 8, LANES))

    side_a, side_b, end_a, end_b = pack(initial_pressure, rock_type, old_saturation)
    sides = swap(side_a, side_b, "gy")
    ends = swap(end_a, end_b, "gx")
    ends_corner = swap(*corners(*sides, nx), "gx")
    pressure, prep, inflow = flow(
        initial_pressure, rock_type, base_flux, old_saturation, sides, ends, ends_corner, tables, well_cells, well_rates
    )
    saturation = ()
    count = lax.axis_size("gx")
    for stage in range(count):
        *saturation, outflow = run_stage(stage, inflow, prep, rock_type.shape, saturation)
        if stage < count - 1:
            inflow = lax.ppermute(outflow, "gx", [(stage, stage + 1)])
    return pressure, saturation[0]


def solution(mesh):
    return jax.shard_map(
        shards,
        mesh=mesh,
        in_specs=(
            P("gx", "gy", None),
            P(),
            P(),
            P("gx", "gy", None),
            P("gx", "gy", None),
            P("gx", "gy", None),
            P(),
            P(),
        ),
        out_specs=(P("gx", "gy", None), P("gx", "gy", None)),
        check_vma=False,
    )
```

time: 220 us -> 97.9 us (0.45)
  the two profiles are of different devices: /device:TPU:14 before, /device:TPU:7 now
where the time goes in v1:
time: 97.9 us; the launch traced here: 97.4 us
  Pallas kernels  48.3 us (49%)
  waiting for transfers between devices  30.5 us (31%)
  starting transfers between devices  11.9 us (12%)
  local copies, waits for them, and re-layouts  5.24 us (5%)
    pallas_call x1, Pallas kernels, flow(): pl.pallas_call(flow_kernel, name='flow', out_shape=(jax.ShapeDtypeStruct(...  29.9 us
    ppermute x3, waiting for transfers between devices, shards(): inflow = lax.ppermute(outflow, 'gx', [(stage, stage + 1)])  19.6 us
    pallas_call x4, Pallas kernels, run_stage(): pl.pallas_call(functools.partial(stage_kernel, stage), name='stage', out_...  12.6 us
    ppermute x3, waiting for transfers between devices, swap(): lax.ppermute(value_a, axis, pairs_a)  10.9 us
    ppermute x3, starting transfers between devices, swap(): lax.ppermute(value_b, axis, pairs_b)  5.49 us
    pallas_call x1, Pallas kernels, pack(): pl.pallas_call(pack_kernel, name='pack', out_shape=(side, side, end, end)...  3.86 us
    unnamed x18, local copies, waits for them, and re-layouts  3.76 us
    ppermute x3, starting transfers between devices, swap(): lax.ppermute(value_a, axis, pairs_a)  3.74 us
  transfers between devices with their start and end apart: 9, of which 2 were waited for; matrix products, arithmetic and copies ran while one was open for 2% of the time, Pallas kernels for 2%

profile of v1, /device:TPU:7, one launch (start us, length us, event | category | flops | bytes accessed | tf_op | source)
XLA Modules:
  0.0 97.4 jit_solution(16141383135854315410)
XLA Ops:
  0.6 3.9 %pack.1 = (f32[704,128]{1,0:T(8,128)}, f32[704,128]{1,0:T(8,128)}, f32[10,32,512]{2,1,0:T(8,128)}, f32[10,32,512]{2,1,0:T(8,128)}) custom-call(f32[16,32,512]{2,1,0:T(8,128)} %p_ref.3, s32[16,32,512]{2,1,0:T(8,128)} %rock_ref.3, f32[16,32,512]{2,1,0:T(8,128)} %sat_ref.3), custom_call_target="tpu_custom_call" | custom-call | tf_op jit(solution)/shard_map/pack/pallas_call | solution.py:84
  4.5 0.7 collective-permute-start.2
  5.2 0.7 collective-permute-start.3
  5.9 0.3 collective-permute-start
  6.2 4.1 %collective-permute-start.1 = (f32[704,128]{1,0:T(8,128)}, f32[704,128]{1,0:T(8,128)S(1)}, u32[]{:S(2)}, u32[]{:S(2)}) collective-permute-start(f32[704,128]{1,0:T(8,128)} %get-tuple-element.19), channel_id=1, source_target_pairs={{1,2},{3,4},{5,6},{2,1},{4,3},{6,5},{9,10},{11,12},{13,14},{10,9},... | collective-permute-start | bytes 1081352 | tf_op jit(solution)/shard_map/ppermute | solution.py:37
  10.4 0.7 broadcast_multiply_fusion.1
  11.0 0.1 pad_bitcast_fusion
  11.1 10.9 %collective-permute-done.ya_ref = f32[704,128]{1,0:T(8,128)S(1)} collective-permute-done((f32[704,128]{1,0:T(8,128)}, f32[704,128]{1,0:T(8,128)S(1)}, u32[]{:S(2)}, u32[]{:S(2)}) %collective-permute-start) | collective-permute-done | bytes 360480 | tf_op jit(solution)/shard_map/ppermute | solution.py:37
  22.1 0.0 copy-start
  22.1 0.0 collective-permute-done.1.yb_ref
  22.1 0.7 copy-done
  22.8 0.0 copy-start.1
  22.8 0.7 copy-done.1
  23.5 2.0 %corners.1 = (f32[256,128]{1,0:T(8,128)}, f32[256,128]{1,0:T(8,128)}) custom-call(f32[704,128]{1,0:T(8,128)} %copy-done, f32[704,128]{1,0:T(8,128)} %copy-done.1), custom_call_target="tpu_custom_call" | custom-call | tf_op jit(solution)/shard_map/corners/pallas_call | solution.py:121
  25.5 2.7 %collective-permute-start.4 = (f32[256,128]{1,0:T(8,128)}, f32[256,128]{1,0:T(8,128)S(1)}, u32[]{:S(2)}, u32[]{:S(2)}) collective-permute-start(f32[256,128]{1,0:T(8,128)} %get-tuple-element.22), channel_id=1, source_target_pairs={{0,8},{16,24},{8,0},{24,16},{1,9},{17,25},{9,1},{25,17},{2,10},{18... | collective-permute-start | bytes 393224 | tf_op jit(solution)/shard_map/ppermute | solution.py:37
  28.2 0.7 collective-permute-start.5
  28.9 0.7 pad_bitcast_fusion.2
  29.6 0.0 collective-permute-done.4.ca_ref
  29.6 0.0 copy-start.4
  29.6 0.0 collective-permute-done.5.cb_ref
  29.6 0.0 copy-start.5
  29.6 0.0 collective-permute-done.2.xa_ref
  29.7 0.0 copy-start.2
  29.7 0.0 collective-permute-done.3.xb_ref
  29.7 0.0 copy-start.3
  29.7 0.7 broadcast_in_dim.2.tables_ref
  30.4 0.0 copy-done.4
  30.4 0.0 copy-done.5
  30.4 0.2 copy-done.2
  30.5 0.2 copy-done.3
  30.8 29.9 %flow.1 = (f32[16,32,512]{2,1,0:T(8,128)}, f32[16,640,128]{2,1,0:T(8,128)}, f32[128,128]{1,0:T(8,128)}) custom-call(f32[16,32,512]{2,1,0:T(8,128)} %p_ref.3, s32[16,32,512]{2,1,0:T(8,128)} %rock_ref.3, f32[16,32,512]{2,1,0:T(8,128)} %flux_ref.1, f32[16,32,512]{2,1,0:T(8,128)} %sat_ref.3, f32[704,128]{1,0:T(8,128)} %copy-done, f32[704,128]{1,0:T(8,128)} %copy-done.1, ...), custom_call_target="tpu_custom_call" | custom-call | tf_op jit(solution)/shard_map/flow/pallas_call | solution.py:405
  60.6 2.2 %stage.4 = (f32[16,32,512]{2,1,0:T(8,128)}, f32[128,128]{1,0:T(8,128)}) custom-call(f32[128,128]{1,0:T(8,128)} %get-tuple-element.25.inflow_ref, f32[16,640,128]{2,1,0:T(8,128)} %get-tuple-element.26.prep_ref), custom_call_target="tpu_custom_call" | custom-call | tf_op jit(solution)/shard_map/stage/pallas_call | solution.py:474
  62.8 0.7 collective-permute-start.6
  63.5 0.0 collective-permute-done.6.inflow_ref
  63.5 0.0 copy-start.7
  63.5 0.6 copy-done.7
  64.1 2.2 %stage.5 = (f32[16,32,512]{2,1,0:T(8,128)}, f32[128,128]{1,0:T(8,128)}) custom-call(f32[128,128]{1,0:T(8,128)} %copy-done.7, f32[16,640,128]{2,1,0:T(8,128)} %get-tuple-element.26.prep_ref, f32[16,32,512]{2,1,0:T(8,128)} %get-tuple-element.28.refs_0_), custom_call_target="tpu_custom_call", output_to_operand_aliasing={{0}: (2, {})} | custom-call | tf_op jit(solution)/shard_map/stage/pallas_call | solution.py:474
  66.3 0.7 collective-permute-start.7
  67.0 0.0 collective-permute-done.7.inflow_ref
  67.0 0.0 copy-start.8
  67.0 0.6 copy-done.8
  67.7 2.2 %stage.6 = (f32[16,32,512]{2,1,0:T(8,128)}, f32[128,128]{1,0:T(8,128)}) custom-call(f32[128,128]{1,0:T(8,128)} %copy-done.8, f32[16,640,128]{2,1,0:T(8,128)} %get-tuple-element.26.prep_ref, f32[16,32,512]{2,1,0:T(8,128)} %get-tuple-element.30.refs_0_), custom_call_target="tpu_custom_call", output_to_operand_aliasing={{0}: (2, {})} | custom-call | tf_op jit(solution)/shard_map/stage/pallas_call | solution.py:474
  69.8 1.3 %collective-permute-start.8 = (f32[128,128]{1,0:T(8,128)}, f32[128,128]{1,0:T(8,128)S(1)}, u32[]{:S(2)}, u32[]{:S(2)}) collective-permute-start(f32[128,128]{1,0:T(8,128)} %get-tuple-element.31), channel_id=1, source_target_pairs={{16,24},{17,25},{18,26},{19,27},{20,28},{21,29},{22,30},{23,31}} | collective-permute-start | bytes 196616 | tf_op jit(solution)/shard_map/ppermute | solution.py:512
  71.1 19.6 %collective-permute-done.8.inflow_ref = f32[128,128]{1,0:T(8,128)S(1)} collective-permute-done((f32[128,128]{1,0:T(8,128)}, f32[128,128]{1,0:T(8,128)S(1)}, u32[]{:S(2)}, u32[]{:S(2)}) %collective-permute-start.8) | collective-permute-done | bytes 65568 | tf_op jit(solution)/shard_map/ppermute | solution.py:512
  90.7 0.0 copy-start.6
  90.7 0.6 copy-done.6
  91.4 6.0 %stage.7 = (f32[16,32,512]{2,1,0:T(8,128)}, f32[128,128]{1,0:T(8,128)}) custom-call(f32[128,128]{1,0:T(8,128)} %copy-done.6, f32[16,640,128]{2,1,0:T(8,128)} %get-tuple-element.26.prep_ref, f32[16,32,512]{2,1,0:T(8,128)} %get-tuple-element.32.refs_0_), custom_call_target="tpu_custom_call", output_to_operand_aliasing={{0}: (2, {})} | custom-call | tf_op jit(solution)/shard_map/stage/pallas_call | solution.py:474
  (1 shorter events, 0.0 us)
Async XLA Ops:
  4.5 25.2 %collective-permute-start.2 = (f32[10,32,512]{2,1,0:T(8,128)}, f32[10,32,512]{2,1,0:T(8,128)S(1)}, u32[]{:S(2)}, u32[]{:S(2)}) collective-permute-start(f32[10,32,512]{2,1,0:T(8,128)} %get-tuple-element.20), channel_id=1, source_target_pairs={{0,8},{16,24},{8,0},{24,16},{1,9},{17,25},{9,1},{25,17},{2,10},{18... | collective-permute-start | bytes 1966088 | tf_op jit(solution)/shard_map/ppermute | solution.py:37
  5.2 24.4 %collective-permute-start.3 = (f32[10,32,512]{2,1,0:T(8,128)}, f32[10,32,512]{2,1,0:T(8,128)S(1)}, u32[]{:S(2)}, u32[]{:S(2)}) collective-permute-start(f32[10,32,512]{2,1,0:T(8,128)} %get-tuple-element.21), channel_id=1, source_target_pairs={{8,16},{16,8},{9,17},{17,9},{10,18},{18,10},{11,19},{19,11},{12,20... | collective-permute-start | bytes 1966088 | tf_op jit(solution)/shard_map/ppermute | solution.py:37
  5.9 16.1 %collective-permute-start = (f32[704,128]{1,0:T(8,128)}, f32[704,128]{1,0:T(8,128)S(1)}, u32[]{:S(2)}, u32[]{:S(2)}) collective-permute-start(f32[704,128]{1,0:T(8,128)} %get-tuple-element.18), channel_id=1, source_target_pairs={{0,1},{2,3},{4,5},{6,7},{1,0},{3,2},{5,4},{7,6},{8,9},{10,11},{12,... | collective-permute-start | bytes 1081352 | tf_op jit(solution)/shard_map/ppermute | solution.py:37
  6.2 15.8 %collective-permute-start.1 = (f32[704,128]{1,0:T(8,128)}, f32[704,128]{1,0:T(8,128)S(1)}, u32[]{:S(2)}, u32[]{:S(2)}) collective-permute-start(f32[704,128]{1,0:T(8,128)} %get-tuple-element.19), channel_id=1, source_target_pairs={{1,2},{3,4},{5,6},{2,1},{4,3},{6,5},{9,10},{11,12},{13,14},{10,9},... | collective-permute-start | bytes 1081352 | tf_op jit(solution)/shard_map/ppermute | solution.py:37
  22.1 0.7 copy-start
  22.8 0.7 copy-start.1
  25.5 4.1 %collective-permute-start.4 = (f32[256,128]{1,0:T(8,128)}, f32[256,128]{1,0:T(8,128)S(1)}, u32[]{:S(2)}, u32[]{:S(2)}) collective-permute-start(f32[256,128]{1,0:T(8,128)} %get-tuple-element.22), channel_id=1, source_target_pairs={{0,8},{16,24},{8,0},{24,16},{1,9},{17,25},{9,1},{25,17},{2,10},{18... | collective-permute-start | bytes 393224 | tf_op jit(solution)/shard_map/ppermute | solution.py:37
  28.2 1.4 %collective-permute-start.5 = (f32[256,128]{1,0:T(8,128)}, f32[256,128]{1,0:T(8,128)S(1)}, u32[]{:S(2)}, u32[]{:S(2)}) collective-permute-start(f32[256,128]{1,0:T(8,128)} %get-tuple-element.23), channel_id=1, source_target_pairs={{8,16},{16,8},{9,17},{17,9},{10,18},{18,10},{11,19},{19,11},{12,20... | collective-permute-start | bytes 393224 | tf_op jit(solution)/shard_map/ppermute | solution.py:37
  29.6 0.8 copy-start.4
  29.6 0.7 copy-start.5
  29.7 0.9 copy-start.2
  29.7 1.1 %copy-start.3 = (f32[10,32,512]{2,1,0:T(8,128)}, f32[10,32,512]{2,1,0:T(8,128)S(1)}, u32[]{:S(2)}) copy-start(f32[10,32,512]{2,1,0:T(8,128)S(1)} %collective-permute-done.3.xb_ref) | copy-start | bytes 1966084
  62.8 0.7 collective-permute-start.6
  63.5 0.6 copy-start.7
  66.3 0.7 collective-permute-start.7
  67.0 0.6 copy-start.8
  69.8 20.9 %collective-permute-start.8 = (f32[128,128]{1,0:T(8,128)}, f32[128,128]{1,0:T(8,128)S(1)}, u32[]{:S(2)}, u32[]{:S(2)}) collective-permute-start(f32[128,128]{1,0:T(8,128)} %get-tuple-element.31), channel_id=1, source_target_pairs={{16,24},{17,25},{18,26},{19,27},{20,28},{21,29},{22,30},{23,31}} | collective-permute-start | bytes 196616 | tf_op jit(solution)/shard_map/ppermute | solution.py:512
  90.7 0.6 copy-start.6

commit v2 on v1

v2 whole, which is shorter than its diff:
```python
import functools
import math

import jax
import jax.numpy as jnp
from jax import lax
from jax.experimental import pallas as pl
from jax.experimental.pallas import tpu as pltpu
from jax.sharding import PartitionSpec as P


PASSES = 4
NEWTON = 3

MOBILITY = 0.5
OMEGA = 0.8
VOLUME = 4.0
COMPRESS = 0.5

LANES = 128
UNROLL = 2
REACH = PASSES + 1
PAD = 8
HBM = pl.BlockSpec(memory_space=pltpu.MemorySpace.HBM)
VMEM = pl.BlockSpec(memory_space=pltpu.VMEM)
SMEM = pl.BlockSpec(memory_space=pltpu.SMEM)


def swap_pairs(axis):
    count = lax.axis_size(axis)
    pairs = []
    for first in (0, 1):
        ups = [(i, i + 1) for i in range(first, count - 1, 2)]
        pairs.append(ups + [(j, i) for i, j in ups])
    return pairs


def swap(value_a, value_b, axis):
    pairs_a, pairs_b = swap_pairs(axis)
    got_a = lax.ppermute(value_a, axis, pairs_a)
    got_b = lax.ppermute(value_b, axis, pairs_b)
    return got_a, got_b


def fetch(source, target, sems, start):
    for c in range(target.shape[0]):
        copy = pltpu.make_async_copy(source.at[:, :, pl.ds(c * LANES, LANES)], target.at[c], sems.at[c])
        copy.start() if start else copy.wait()


def pack_sides_kernel(p_ref, rock_ref, sat_ref, ya_ref, yb_ref, p, rock, sat, sems):
    chunks, nx = p.shape[1], p.shape[2]
    ny = p_ref.shape[1]
    even = lax.rem(lax.axis_index("gy"), 2) == 0
    outs = ((ya_ref, even), (yb_ref, jnp.logical_not(even)))

    def copies(i):
        _, high = outs[i]
        tile = pl.ds(pl.multiple_of(jnp.where(high, ny - 8, 0), 8), 8)
        return [
            pltpu.make_async_copy(source.at[:, tile, pl.ds(c * LANES, LANES)], target.at[i, c], sems.at[i, n, c])
            for n, (source, target) in enumerate(((p_ref, p), (rock_ref, rock), (sat_ref, sat)))
            for c in range(chunks)
        ]

    for i in range(2):
        for copy in copies(i):
            copy.start()
    p2, rock2, sat2 = (f.reshape(2 * chunks * nx * 8, LANES) for f in (p, rock, sat))
    rows = (2 * REACH + 1) * nx
    for i, (out, high) in enumerate(outs):
        for copy in copies(i):
            copy.wait()
        first = jnp.where(high, 8 - REACH, 0)
        edge = jnp.where(high, 7, 0)
        for c in range(chunks):
            base = (i * chunks + c) * nx * 8
            for j in range(REACH):
                out[pl.ds(c * rows + j * nx, nx), :] = p2[pl.ds(base + first + j, nx, stride=8), :]
                kinds = rock2[pl.ds(base + first + j, nx, stride=8), :]
                out[pl.ds(c * rows + (REACH + j) * nx, nx), :] = kinds.astype(jnp.float32) + 1.0
            out[pl.ds(c * rows + 2 * REACH * nx, nx), :] = sat2[pl.ds(base + edge, nx, stride=8), :]


def pack_sides(pressure, rock_type, saturation):
    nx, _, nz = pressure.shape
    chunks = nz // LANES
    side = jax.ShapeDtypeStruct((chunks * (2 * REACH + 1) * nx, LANES), jnp.float32)
    block = (2, chunks, nx, 8, LANES)
    return pl.pallas_call(
        pack_sides_kernel,
        name="pack_sides",
        out_shape=(side, side),
        in_specs=[HBM] * 3,
        out_specs=(VMEM,) * 2,
        scratch_shapes=[
            pltpu.VMEM(block, jnp.float32),
            pltpu.VMEM(block, jnp.int32),
            pltpu.VMEM(block, jnp.float32),
            pltpu.SemaphoreType.DMA((2, 3, chunks)),
        ],
        compiler_params=pltpu.CompilerParams(vmem_limit_bytes=63 << 20),
    )(pressure, rock_type, saturation)


def pack_ends_kernel(p_ref, rock_ref, _, xa_ref, xb_ref, rock, sems):
    nx = p_ref.shape[0]
    even = lax.rem(lax.axis_index("gx"), 2) == 0
    copies = []
    for i, (out, high) in enumerate(((xa_ref, even), (xb_ref, jnp.logical_not(even)))):
        layers = pl.ds(jnp.where(high, nx - REACH, 0), REACH)
        copies.append((
            pltpu.make_async_copy(p_ref.at[layers], out.at[pl.ds(0, REACH)], sems.at[i, 0]),
            pltpu.make_async_copy(rock_ref.at[layers], rock.at[i], sems.at[i, 1]),
        ))
    for pair in copies:
        for copy in pair:
            copy.start()
    for i, out in enumerate((xa_ref, xb_ref)):
        copies[i][1].wait()
        for j in range(REACH):
            out[REACH + j] = rock[i, j].astype(jnp.float32) + 1.0
        copies[i][0].wait()


def pack_ends(pressure, rock_type, after):
    _, ny, nz = pressure.shape
    end = jax.ShapeDtypeStruct((2 * REACH, ny, nz), jnp.float32)
    return pl.pallas_call(
        pack_ends_kernel,
        name="pack_ends",
        out_shape=(end, end),
        in_specs=[HBM] * 2 + [pl.BlockSpec(memory_space=pl.ANY)],
        out_specs=(VMEM,) * 2,
        scratch_shapes=[pltpu.VMEM((2, REACH, ny, nz), jnp.int32), pltpu.SemaphoreType.DMA((2, 2))],
        compiler_params=pltpu.CompilerParams(vmem_limit_bytes=60 << 20),
    )(pressure, rock_type, after)


def corner_kernel(nx, ya_ref, yb_ref, _, ca_ref, cb_ref):
    rows = (2 * REACH + 1) * nx
    chunks = ya_ref.shape[0] // rows
    even_y = lax.rem(lax.axis_index("gy"), 2) == 0
    even_x = lax.rem(lax.axis_index("gx"), 2) == 0
    for out, high in ((ca_ref, even_x), (cb_ref, jnp.logical_not(even_x))):
        layer = jnp.where(high, nx - PASSES, 0)
        for c in range(chunks):
            for kind in range(2):
                for i in range(PASSES):
                    for side in range(2):
                        start = c * rows + (kind * REACH + 1 - side) * nx + layer + i
                        from_a = ya_ref[pl.ds(start, PASSES, stride=nx), :]
                        from_b = yb_ref[pl.ds(start, PASSES, stride=nx), :]
                        mine = jnp.where(even_y, from_b, from_a) if side == 0 else jnp.where(even_y, from_a, from_b)
                        at = ((c * 2 + kind) * PASSES + i) * 2 + side
                        out[pl.ds(at * PASSES, PASSES), :] = mine


def corners(side_a, side_b, nx, after):
    chunks = side_a.shape[0] // ((2 * REACH + 1) * nx)
    shape = jax.ShapeDtypeStruct((chunks * 4 * PASSES * PASSES, LANES), jnp.float32)
    return pl.pallas_call(
        functools.partial(corner_kernel, nx),
        name="corners",
        out_shape=(shape, shape),
        in_specs=[VMEM] * 2 + [pl.BlockSpec(memory_space=pl.ANY)],
        out_specs=(VMEM,) * 2,
        compiler_params=pltpu.CompilerParams(vmem_limit_bytes=4 << 20),
    )(side_a, side_b, after)


def fraction(water):
    denom = water * water + MOBILITY * (1.0 - water) ** 2
    return water * water / denom


def transmit(left, right):
    return 2.0 * left * right / jnp.maximum(left + right, 1e-30)


def look_up(table, kinds):
    return jnp.take_along_axis(table, kinds, axis=1, mode="promise_in_bounds")


def deeper(values):
    turned = [pltpu.roll(v, LANES - 1, 1) for v in values]
    last = lax.broadcasted_iota(jnp.int32, turned[0].shape, 1) == LANES - 1
    return [jnp.where(last, turned[(c + 1) % len(values)], turned[c]) for c in range(len(values))]


def shallower(values):
    turned = [pltpu.roll(v, 1, 1) for v in values]
    first = lax.broadcasted_iota(jnp.int32, turned[0].shape, 1) == 0
    return [jnp.where(first, turned[c - 1], turned[c]) for c in range(len(values))]


def upwind(flow, own, far):
    return jnp.maximum(flow, 0.0) * own + jnp.minimum(flow, 0.0) * far


def flat(ref):
    return ref.reshape(math.prod(ref.shape[:-1]), LANES)


def rock_tables(perm_ref, poro_ref):
    lane = lax.broadcasted_iota(jnp.int32, (8, LANES), 1)
    perm, poro = jnp.zeros((8, LANES), jnp.float32), jnp.zeros((8, LANES), jnp.float32)
    for kind in range(perm_ref.shape[0]):
        perm = jnp.where(lane == kind + 1, perm_ref[kind], perm)
        poro = jnp.where(lane == kind + 1, poro_ref[kind], poro)
    return perm, jnp.where(lane == 0, 1.0, COMPRESS * (VOLUME * poro))


def rates_kernel(nx, ny, cells_ref, rates_ref, out_ref):
    chunks, layers, pitch, _ = out_ref.shape
    rank_x, rank_y = lax.axis_index("gx"), lax.axis_index("gy")
    sub = lax.broadcasted_iota(jnp.int32, (8, LANES), 0)
    lane = lax.broadcasted_iota(jnp.int32, (8, LANES), 1)
    out2 = flat(out_ref)

    def clear(layer, _):
        for c in range(chunks):
            out_ref[c, layer] = jnp.zeros((pitch, LANES), jnp.float32)
        return 0

    lax.fori_loop(0, layers, clear, 0)

    def add_well(w, _):
        x = cells_ref[0, w] - rank_x * nx + REACH
        y = cells_ref[1, w] - rank_y * ny + PAD
        z = cells_ref[2, w]

        @pl.when((x >= 0) & (x < layers) & (y >= 0) & (y < pitch))
        def _():
            row = (lax.shift_right_logical(z, 7) * layers + x) * pitch + y
            tile = pl.multiple_of(lax.shift_left(lax.shift_right_logical(row, 3), 3), 8)
            here = (sub == row - tile) & (lane == lax.bitwise_and(z, LANES - 1))
            out2[pl.ds(tile, 8), :] = out2[pl.ds(tile, 8), :] + jnp.where(here, rates_ref[w], 0.0)

        return 0

    lax.fori_loop(0, cells_ref.shape[1], add_well, 0)


def wide_shape(block):
    nx, ny, nz = block
    return (nz // LANES, nx + 2 * REACH, ny + 2 * PAD, LANES)


def rates_field(block, well_cells, well_rates):
    return pl.pallas_call(
        functools.partial(rates_kernel, *block[:2]),
        name="rates",
        out_shape=jax.ShapeDtypeStruct(wide_shape(block), jnp.float32),
        in_specs=[SMEM] * 2,
        out_specs=VMEM,
        cost_estimate=pl.CostEstimate(flops=0, bytes_accessed=12 << 20, transcendentals=0),
        compiler_params=pltpu.CompilerParams(vmem_limit_bytes=4 << 20),
    )(well_cells, well_rates)


def ready_kernel(
    p_ref, rock_ref, sat_ref, xa_ref, xb_ref, rates_ref, perm_ref, poro_ref,
    press, perms, stores, trans_x, trans_y, trans_z, scale, drive, frac, slope, rock, sat, sems,
):
    chunks, layers, pitch, _ = press.shape
    _, nx, ny, _ = rock.shape
    depth, step = layers * pitch, ny // 8
    even_x = lax.rem(lax.axis_index("gx"), 2) == 0
    own_p = press.at[:, pl.ds(REACH, nx), pl.ds(PAD, ny), :]
    fetch(rock_ref, rock, sems.at[0], True)
    fetch(p_ref, own_p, sems.at[1], True)
    fetch(sat_ref, sat, sems.at[2], True)
    perm_table, store_table = rock_tables(perm_ref, poro_ref)
    zero = jnp.zeros((8, LANES), jnp.float32)
    lane = lax.broadcasted_iota(jnp.int32, (8, LANES), 1)

    def clear(layer, _):
        for c in range(chunks):
            for ref in (press, perms, stores):
                for t in (0, pitch // 8 - 1):
                    ref[c, layer, pl.ds(t * 8, 8), :] = zero
        return 0

    lax.fori_loop(0, layers, clear, 0)

    def look(layer, kinds_of):
        for c in range(chunks):
            for t in range(ny // 8):
                kind = kinds_of(c, t)
                perms[c, layer, pl.ds(PAD + t * 8, 8), :] = look_up(perm_table, kind)
                stores[c, layer, pl.ds(PAD + t * 8, 8), :] = look_up(store_table, kind)

    def look_ends(j, _):
        for c in range(chunks):
            a, b = (ref[j, :, pl.ds(c * LANES, LANES)] for ref in (xa_ref, xb_ref))
            press[c, j, pl.ds(PAD, ny), :] = jnp.where(even_x, b, a)
            press[c, REACH + nx + j, pl.ds(PAD, ny), :] = jnp.where(even_x, a, b)

        def side(low):
            def kinds_of(c, t):
                a, b = (ref[REACH + j, pl.ds(t * 8, 8), pl.ds(c * LANES, LANES)] for ref in (xa_ref, xb_ref))
                return (jnp.where(even_x, b, a) if low else jnp.where(even_x, a, b)).astype(jnp.int32)

            return kinds_of

        look(j, side(True))
        look(REACH + nx + j, side(False))
        return 0

    lax.fori_loop(0, REACH, look_ends, 0)
    fetch(rock_ref, rock, sems.at[0], False)

    def look_own(layer, _):
        look(REACH + layer, lambda c, t: rock[c, layer, pl.ds(t * 8, 8), :] + 1)
        return 0

    lax.fori_loop(0, nx, look_own, 0)
    fetch(p_ref, own_p, sems.at[1], False)

    press2, perms2, stores2, rates2 = map(flat, (press, perms, stores, rates_ref))
    tx2, ty2, tz2, scale2, drive2 = map(flat, (trans_x, trans_y, trans_z, scale, drive))

    def rows(layer, k, c):
        return pl.ds(c * depth + layer * pitch + PAD + k, 8, stride=step)

    def prepare(layer, _):
        perm = {k: [perms2[rows(layer, k, c), :] for c in range(chunks)] for k in range(-1, step + 1)}
        t_s = [transmit(perm[-1][c], perm[0][c]) for c in range(chunks)]
        for k in range(step):
            deep = deeper(perm[k])
            t_z = [transmit(perm[k][c], deep[c]) for c in range(chunks)]
            t_z[-1] = jnp.where(lane == LANES - 1, 0.0, t_z[-1])
            above = shallower(t_z)
            for c in range(chunks):
                at = rows(layer, k, c)
                t_x = transmit(perm[k][c], perms2[rows(layer + 1, k, c), :])
                t_n = transmit(perm[k][c], perm[k + 1][c])
                t_w = tx2[rows(jnp.maximum(layer - 1, 0), k, c), :]
                tx2[at, :], ty2[at, :], tz2[at, :] = t_x, t_n, t_z[c]
                store = stores2[at, :]
                factor = OMEGA / (store + ((t_x + t_w) + (t_n + t_s[c]) + (t_z[c] + above[c])))
                scale2[at, :] = factor
                drive2[at, :] = factor * (store * press2[at, :] + rates2[at, :])
                t_s[c] = t_n
        return 0

    lax.fori_loop(0, layers - 1, prepare, 0)
    fetch(sat_ref, sat, sems.at[2], False)

    def old_fraction(layer, _):
        for c in range(chunks):
            s = sat[c, layer]
            inverse = 1.0 / (s * s + MOBILITY * (1.0 - s) ** 2)
            frac[c, layer, pl.ds(PAD, ny), :] = s * s * inverse
            slope[c, layer] = 2.0 * MOBILITY * s * (1.0 - s) * (inverse * inverse)
        return 0

    lax.fori_loop(0, nx, old_fraction, 0)


def ready(pressure, rock_type, saturation, ends, rates, rock_perm, rock_poro):
    nx, ny, nz = pressure.shape
    chunks = nz // LANES
    assert ny % 8 == 0 and nz % LANES == 0
    wide = jax.ShapeDtypeStruct(wide_shape(pressure.shape), jnp.float32)
    block = (chunks, nx, ny, LANES)
    return pl.pallas_call(
        ready_kernel,
        name="ready",
        out_shape=(wide,) * 8 + (jax.ShapeDtypeStruct((chunks, nx, ny + 2 * PAD, LANES), jnp.float32), jax.ShapeDtypeStruct(block, jnp.float32)),
        in_specs=[HBM] * 3 + [VMEM] * 3 + [SMEM] * 2,
        out_specs=(VMEM,) * 10,
        scratch_shapes=[pltpu.VMEM(block, jnp.int32), pltpu.VMEM(block, jnp.float32), pltpu.SemaphoreType.DMA((3, chunks))],
        cost_estimate=pl.CostEstimate(flops=0, bytes_accessed=24 << 20, transcendentals=0),
        compiler_params=pltpu.CompilerParams(vmem_limit_bytes=4 << 20),
    )(pressure, rock_type, saturation, *ends, rates, rock_perm, rock_poro)


def flow_kernel(
    flux_ref, sat_ref, ya_ref, yb_ref, ca_ref, cb_ref, rates_ref, slope_ref, perm_ref, poro_ref, *refs
):
    press, perms, stores, trans_x, trans_y, trans_z, scale, drive, frac = refs[9:18]
    press_ref, prep_ref, inlet_ref, other, flux, sat, sems = refs[18:]
    chunks, layers, pitch, _ = press.shape
    _, nx, ny, _ = flux.shape
    depth, step = layers * pitch, ny // 8
    tiles = (ny + 2 * PASSES) // 8
    side_rows = (2 * REACH + 1) * nx
    even_x, even_y = lax.rem(lax.axis_index("gx"), 2) == 0, lax.rem(lax.axis_index("gy"), 2) == 0
    press2, other2, perms2, stores2, rates2, frac2 = map(flat, (press, other, perms, stores, rates_ref, frac))
    tx2, ty2, tz2, scale2, drive2 = map(flat, (trans_x, trans_y, trans_z, scale, drive))
    flux2, sat2, slope2 = map(flat, (flux, sat, slope_ref))
    fetch(flux_ref, flux, sems.at[0], True)
    fetch(sat_ref, sat, sems.at[1], True)
    perm_table, store_table = rock_tables(perm_ref, poro_ref)
    lane = lax.broadcasted_iota(jnp.int32, (8, LANES), 1)

    for c in range(chunks):
        for j in range(REACH):
            for half in range(nx // 8):
                start = c * side_rows + j * nx + half * 8
                at = c * depth + (REACH + half * 8) * pitch + j
                low = pl.ds(at + PAD - REACH, 8, stride=pitch)
                high = pl.ds(at + PAD + ny, 8, stride=pitch)
                a, b = ya_ref[pl.ds(start, 8), :], yb_ref[pl.ds(start, 8), :]
                press2[low, :], press2[high, :] = jnp.where(even_y, b, a), jnp.where(even_y, a, b)
                a, b = (ref[pl.ds(start + REACH * nx, 8), :].astype(jnp.int32) for ref in (ya_ref, yb_ref))
                for where, kind in ((low, jnp.where(even_y, b, a)), (high, jnp.where(even_y, a, b))):
                    perms2[where, :], stores2[where, :] = look_up(perm_table, kind), look_up(store_table, kind)
        start = c * side_rows + 2 * REACH * nx
        a, b = fraction(ya_ref[pl.ds(start, nx), :]), fraction(yb_ref[pl.ds(start, nx), :])
        at = c * nx * pitch
        frac2[pl.ds(at + PAD - 1, nx, stride=pitch), :] = jnp.where(even_y, b, a)
        frac2[pl.ds(at + PAD + ny, nx, stride=pitch), :] = jnp.where(even_y, a, b)
        both = 2 * PASSES
        for k in range(PASSES):
            start = (c * 2 * PASSES + k) * both
            a, b = ca_ref[pl.ds(start, both), :], cb_ref[pl.ds(start, both), :]
            ends = ((1 + k, jnp.where(even_x, b, a)), (REACH + nx + k, jnp.where(even_x, a, b)))
            start += PASSES * both
            a, b = (ref[pl.ds(start, both), :].astype(jnp.int32) for ref in (ca_ref, cb_ref))
            kinds = (jnp.where(even_x, b, a), jnp.where(even_x, a, b))
            for (layer, value), kind in zip(ends, kinds):
                for ref, new in ((press2, value), (perms2, look_up(perm_table, kind)), (stores2, look_up(store_table, kind))):
                    at = c * depth + layer * pitch + PAD
                    ref[pl.ds(at - PASSES, PASSES), :] = new[:PASSES]
                    ref[pl.ds(at + ny, PASSES), :] = new[PASSES:]

    def complete(group, _):
        for first in (PAD - PASSES, PAD + ny - 1):
            def rows(k, by, c):
                return pl.ds(c * depth + (1 + group * 8 + by) * pitch + first + k, 8, stride=pitch)

            perm = {k: [perms2[rows(k, 0, c), :] for c in range(chunks)] for k in range(-1, PASSES + 2)}
            t_s = [transmit(perm[-1][c], perm[0][c]) for c in range(chunks)]
            for c in range(chunks):
                ty2[rows(-1, 0, c), :] = t_s[c]
            for k in range(PASSES + 1):
                deep = deeper(perm[k])
                t_z = [transmit(perm[k][c], deep[c]) for c in range(chunks)]
                t_z[-1] = jnp.where(lane == LANES - 1, 0.0, t_z[-1])
                above = shallower(t_z)
                for c in range(chunks):
                    at = rows(k, 0, c)
                    t_x = transmit(perm[k][c], perms2[rows(k, 1, c), :])
                    t_w = transmit(perm[k][c], perms2[rows(k, -1, c), :])
                    t_n = transmit(perm[k][c], perm[k + 1][c])
                    tx2[at, :], ty2[at, :], tz2[at, :] = t_x, t_n, t_z[c]
                    store = stores2[at, :]
                    factor = OMEGA / (store + ((t_x + t_w) + (t_n + t_s[c]) + (t_z[c] + above[c])))
                    scale2[at, :] = factor
                    drive2[at, :] = factor * (store * press2[at, :] + rates2[at, :])
                    t_s[c] = t_n
        return 0

    lax.fori_loop(0, (layers - 2) // 8, complete, 0)

    def relax(source, target, number):
        def one(layer, _):
            def rows(k, c, by=0):
                return pl.ds(c * depth + (layer + by) * pitch + PAD - PASSES + k, 8, stride=tiles)

            now = {k: [source[rows(k, c), :] for c in range(chunks)] for k in range(-1, tiles + 1)}
            for k in range(tiles):
                here = now[k]
                t_z = [tz2[rows(k, c), :] for c in range(chunks)]
                deep = deeper(here)
                shallow = shallower([t_z[c] * here[c] for c in range(chunks)])
                for c in range(chunks):
                    at = rows(k, c)
                    total = (
                        (tx2[at, :] * source[rows(k, c, 1), :] + tx2[rows(k, c, -1), :] * source[rows(k, c, -1), :])
                        + (ty2[at, :] * now[k + 1][c] + ty2[rows(k - 1, c), :] * now[k - 1][c])
                        + (t_z[c] * deep[c] + shallow[c])
                    )
                    target[at, :] = (1.0 - OMEGA) * here[c] + (drive2[at, :] + scale2[at, :] * total)
            return 0

        lax.fori_loop(min(number + 1, REACH), layers - number, one, 0, unroll=UNROLL)

    for number in range(1, PASSES + 1):
        source, target = (press2, other2) if number % 2 else (other2, press2)
        relax(source, target, number)
    final, final2 = (press, press2) if PASSES % 2 == 0 else (other, other2)

    def send_out(start):
        for c in range(chunks):
            copy = pltpu.make_async_copy(
                final.at[c, pl.ds(REACH, nx), pl.ds(PAD, ny), :], press_ref.at[:, :, pl.ds(c * LANES, LANES)], sems.at[2, c]
            )
            copy.start() if start else copy.wait()

    send_out(True)
    fetch(flux_ref, flux, sems.at[0], False)
    fetch(sat_ref, sat, sems.at[1], False)
    for c in range(chunks):
        inlet_ref[pl.ds(c * ny, ny), :] = flux[c, 0]

    def fluxes(layer, _):
        def wide(ref, k, by=0):
            return [ref[pl.ds(c * depth + (REACH + layer + by) * pitch + PAD + k, 8, stride=step), :] for c in range(chunks)]

        def own(ref, k):
            return [ref[pl.ds((c * nx + layer) * ny + k, 8, stride=step), :] for c in range(chunks)]

        here = {k: wide(final2, k) for k in range(-1, step + 1)}
        old = {
            k: [frac2[pl.ds((c * nx + layer) * pitch + PAD + k, 8, stride=step), :] for c in range(chunks)]
            for k in range(-1, step + 1)
        }
        south = None
        for k in range(-1, step):
            t_y = wide(ty2, k)
            north = [upwind(t_y[c] * (here[k][c] - here[k + 1][c]), old[k][c], old[k + 1][c]) for c in range(chunks)]
            if k >= 0:
                t_z, below, old_below = wide(tz2, k), deeper(here[k]), deeper(old[k])
                down = [upwind(t_z[c] * (here[k][c] - below[c]), old[k][c], old_below[c]) for c in range(chunks)]
                from_above = shallower(down)
                east, t_x, rate, store = wide(final2, k, 1), wide(tx2, k), wide(rates2, k), wide(stores2, k)
                imposed, water, bend = own(flux2, k), own(sat2, k), own(slope2, k)
                for c in range(chunks):
                    leaving = (north[c] - south[c]) + (down[c] - from_above[c])
                    explicit = jnp.maximum(rate[c], 0.0) + jnp.minimum(rate[c], 0.0) * old[k][c] - leaving
                    through = jnp.maximum(imposed[c] + t_x[c] * (here[k][c] - east[c]), 0.0)
                    volume = store[c] * (1.0 / COMPRESS)
                    gain = 1.0 / (volume + through * bend[c])
                    first = water[c] - (through * old[k][c] - explicit) * gain
                    for i, value in enumerate((first, gain, through, volume, volume * water[c] + explicit)):
                        prep_ref[layer, pl.ds((i * chunks + c) * ny + k, 8, stride=step), :] = value
            south = north
        return 0

    lax.fori_loop(0, nx, fluxes, 0)
    send_out(False)


def flow(base_flux, saturation, sides, ends_corner, rates, made, rock_perm, rock_poro):
    nx, ny, nz = base_flux.shape
    chunks = nz // LANES
    *fields, slope = made
    block = pltpu.VMEM((chunks, nx, ny, LANES), jnp.float32)
    inputs = (base_flux, saturation, *sides, *ends_corner, rates, slope, rock_perm, rock_poro, *fields)
    first = len(inputs) - len(fields)
    return pl.pallas_call(
        flow_kernel,
        name="flow",
        out_shape=tuple(jax.ShapeDtypeStruct(f.shape, f.dtype) for f in fields) + (
            jax.ShapeDtypeStruct(base_flux.shape, jnp.float32),
            jax.ShapeDtypeStruct((nx, 5 * chunks * ny, LANES), jnp.float32),
            jax.ShapeDtypeStruct((chunks * ny, LANES), jnp.float32),
        ),
        in_specs=[HBM] * 2 + [VMEM] * 6 + [SMEM] * 2 + [VMEM] * len(fields),
        out_specs=(VMEM,) * len(fields) + (HBM, VMEM, VMEM),
        input_output_aliases={first + i: i for i in range(len(fields))},
        scratch_shapes=[pltpu.VMEM(wide_shape(base_flux.shape), jnp.float32), block, block, pltpu.SemaphoreType.DMA((3, chunks))],
        compiler_params=pltpu.CompilerParams(vmem_limit_bytes=8 << 20),
    )(*inputs)[-3:]


def stage_kernel(stage, inflow_ref, prep_ref, *refs):
    sat_ref, out_ref, sat, out_sems = refs[-4:]
    nx, rows, _ = prep_ref.shape
    plane = rows // 5
    chunks, _, ny, _ = sat.shape

    @pl.when(lax.axis_index("gx") == stage)
    def _():
        def send(layer):
            return [
                pltpu.make_async_copy(sat.at[c, layer], sat_ref.at[layer, :, pl.ds(c * LANES, LANES)], out_sems.at[layer, c])
                for c in range(chunks)
            ]

        def advance(layer, incoming):
            first, gain, through, volume, held = (prep_ref[layer, pl.ds(i * plane, plane), :] for i in range(5))
            known = held + incoming
            water = jnp.clip(first + gain * incoming, 0.0, 1.0)
            for _ in range(NEWTON - 1):
                square = water * water
                part = 1.5 * square
                denom = part + (0.5 - water)
                denom = denom * denom
                top = denom * known + through * (square * (0.5 - part))
                bottom = denom * volume + through * (water - square)
                water = jnp.clip(top / bottom, 0.0, 1.0)
            for c in range(chunks):
                sat[c, layer] = water[c * ny : (c + 1) * ny]
            for copy in send(layer):
                copy.start()
            square = water * water
            return (through * square) / (1.5 * square + (0.5 - water))

        out_ref[...] = lax.fori_loop(0, nx, advance, inflow_ref[...])

        def finish(layer, _):
            for copy in send(layer):
                copy.wait()
            return 0

        lax.fori_loop(0, nx, finish, 0)


def run_stage(stage, inflow, prep, shape, saturation):
    nx, ny, nz = shape
    chunks = nz // LANES
    block = jax.ShapeDtypeStruct(shape, jnp.float32)
    return pl.pallas_call(
        functools.partial(stage_kernel, stage),
        name="stage",
        out_shape=(block, jax.ShapeDtypeStruct(inflow.shape, jnp.float32)),
        in_specs=[VMEM, VMEM] + [HBM] * len(saturation),
        out_specs=(HBM, VMEM),
        input_output_aliases={2: 0} if saturation else {},
        scratch_shapes=[
            pltpu.VMEM((chunks, nx, ny, LANES), jnp.float32),
            pltpu.SemaphoreType.DMA((nx, chunks)),
        ],
        compiler_params=pltpu.CompilerParams(vmem_limit_bytes=12 << 20),
    )(inflow, prep, *saturation)


def step(rock_type, rock_perm, rock_poro, base_flux, initial_pressure, old_saturation, well_cells, well_rates):
    nx = rock_type.shape[0]
    sides = pack_sides(initial_pressure, rock_type, old_saturation)
    sides_got = swap(*sides, "gy")
    ends = swap(*pack_ends(initial_pressure, rock_type, sides[0]), "gx")
    rates = rates_field(rock_type.shape, well_cells, well_rates)
    made = ready(initial_pressure, rock_type, old_saturation, ends, rates, rock_perm, rock_poro)
    ends_corner = swap(*corners(*sides_got, nx, made[-1]), "gx")
    pressure, prep, inflow = flow(base_flux, old_saturation, sides_got, ends_corner, rates, made, rock_perm, rock_poro)
    saturation = ()
    count = lax.axis_size("gx")
    for stage in range(count):
        *saturation, outflow = run_stage(stage, inflow, prep, rock_type.shape, saturation)
        if stage < count - 1:
            inflow = lax.ppermute(outflow, "gx", [(stage, stage + 1)])
    return pressure, saturation[0]


def solution(mesh):
    return jax.shard_map(
        step,
        mesh=mesh,
        in_specs=(
            P("gx", "gy", None),
            P(),
            P(),
            P("gx", "gy", None),
            P("gx", "gy", None),
            P("gx", "gy", None),
            P(),
            P(),
        ),
        out_specs=(P("gx", "gy", None), P("gx", "gy", None)),
        check_vma=False,
    )
```

time: 97.9 us -> 70.3 us (0.72)
  the two profiles are of different devices: /device:TPU:7 before, /device:TPU:11 now
where the time goes in v2:
time: 70.3 us; the launch traced here: 70 us
  Pallas kernels  38.5 us (55%)
  waiting for transfers between devices  20.8 us (30%)
  starting transfers between devices  9.72 us (14%)
  between operations  0.89 us (1%)
    ppermute x3, waiting for transfers between devices, step(): inflow = lax.ppermute(outflow, 'gx', [(stage, stage + 1)])  17.1 us
    pallas_call x1, Pallas kernels, flow(): pl.pallas_call(flow_kernel, name='flow', out_shape=tuple((jax.ShapeDtypeS...  14.7 us
    pallas_call x1, Pallas kernels, ready(): pl.pallas_call(ready_kernel, name='ready', out_shape=(wide,) * 8 + (jax.S...  9.84 us
    pallas_call x4, Pallas kernels, run_stage(): pl.pallas_call(functools.partial(stage_kernel, stage), name='stage', out_...  5.5 us
    ppermute x3, starting transfers between devices, swap(): got_b = lax.ppermute(value_b, axis, pairs_b)  4.38 us
    ppermute x3, waiting for transfers between devices, swap(): got_a = lax.ppermute(value_a, axis, pairs_a)  3.72 us
    pallas_call x1, Pallas kernels, rates_field(): pl.pallas_call(functools.partial(rates_kernel, *block[:2]), name='rates',...  3.24 us
    ppermute x3, starting transfers between devices, swap(): got_a = lax.ppermute(value_a, axis, pairs_a)  2.72 us
  transfers between devices with their start and end apart: 9, of which 3 were waited for; matrix products, arithmetic and copies ran while one was open for 0% of the time, Pallas kernels for 19%

profile of v2, /device:TPU:11, one launch (start us, length us, event | category | flops | bytes accessed | tf_op | source)
XLA Modules:
  0.0 70.0 jit_solution(14049691770162499199)
XLA Ops:
  0.6 0.0 copy-start.7
  0.6 0.0 copy-start.4
  0.6 2.5 %pack_sides.1 = (f32[704,128]{1,0:T(8,128)}, f32[704,128]{1,0:T(8,128)}) custom-call(f32[16,32,512]{2,1,0:T(8,128)} %p_ref.5, s32[16,32,512]{2,1,0:T(8,128)} %rock_ref.5, f32[16,32,512]{2,1,0:T(8,128)} %sat_ref.5), custom_call_target="tpu_custom_call" | custom-call | tf_op jit(solution)/shard_map/pack_sides/pallas_call | solution.py:90
  3.2 0.0 copy-start
  3.2 0.0 copy-start.1
  3.2 0.0 copy-start.2
  3.2 0.0 copy-start.5
  3.2 0.0 copy-start.6
  3.2 2.5 %pack_ends.1 = (f32[10,32,512]{2,1,0:T(8,128)}, f32[10,32,512]{2,1,0:T(8,128)}) custom-call(f32[16,32,512]{2,1,0:T(8,128)} %p_ref.5, s32[16,32,512]{2,1,0:T(8,128)} %rock_ref.5, f32[704,128]{1,0:T(8,128)} %get-tuple-element.28._), custom_call_target="tpu_custom_call" | custom-call | tf_op jit(solution)/shard_map/pack_ends/pallas_call | solution.py:129
  5.8 0.7 %collective-permute-start.2 = (f32[10,32,512]{2,1,0:T(8,128)}, f32[10,32,512]{2,1,0:T(8,128)S(1)}, u32[]{:S(2)}, u32[]{:S(2)}) collective-permute-start(f32[10,32,512]{2,1,0:T(8,128)} %get-tuple-element.30), channel_id=1, source_target_pairs={{0,8},{16,24},{8,0},{24,16},{1,9},{17,25},{9,1},{25,17},{2,10},{18... | collective-permute-start | bytes 1966088 | tf_op jit(solution)/shard_map/ppermute | solution.py:40
  6.5 0.7 collective-permute-start.3
  7.2 3.0 %collective-permute-start.1 = (f32[704,128]{1,0:T(8,128)}, f32[704,128]{1,0:T(8,128)S(1)}, u32[]{:S(2)}, u32[]{:S(2)}) collective-permute-start(f32[704,128]{1,0:T(8,128)} %get-tuple-element.29), channel_id=1, source_target_pairs={{1,2},{3,4},{5,6},{2,1},{4,3},{6,5},{9,10},{11,12},{13,14},{10,9},... | collective-permute-start | bytes 1081352 | tf_op jit(solution)/shard_map/ppermute | solution.py:41
  10.3 1.4 %collective-permute-start = (f32[704,128]{1,0:T(8,128)}, f32[704,128]{1,0:T(8,128)S(1)}, u32[]{:S(2)}, u32[]{:S(2)}) collective-permute-start(f32[704,128]{1,0:T(8,128)} %get-tuple-element.28._), channel_id=1, source_target_pairs={{0,1},{2,3},{4,5},{6,7},{1,0},{3,2},{5,4},{7,6},{8,9},{10,11},{12,... | collective-permute-start | bytes 1081352 | tf_op jit(solution)/shard_map/ppermute | solution.py:40
  11.7 0.0 copy-done.7
  11.7 0.0 copy-done.4
  11.7 3.2 %rates.1.rates_ref = f32[4,26,48,128]{3,2,1,0:T(8,128)S(1)} custom-call(s32[3,128]{1,0:T(4,128)S(1)} %copy-done.4, f32[128]{0:T(128)S(1)} %copy-done.7), custom_call_target="tpu_custom_call" | custom-call | bytes 12582912 | tf_op jit(solution)/shard_map/rates/pallas_call | solution.py:251
  14.9 0.0 copy-start.3
  14.9 0.0 collective-permute-done.2.xa_ref
  14.9 0.0 collective-permute-done.3.xb_ref
  15.0 0.0 copy-done
  15.0 0.0 copy-done.1
  15.0 0.0 copy-done.2
  15.0 0.0 copy-done.5
  15.0 0.0 copy-done.6
  15.0 9.8 %ready.1 = (f32[4,26,48,128]{3,2,1,0:T(8,128)S(1)}, f32[4,26,48,128]{3,2,1,0:T(8,128)S(1)}, f32[4,26,48,128]{3,2,1,0:T(8,128)S(1)}, f32[4,26,48,128]{3,2,1,0:T(8...) custom-call(f32[16,32,512]{2,1,0:T(8,128)S(1)} %copy-done, ...), custom_call_target="tpu_custom_call" | custom-call | bytes 25165824 | tf_op jit(solution)/shard_map/ready/pallas_call | solution.py:368
  24.9 0.0 collective-permute-done.1.yb_ref
  24.9 3.4 %collective-permute-done.ya_ref = f32[704,128]{1,0:T(8,128)S(1)} collective-permute-done((f32[704,128]{1,0:T(8,128)}, f32[704,128]{1,0:T(8,128)S(1)}, u32[]{:S(2)}, u32[]{:S(2)}) %collective-permute-start) | collective-permute-done | bytes 360480 | tf_op jit(solution)/shard_map/ppermute | solution.py:40
  28.3 0.2 corners.1
  28.4 0.6 collective-permute-start.4
  29.0 0.7 collective-permute-start.5
  29.7 0.3 collective-permute-done.4.ca_ref
  30.0 0.0 collective-permute-done.5.cb_ref
  30.0 0.0 copy-done.3
  30.0 14.7 %flow.1 = (f32[4,26,48,128]{3,2,1,0:T(8,128)S(1)}, f32[4,26,48,128]{3,2,1,0:T(8,128)S(1)}, f32[4,26,48,128]{3,2,1,0:T(8,128)S(1)}, f32[4,26,48,128]{3,2,1,0:T(8,...) custom-call(f32[16,32,512]{2,1,0:T(8,128)S(1)} %copy-done.3, ...), custom_call_target="tpu_custom_call", output_to_operand_aliasing={{0}: (10, {}), {1}: (11, {}), {2}: (12, {}), {3}: (13, {}),... | custom-call | tf_op jit(solution)/shard_map/flow/pallas_call | solution.py:545
  44.7 0.6 stage.4
  45.3 0.7 collective-permute-start.6
  46.0 0.0 collective-permute-done.6.inflow_ref
  46.0 0.6 stage.5
  46.6 0.7 collective-permute-start.7
  47.3 0.0 collective-permute-done.7.inflow_ref
  47.3 0.6 stage.6
  47.9 1.3 %collective-permute-start.8 = (f32[128,128]{1,0:T(8,128)S(1)}, f32[128,128]{1,0:T(8,128)S(1)}, u32[]{:S(2)}, u32[]{:S(2)}) collective-permute-start(f32[128,128]{1,0:T(8,128)S(1)} %get-tuple-element.51), channel_id=1, source_target_pairs={{16,24},{17,25},{18,26},{19,27},{20,28},{21,29},{22,30},{23,31}} | collective-permute-start | bytes 196616 | tf_op jit(solution)/shard_map/ppermute | solution.py:637
  49.2 17.1 %collective-permute-done.8.inflow_ref = f32[128,128]{1,0:T(8,128)S(1)} collective-permute-done((f32[128,128]{1,0:T(8,128)S(1)}, f32[128,128]{1,0:T(8,128)S(1)}, u32[]{:S(2)}, u32[]{:S(2)}) %collective-permute-start.8) | collective-permute-done | bytes 65568 | tf_op jit(solution)/shard_map/ppermute | solution.py:637
  66.3 3.7 %stage.7 = (f32[16,32,512]{2,1,0:T(8,128)}, f32[128,128]{1,0:T(8,128)}) custom-call(f32[128,128]{1,0:T(8,128)S(1)} %collective-permute-done.8.inflow_ref, f32[16,640,128]{2,1,0:T(8,128)S(1)} %get-tuple-element.46.prep_ref, f32[16,32,512]{2,1,0:T(8,128)} %get-tuple-element.52.refs_0_), custom_call_target="tpu_custom_call", output_to_operand_aliasing={{0}: (2, {})} | custom-call | tf_op jit(solution)/shard_map/stage/pallas_call | solution.py:608
Async XLA Ops:
  0.6 11.0 %copy-start.7 = (f32[128]{0:T(128)S(1)}, f32[128]{0:T(128)}, u32[]{:S(2)}) copy-start(f32[128]{0:T(128)} %rates_ref.1) | copy-start | bytes 1540
  0.6 11.0 %copy-start.4 = (s32[3,128]{1,0:T(4,128)S(1)}, s32[3,128]{1,0:T(4,128)}, u32[]{:S(2)}) copy-start(s32[3,128]{1,0:T(4,128)} %cells_ref.1) | copy-start | bytes 4612
  3.2 11.8 %copy-start = (f32[16,32,512]{2,1,0:T(8,128)S(1)}, f32[16,32,512]{2,1,0:T(8,128)}, u32[]{:S(2)}) copy-start(f32[16,32,512]{2,1,0:T(8,128)} %p_ref.5) | copy-start | bytes 3145732
  3.2 11.8 %copy-start.1 = (s32[16,32,512]{2,1,0:T(8,128)S(1)}, s32[16,32,512]{2,1,0:T(8,128)}, u32[]{:S(2)}) copy-start(s32[16,32,512]{2,1,0:T(8,128)} %rock_ref.5) | copy-start | bytes 3145732
  3.2 11.8 %copy-start.2 = (f32[16,32,512]{2,1,0:T(8,128)S(1)}, f32[16,32,512]{2,1,0:T(8,128)}, u32[]{:S(2)}) copy-start(f32[16,32,512]{2,1,0:T(8,128)} %sat_ref.5) | copy-start | bytes 3145732
  3.2 11.8 %copy-start.5 = (f32[8]{0:T(128)S(1)}, f32[8]{0:T(128)}, u32[]{:S(2)}) copy-start(f32[8]{0:T(128)} %perm_ref.3) | copy-start | bytes 100
  3.2 11.8 %copy-start.6 = (f32[8]{0:T(128)S(1)}, f32[8]{0:T(128)}, u32[]{:S(2)}) copy-start(f32[8]{0:T(128)} %poro_ref.3) | copy-start | bytes 100
  5.8 9.2 %collective-permute-start.2 = (f32[10,32,512]{2,1,0:T(8,128)}, f32[10,32,512]{2,1,0:T(8,128)S(1)}, u32[]{:S(2)}, u32[]{:S(2)}) collective-permute-start(f32[10,32,512]{2,1,0:T(8,128)} %get-tuple-element.30), channel_id=1, source_target_pairs={{0,8},{16,24},{8,0},{24,16},{1,9},{17,25},{9,1},{25,17},{2,10},{18... | collective-permute-start | bytes 1966088 | tf_op jit(solution)/shard_map/ppermute | solution.py:40
  6.5 8.4 %collective-permute-start.3 = (f32[10,32,512]{2,1,0:T(8,128)}, f32[10,32,512]{2,1,0:T(8,128)S(1)}, u32[]{:S(2)}, u32[]{:S(2)}) collective-permute-start(f32[10,32,512]{2,1,0:T(8,128)} %get-tuple-element.31), channel_id=1, source_target_pairs={{8,16},{16,8},{9,17},{17,9},{10,18},{18,10},{11,19},{19,11},{12,20... | collective-permute-start | bytes 1966088 | tf_op jit(solution)/shard_map/ppermute | solution.py:41
  7.2 17.7 %collective-permute-start.1 = (f32[704,128]{1,0:T(8,128)}, f32[704,128]{1,0:T(8,128)S(1)}, u32[]{:S(2)}, u32[]{:S(2)}) collective-permute-start(f32[704,128]{1,0:T(8,128)} %get-tuple-element.29), channel_id=1, source_target_pairs={{1,2},{3,4},{5,6},{2,1},{4,3},{6,5},{9,10},{11,12},{13,14},{10,9},... | collective-permute-start | bytes 1081352 | tf_op jit(solution)/shard_map/ppermute | solution.py:41
  10.3 18.0 %collective-permute-start = (f32[704,128]{1,0:T(8,128)}, f32[704,128]{1,0:T(8,128)S(1)}, u32[]{:S(2)}, u32[]{:S(2)}) collective-permute-start(f32[704,128]{1,0:T(8,128)} %get-tuple-element.28._), channel_id=1, source_target_pairs={{0,1},{2,3},{4,5},{6,7},{1,0},{3,2},{5,4},{7,6},{8,9},{10,11},{12,... | collective-permute-start | bytes 1081352 | tf_op jit(solution)/shard_map/ppermute | solution.py:40
  14.9 15.1 %copy-start.3 = (f32[16,32,512]{2,1,0:T(8,128)S(1)}, f32[16,32,512]{2,1,0:T(8,128)}, u32[]{:S(2)}) copy-start(f32[16,32,512]{2,1,0:T(8,128)} %flux_ref.1) | copy-start | bytes 3145732
  28.4 1.5 %collective-permute-start.4 = (f32[256,128]{1,0:T(8,128)S(1)}, f32[256,128]{1,0:T(8,128)S(1)}, u32[]{:S(2)}, u32[]{:S(2)}) collective-permute-start(f32[256,128]{1,0:T(8,128)S(1)} %get-tuple-element.33), channel_id=1, source_target_pairs={{0,8},{16,24},{8,0},{24,16},{1,9},{17,25},{9,1},{25,17},{2,10},{18... | collective-permute-start | bytes 393224 | tf_op jit(solution)/shard_map/ppermute | solution.py:40
  29.0 1.0 %collective-permute-start.5 = (f32[256,128]{1,0:T(8,128)S(1)}, f32[256,128]{1,0:T(8,128)S(1)}, u32[]{:S(2)}, u32[]{:S(2)}) collective-permute-start(f32[256,128]{1,0:T(8,128)S(1)} %get-tuple-element.34), channel_id=1, source_target_pairs={{8,16},{16,8},{9,17},{17,9},{10,18},{18,10},{11,19},{19,11},{12,20... | collective-permute-start | bytes 393224 | tf_op jit(solution)/shard_map/ppermute | solution.py:41
  45.3 0.7 collective-permute-start.6
  46.6 0.7 collective-permute-start.7
  47.9 18.4 %collective-permute-start.8 = (f32[128,128]{1,0:T(8,128)S(1)}, f32[128,128]{1,0:T(8,128)S(1)}, u32[]{:S(2)}, u32[]{:S(2)}) collective-permute-start(f32[128,128]{1,0:T(8,128)S(1)} %get-tuple-element.51), channel_id=1, source_target_pairs={{16,24},{17,25},{18,26},{19,27},{20,28},{21,29},{22,30},{23,31}} | collective-permute-start | bytes 196616 | tf_op jit(solution)/shard_map/ppermute | solution.py:637

commit v3 on v2

--- a/solution.py
+++ b/solution.py
@@ -19,8 +19,10 @@
 
 LANES = 128
 UNROLL = 2
+ENDS_LIMIT = 59 << 20
+SIDES_LIMIT = 62 << 20
 REACH = PASSES + 1
-PAD = 8
+PAD = REACH + 1
 HBM = pl.BlockSpec(memory_space=pltpu.MemorySpace.HBM)
 VMEM = pl.BlockSpec(memory_space=pltpu.VMEM)
 SMEM = pl.BlockSpec(memory_space=pltpu.SMEM)
@@ -99,7 +101,7 @@
             pltpu.VMEM(block, jnp.float32),
             pltpu.SemaphoreType.DMA((2, 3, chunks)),
         ],
-        compiler_params=pltpu.CompilerParams(vmem_limit_bytes=63 << 20),
+        compiler_params=pltpu.CompilerParams(vmem_limit_bytes=SIDES_LIMIT),
     )(pressure, rock_type, saturation)
 
 
@@ -133,7 +135,7 @@
         in_specs=[HBM] * 2 + [pl.BlockSpec(memory_space=pl.ANY)],
         out_specs=(VMEM,) * 2,
         scratch_shapes=[pltpu.VMEM((2, REACH, ny, nz), jnp.int32), pltpu.SemaphoreType.DMA((2, 2))],
-        compiler_params=pltpu.CompilerParams(vmem_limit_bytes=60 << 20),
+        compiler_params=pltpu.CompilerParams(vmem_limit_bytes=ENDS_LIMIT),
     )(pressure, rock_type, after)
 
 
@@ -211,121 +213,82 @@
     return perm, jnp.where(lane == 0, 1.0, COMPRESS * (VOLUME * poro))
 
 
-def rates_kernel(nx, ny, cells_ref, rates_ref, out_ref):
-    chunks, layers, pitch, _ = out_ref.shape
+def rates_kernel(block, cells_ref, rates_ref, out_ref):
+    (nx, ny, _), (_, layers, pitch) = block, wide_sizes(block)
     rank_x, rank_y = lax.axis_index("gx"), lax.axis_index("gy")
     sub = lax.broadcasted_iota(jnp.int32, (8, LANES), 0)
     lane = lax.broadcasted_iota(jnp.int32, (8, LANES), 1)
-    out2 = flat(out_ref)
-
-    def clear(layer, _):
-        for c in range(chunks):
-            out_ref[c, layer] = jnp.zeros((pitch, LANES), jnp.float32)
+    share = out_ref.shape[0] // layers
+    low_x, low_y = rank_x * nx - REACH, rank_y * ny - PAD
+
+    def clear(i, _):
+        out_ref[pl.ds(pl.multiple_of(i * share, 8), share), :] = jnp.zeros((share, LANES), jnp.float32)
         return 0
 
     lax.fori_loop(0, layers, clear, 0)
 
-    def add_well(w, _):
-        x = cells_ref[0, w] - rank_x * nx + REACH
-        y = cells_ref[1, w] - rank_y * ny + PAD
-        z = cells_ref[2, w]
-
-        @pl.when((x >= 0) & (x < layers) & (y >= 0) & (y < pitch))
+    def some_wells(first, count):
+        def place(w):
+            return cells_ref[0, w] - low_x, cells_ref[1, w] - low_y
+
+        near = [(x >= 0) & (x < layers) & (y >= 0) & (y < pitch) for x, y in map(place, (first + i for i in range(count)))]
+
+        @pl.when(functools.reduce(jnp.logical_or, near))
         def _():
-            row = (lax.shift_right_logical(z, 7) * layers + x) * pitch + y
-            tile = pl.multiple_of(lax.shift_left(lax.shift_right_logical(row, 3), 3), 8)
-            here = (sub == row - tile) & (lane == lax.bitwise_and(z, LANES - 1))
-            out2[pl.ds(tile, 8), :] = out2[pl.ds(tile, 8), :] + jnp.where(here, rates_ref[w], 0.0)
-
-        return 0
-
-    lax.fori_loop(0, cells_ref.shape[1], add_well, 0)
+            for i in range(count):
+                @pl.when(near[i])
+                def _(w=first + i):
+                    (x, y), z = place(w), cells_ref[2, w]
+                    row = (lax.shift_right_logical(z, 7) * layers + x) * pitch + y
+                    tile = pl.multiple_of(lax.shift_left(lax.shift_right_logical(row, 3), 3), 8)
+                    here = (sub == row - tile) & (lane == lax.bitwise_and(z, LANES - 1))
+                    out_ref[pl.ds(tile, 8), :] = out_ref[pl.ds(tile, 8), :] + jnp.where(here, rates_ref[w], 0.0)
+
+    wells, batch = cells_ref.shape[1], 8
+
+    def wells_of(i, _):
+        some_wells(i * batch, batch)
+        return 0
+
+    lax.fori_loop(0, wells // batch, wells_of, 0)
+    if wells % batch:
+        some_wells(wells - wells % batch, wells % batch)
+
+
+def wide_sizes(block):
+    nx, ny, nz = block
+    return nz // LANES, nx + 2 * REACH, ny + 2 * PAD
 
 
 def wide_shape(block):
-    nx, ny, nz = block
-    return (nz // LANES, nx + 2 * REACH, ny + 2 * PAD, LANES)
+    rows = math.prod(wide_sizes(block))
+    assert block[0] % 8 == 0 and block[1] % 8 == 0 and block[2] % LANES == 0
+    return jax.ShapeDtypeStruct((rows, LANES), jnp.float32)
 
 
 def rates_field(block, well_cells, well_rates):
     return pl.pallas_call(
-        functools.partial(rates_kernel, *block[:2]),
+        functools.partial(rates_kernel, block),
         name="rates",
-        out_shape=jax.ShapeDtypeStruct(wide_shape(block), jnp.float32),
+        out_shape=wide_shape(block),
         in_specs=[SMEM] * 2,
         out_specs=VMEM,
-        cost_estimate=pl.CostEstimate(flops=0, bytes_accessed=12 << 20, transcendentals=0),
+        cost_estimate=pl.CostEstimate(flops=0, bytes_accessed=6 << 20, transcendentals=0),
         compiler_params=pltpu.CompilerParams(vmem_limit_bytes=4 << 20),
     )(well_cells, well_rates)
 
 
-def ready_kernel(
-    p_ref, rock_ref, sat_ref, xa_ref, xb_ref, rates_ref, perm_ref, poro_ref,
-    press, perms, stores, trans_x, trans_y, trans_z, scale, drive, frac, slope, rock, sat, sems,
-):
-    chunks, layers, pitch, _ = press.shape
-    _, nx, ny, _ = rock.shape
-    depth, step = layers * pitch, ny // 8
-    even_x = lax.rem(lax.axis_index("gx"), 2) == 0
-    own_p = press.at[:, pl.ds(REACH, nx), pl.ds(PAD, ny), :]
-    fetch(rock_ref, rock, sems.at[0], True)
-    fetch(p_ref, own_p, sems.at[1], True)
-    fetch(sat_ref, sat, sems.at[2], True)
-    perm_table, store_table = rock_tables(perm_ref, poro_ref)
-    zero = jnp.zeros((8, LANES), jnp.float32)
+def prepare_layers(block, fields, rates, first, last):
+    press, perms, stores, trans_x, trans_y, trans_z, scale, drive = fields
+    chunks, layers, pitch = wide_sizes(block)
+    step = block[1] // 8
     lane = lax.broadcasted_iota(jnp.int32, (8, LANES), 1)
 
-    def clear(layer, _):
-        for c in range(chunks):
-            for ref in (press, perms, stores):
-                for t in (0, pitch // 8 - 1):
-                    ref[c, layer, pl.ds(t * 8, 8), :] = zero
-        return 0
-
-    lax.fori_loop(0, layers, clear, 0)
-
-    def look(layer, kinds_of):
-        for c in range(chunks):
-            for t in range(ny // 8):
-                kind = kinds_of(c, t)
-                perms[c, layer, pl.ds(PAD + t * 8, 8), :] = look_up(perm_table, kind)
-                stores[c, layer, pl.ds(PAD + t * 8, 8), :] = look_up(store_table, kind)
-
-    def look_ends(j, _):
-        for c in range(chunks):
-            a, b = (ref[j, :, pl.ds(c * LANES, LANES)] for ref in (xa_ref, xb_ref))
-            press[c, j, pl.ds(PAD, ny), :] = jnp.where(even_x, b, a)
-            press[c, REACH + nx + j, pl.ds(PAD, ny), :] = jnp.where(even_x, a, b)
-
-        def side(low):
-            def kinds_of(c, t):
-                a, b = (ref[REACH + j, pl.ds(t * 8, 8), pl.ds(c * LANES, LANES)] for ref in (xa_ref, xb_ref))
-                return (jnp.where(even_x, b, a) if low else jnp.where(even_x, a, b)).astype(jnp.int32)
-
-            return kinds_of
-
-        look(j, side(True))
-        look(REACH + nx + j, side(False))
-        return 0
-
-    lax.fori_loop(0, REACH, look_ends, 0)
-    fetch(rock_ref, rock, sems.at[0], False)
-
-    def look_own(layer, _):
-        look(REACH + layer, lambda c, t: rock[c, layer, pl.ds(t * 8, 8), :] + 1)
-        return 0
-
-    lax.fori_loop(0, nx, look_own, 0)
-    fetch(p_ref, own_p, sems.at[1], False)
-
-    press2, perms2, stores2, rates2 = map(flat, (press, perms, stores, rates_ref))
-    tx2, ty2, tz2, scale2, drive2 = map(flat, (trans_x, trans_y, trans_z, scale, drive))
-
     def rows(layer, k, c):
-        return pl.ds(c * depth + layer * pitch + PAD + k, 8, stride=step)
+        return pl.ds((c * layers + layer) * pitch + PAD + k, 8, stride=step)
 
     def prepare(layer, _):
-        perm = {k: [perms2[rows(layer, k, c), :] for c in range(chunks)] for k in range(-1, step + 1)}
+        perm = {k: [perms[rows(layer, k, c), :] for c in range(chunks)] for k in range(-1, step + 1)}
         t_s = [transmit(perm[-1][c], perm[0][c]) for c in range(chunks)]
         for k in range(step):
             deep = deeper(perm[k])
@@ -334,63 +297,143 @@
             above = shallower(t_z)
             for c in range(chunks):
                 at = rows(layer, k, c)
-                t_x = transmit(perm[k][c], perms2[rows(layer + 1, k, c), :])
+                t_x = transmit(perm[k][c], perms[rows(layer + 1, k, c), :])
                 t_n = transmit(perm[k][c], perm[k + 1][c])
-                t_w = tx2[rows(jnp.maximum(layer - 1, 0), k, c), :]
-                tx2[at, :], ty2[at, :], tz2[at, :] = t_x, t_n, t_z[c]
-                store = stores2[at, :]
+                t_w = trans_x[rows(jnp.maximum(layer - 1, 0), k, c), :]
+                trans_x[at, :], trans_y[at, :], trans_z[at, :] = t_x, t_n, t_z[c]
+                store = stores[at, :]
                 factor = OMEGA / (store + ((t_x + t_w) + (t_n + t_s[c]) + (t_z[c] + above[c])))
-                scale2[at, :] = factor
-                drive2[at, :] = factor * (store * press2[at, :] + rates2[at, :])
+                scale[at, :] = factor
+                drive[at, :] = factor * (store * press[at, :] + rates[at, :])
                 t_s[c] = t_n
         return 0
 
-    lax.fori_loop(0, layers - 1, prepare, 0)
+    lax.fori_loop(first, last, prepare, 0)
+
+
+def ready_own_kernel(block, p_ref, rock_ref, sat_ref, rates_ref, perm_ref, poro_ref, *refs):
+    fields, (frac, slope, p, rock, sat, sems) = refs[:8], refs[8:]
+    press, perms, stores = fields[:3]
+    (nx, ny, _), (chunks, layers, pitch) = block, wide_sizes(block)
+    step = ny // 8
+    fetch(rock_ref, rock, sems.at[0], True)
+    fetch(p_ref, p, sems.at[1], True)
+    fetch(sat_ref, sat, sems.at[2], True)
+    perm_table, store_table = rock_tables(perm_ref, poro_ref)
+    p2, rock2, sat2, slope2 = map(flat, (p, rock, sat, slope))
+    fetch(rock_ref, rock, sems.at[0], False)
+    fetch(p_ref, p, sems.at[1], False)
+
+    def look(layer, _):
+        for c in range(chunks):
+            for k in range(step):
+                own = pl.ds((c * nx + layer) * ny + k, 8, stride=step)
+                at = pl.ds((c * layers + REACH + layer) * pitch + PAD + k, 8, stride=step)
+                kind = rock2[own, :] + 1
+                perms[at, :], stores[at, :] = look_up(perm_table, kind), look_up(store_table, kind)
+                press[at, :] = p2[own, :]
+        return 0
+
+    lax.fori_loop(0, nx, look, 0)
+    prepare_layers(block, fields, rates_ref, REACH, REACH + nx)
     fetch(sat_ref, sat, sems.at[2], False)
 
     def old_fraction(layer, _):
         for c in range(chunks):
-            s = sat[c, layer]
-            inverse = 1.0 / (s * s + MOBILITY * (1.0 - s) ** 2)
-            frac[c, layer, pl.ds(PAD, ny), :] = s * s * inverse
-            slope[c, layer] = 2.0 * MOBILITY * s * (1.0 - s) * (inverse * inverse)
+            for k in range(step):
+                own = pl.ds((c * nx + layer) * ny + k, 8, stride=step)
+                s = sat2[own, :]
+                inverse = 1.0 / (s * s + MOBILITY * (1.0 - s) ** 2)
+                frac[pl.ds((c * nx + layer) * pitch + PAD + k, 8, stride=step), :] = s * s * inverse
+                slope2[own, :] = 2.0 * MOBILITY * s * (1.0 - s) * (inverse * inverse)
         return 0
 
     lax.fori_loop(0, nx, old_fraction, 0)
 
 
-def ready(pressure, rock_type, saturation, ends, rates, rock_perm, rock_poro):
-    nx, ny, nz = pressure.shape
-    chunks = nz // LANES
-    assert ny % 8 == 0 and nz % LANES == 0
-    wide = jax.ShapeDtypeStruct(wide_shape(pressure.shape), jnp.float32)
-    block = (chunks, nx, ny, LANES)
+def ready_own(pressure, rock_type, saturation, rates, rock_perm, rock_poro):
+    block = pressure.shape
+    (nx, ny, _), (chunks, _, pitch) = block, wide_sizes(block)
+    own = (chunks, nx, ny, LANES)
     return pl.pallas_call(
-        ready_kernel,
-        name="ready",
-        out_shape=(wide,) * 8 + (jax.ShapeDtypeStruct((chunks, nx, ny + 2 * PAD, LANES), jnp.float32), jax.ShapeDtypeStruct(block, jnp.float32)),
-        in_specs=[HBM] * 3 + [VMEM] * 3 + [SMEM] * 2,
+        functools.partial(ready_own_kernel, block),
+        name="ready_own",
+        out_shape=(wide_shape(block),) * 8
+        + (jax.ShapeDtypeStruct((chunks * nx * pitch, LANES), jnp.float32), jax.ShapeDtypeStruct(own, jnp.float32)),
+        in_specs=[HBM] * 3 + [VMEM] + [SMEM] * 2,
         out_specs=(VMEM,) * 10,
-        scratch_shapes=[pltpu.VMEM(block, jnp.int32), pltpu.VMEM(block, jnp.float32), pltpu.SemaphoreType.DMA((3, chunks))],
-        cost_estimate=pl.CostEstimate(flops=0, bytes_accessed=24 << 20, transcendentals=0),
+        scratch_shapes=[
+            pltpu.VMEM(own, jnp.float32),
+            pltpu.VMEM(own, jnp.int32),
+            pltpu.VMEM(own, jnp.float32),
+            pltpu.SemaphoreType.DMA((3, chunks)),
+        ],
+        cost_estimate=pl.CostEstimate(flops=0, bytes_accessed=18 << 20, transcendentals=0),
+        compiler_params=pltpu.CompilerParams(vmem_limit_bytes=5 << 20),
+    )(pressure, rock_type, saturation, rates, rock_perm, rock_poro)
+
+
+def ready_ends_kernel(block, xa_ref, xb_ref, rates_ref, perm_ref, poro_ref, *refs):
+    fields, (ends_a, ends_b, sems) = refs[8:16], refs[16:]
+    press, perms, stores = fields[:3]
+    (nx, ny, _), (chunks, layers, pitch) = block, wide_sizes(block)
+    step = ny // 8
+    even = lax.rem(lax.axis_index("gx"), 2) == 0
+    fetch(xa_ref, ends_a, sems.at[0], True)
+    fetch(xb_ref, ends_b, sems.at[1], True)
+    perm_table, store_table = rock_tables(perm_ref, poro_ref)
+    fetch(xa_ref, ends_a, sems.at[0], False)
+    fetch(xb_ref, ends_b, sems.at[1], False)
+    a2, b2 = flat(ends_a), flat(ends_b)
+
+    def look(j, _):
+        for c in range(chunks):
+            for k in range(step):
+                got = pl.ds((c * 2 * REACH + j) * ny + k, 8, stride=step)
+                kinds_got = pl.ds((c * 2 * REACH + REACH + j) * ny + k, 8, stride=step)
+                for low in (True, False):
+                    at = pl.ds((c * layers + j + (0 if low else REACH + nx)) * pitch + PAD + k, 8, stride=step)
+                    one, two = (b2, a2) if low else (a2, b2)
+                    press[at, :] = jnp.where(even, one[got, :], two[got, :])
+                    kind = jnp.where(even, one[kinds_got, :], two[kinds_got, :]).astype(jnp.int32)
+                    perms[at, :], stores[at, :] = look_up(perm_table, kind), look_up(store_table, kind)
+        return 0
+
+    lax.fori_loop(0, REACH, look, 0)
+    prepare_layers(block, fields, rates_ref, 0, REACH + 1)
+    prepare_layers(block, fields, rates_ref, REACH + nx - 1, layers - 1)
+
+
+def ready_ends(block, ends, rates, rock_perm, rock_poro, fields):
+    (_, ny, _), (chunks, _, _) = block, wide_sizes(block)
+    inputs = (*ends, rates, rock_perm, rock_poro, *fields)
+    end = pltpu.VMEM((chunks, 2 * REACH, ny, LANES), jnp.float32)
+    return pl.pallas_call(
+        functools.partial(ready_ends_kernel, block),
+        name="ready_ends",
+        out_shape=tuple(jax.ShapeDtypeStruct(f.shape, f.dtype) for f in fields),
+        in_specs=[VMEM] * 3 + [SMEM] * 2 + [VMEM] * len(fields),
+        out_specs=(VMEM,) * len(fields),
+        input_output_aliases={5 + i: i for i in range(len(fields))},
+        scratch_shapes=[end, end, pltpu.SemaphoreType.DMA((2, chunks))],
+        cost_estimate=pl.CostEstimate(flops=0, bytes_accessed=9 << 20, transcendentals=0),
         compiler_params=pltpu.CompilerParams(vmem_limit_bytes=4 << 20),
-    )(pressure, rock_type, saturation, *ends, rates, rock_perm, rock_poro)
+    )(*inputs)
 
 
 def flow_kernel(
-    flux_ref, sat_ref, ya_ref, yb_ref, ca_ref, cb_ref, rates_ref, slope_ref, perm_ref, poro_ref, *refs
+    block, flux_ref, sat_ref, ya_ref, yb_ref, ca_ref, cb_ref, rates_ref, slope_ref, perm_ref, poro_ref, *refs
 ):
     press, perms, stores, trans_x, trans_y, trans_z, scale, drive, frac = refs[9:18]
-    press_ref, prep_ref, inlet_ref, other, flux, sat, sems = refs[18:]
-    chunks, layers, pitch, _ = press.shape
-    _, nx, ny, _ = flux.shape
+    press_ref, prep_ref, inlet_ref, other, flux, sat, leave, sems = refs[18:]
+    (nx, ny, _), (chunks, layers, pitch) = block, wide_sizes(block)
     depth, step = layers * pitch, ny // 8
     tiles = (ny + 2 * PASSES) // 8
     side_rows = (2 * REACH + 1) * nx
     even_x, even_y = lax.rem(lax.axis_index("gx"), 2) == 0, lax.rem(lax.axis_index("gy"), 2) == 0
-    press2, other2, perms2, stores2, rates2, frac2 = map(flat, (press, other, perms, stores, rates_ref, frac))
-    tx2, ty2, tz2, scale2, drive2 = map(flat, (trans_x, trans_y, trans_z, scale, drive))
-    flux2, sat2, slope2 = map(flat, (flux, sat, slope_ref))
+    press2, other2, perms2, stores2, rates2, frac2 = press, other, perms, stores, rates_ref, frac
+    tx2, ty2, tz2, scale2, drive2 = trans_x, trans_y, trans_z, scale, drive
+    flux2, sat2, slope2, leave2 = map(flat, (flux, sat, slope_ref, leave))
     fetch(flux_ref, flux, sems.at[0], True)
     fetch(sat_ref, sat, sems.at[1], True)
     perm_table, store_table = rock_tables(perm_ref, poro_ref)
@@ -482,15 +525,22 @@
     for number in range(1, PASSES + 1):
         source, target = (press2, other2) if number % 2 else (other2, press2)
         relax(source, target, number)
-    final, final2 = (press, press2) if PASSES % 2 == 0 else (other, other2)
+    final2 = press2 if PASSES % 2 == 0 else other2
 
     def send_out(start):
         for c in range(chunks):
-            copy = pltpu.make_async_copy(
-                final.at[c, pl.ds(REACH, nx), pl.ds(PAD, ny), :], press_ref.at[:, :, pl.ds(c * LANES, LANES)], sems.at[2, c]
-            )
+            copy = pltpu.make_async_copy(leave.at[c], press_ref.at[:, :, pl.ds(c * LANES, LANES)], sems.at[2, c])
             copy.start() if start else copy.wait()
 
+    def gather(layer, _):
+        for c in range(chunks):
+            for k in range(step):
+                at = pl.ds(c * depth + (REACH + layer) * pitch + PAD + k, 8, stride=step)
+                leave2[pl.ds((c * nx + layer) * ny + k, 8, stride=step), :] = final2[at, :]
+        return 0
+
+    step = ny // 8
+    lax.fori_loop(0, nx, gather, 0)
     send_out(True)
     fetch(flux_ref, flux, sems.at[0], False)
     fetch(sat_ref, sat, sems.at[1], False)
@@ -539,11 +589,11 @@
     nx, ny, nz = base_flux.shape
     chunks = nz // LANES
     *fields, slope = made
-    block = pltpu.VMEM((chunks, nx, ny, LANES), jnp.float32)
+    own = pltpu.VMEM((chunks, nx, ny, LANES), jnp.float32)
     inputs = (base_flux, saturation, *sides, *ends_corner, rates, slope, rock_perm, rock_poro, *fields)
     first = len(inputs) - len(fields)
     return pl.pallas_call(
-        flow_kernel,
+        functools.partial(flow_kernel, base_flux.shape),
         name="flow",
         out_shape=tuple(jax.ShapeDtypeStruct(f.shape, f.dtype) for f in fields) + (
             jax.ShapeDtypeStruct(base_flux.shape, jnp.float32),
@@ -553,7 +603,7 @@
         in_specs=[HBM] * 2 + [VMEM] * 6 + [SMEM] * 2 + [VMEM] * len(fields),
         out_specs=(VMEM,) * len(fields) + (HBM, VMEM, VMEM),
         input_output_aliases={first + i: i for i in range(len(fields))},
-        scratch_shapes=[pltpu.VMEM(wide_shape(base_flux.shape), jnp.float32), block, block, pltpu.SemaphoreType.DMA((3, chunks))],
+        scratch_shapes=[pltpu.VMEM(wide_shape(base_flux.shape).shape, jnp.float32), own, own, own, pltpu.SemaphoreType.DMA((3, chunks))],
         compiler_params=pltpu.CompilerParams(vmem_limit_bytes=8 << 20),
     )(*inputs)[-3:]
 
@@ -626,8 +676,10 @@
     sides_got = swap(*sides, "gy")
     ends = swap(*pack_ends(initial_pressure, rock_type, sides[0]), "gx")
     rates = rates_field(rock_type.shape, well_cells, well_rates)
-    made = ready(initial_pressure, rock_type, old_saturation, ends, rates, rock_perm, rock_poro)
-    ends_corner = swap(*corners(*sides_got, nx, made[-1]), "gx")
+    *fields, frac, slope = ready_own(initial_pressure, rock_type, old_saturation, rates, rock_perm, rock_poro)
+    ends_corner = swap(*corners(*sides_got, nx, slope), "gx")
+    fields = ready_ends(rock_type.shape, ends, rates, rock_perm, rock_poro, fields)
+    made = (*fields, frac, slope)
     pressure, prep, inflow = flow(base_flux, old_saturation, sides_got, ends_corner, rates, made, rock_perm, rock_poro)
     saturation = ()
     count = lax.axis_size("gx")

time: 70.3 us -> 68.8 us (0.979)
  Pallas kernels: 38.5 us -> 36.6 us
    ppermute x3, waiting for transfers between devices: 3.72 us -> 7.3 us  [swap(): got_a = lax.ppermute(value_a, axis, pairs_a)]
    ppermute x3, waiting for transfers between devices: 17.1 us -> 13.8 us  [step(): inflow = lax.ppermute(outflow, 'gx', [(stage, stage + 1)])]
    pallas_call x3 -> x4, Pallas kernels: 27.8 us -> 25.9 us  [the longest x1 12.9 us: flow(): pl.pallas_call(functools.partial(flow_kernel, base_flux.shape), name='flo...]
  transfers between devices with their start and end apart: 9 -> 9, of which waited for: 3 -> 2; matrix products, arithmetic and copies ran while one was open for 0% -> 0% of each run, Pallas kernels for 19% -> 19%
where the time goes in v3:
time: 68.8 us; the launch traced here: 68.5 us
  Pallas kernels  36.6 us (53%)
  waiting for transfers between devices  21.1 us (31%)
  starting transfers between devices  9.72 us (14%)
  between operations  0.95 us (1%)
    ppermute x3, waiting for transfers between devices, step(): inflow = lax.ppermute(outflow, 'gx', [(stage, stage + 1)])  13.8 us
    pallas_call x1, Pallas kernels, flow(): pl.pallas_call(functools.partial(flow_kernel, base_flux.shape), name='flo...  12.9 us
    ppermute x3, waiting for transfers between devices, swap(): got_a = lax.ppermute(value_a, axis, pairs_a)  7.3 us
    pallas_call x1, Pallas kernels, ready_own(): pl.pallas_call(functools.partial(ready_own_kernel, block), name='ready_ow...  6.81 us
    pallas_call x4, Pallas kernels, run_stage(): pl.pallas_call(functools.partial(stage_kernel, stage), name='stage', out_...  5.51 us
    ppermute x3, starting transfers between devices, swap(): got_b = lax.ppermute(value_b, axis, pairs_b)  4.38 us
    pallas_call x1, Pallas kernels, ready_ends(): pl.pallas_call(functools.partial(ready_ends_kernel, block), name='ready_e...  4.02 us
    ppermute x3, starting transfers between devices, swap(): got_a = lax.ppermute(value_a, axis, pairs_a)  2.72 us
  transfers between devices with their start and end apart: 9, of which 2 were waited for; matrix products, arithmetic and copies ran while one was open for 0% of the time, Pallas kernels for 19%

profile of v3, /device:TPU:11, one launch (start us, length us, event | category | flops | bytes accessed | tf_op | source)
XLA Modules:
  0.0 68.5 jit_solution(6037942145128950383)
XLA Ops:
  0.6 0.0 copy-start.7
  0.6 0.0 copy-start.6
  0.6 2.5 %pack_sides.1 = (f32[704,128]{1,0:T(8,128)}, f32[704,128]{1,0:T(8,128)}) custom-call(f32[16,32,512]{2,1,0:T(8,128)} %p_ref.5, s32[16,32,512]{2,1,0:T(8,128)} %rock_ref.5, f32[16,32,512]{2,1,0:T(8,128)} %sat_ref.5), custom_call_target="tpu_custom_call" | custom-call | tf_op jit(solution)/shard_map/pack_sides/pallas_call | solution.py:92
  3.2 0.0 copy-start.9
  3.2 0.0 copy-start.8
  3.2 0.0 copy-start
  3.2 0.0 copy-start.1
  3.2 0.0 copy-start.2
  3.2 0.0 copy-start.4
  3.2 0.0 copy-start.5
  3.2 2.5 %pack_ends.1 = (f32[10,32,512]{2,1,0:T(8,128)}, f32[10,32,512]{2,1,0:T(8,128)}) custom-call(f32[16,32,512]{2,1,0:T(8,128)} %p_ref.5, s32[16,32,512]{2,1,0:T(8,128)} %rock_ref.5, f32[704,128]{1,0:T(8,128)} %get-tuple-element.36._), custom_call_target="tpu_custom_call" | custom-call | tf_op jit(solution)/shard_map/pack_ends/pallas_call | solution.py:131
  5.8 0.7 %collective-permute-start.4 = (f32[10,32,512]{2,1,0:T(8,128)}, f32[10,32,512]{2,1,0:T(8,128)S(1)}, u32[]{:S(2)}, u32[]{:S(2)}) collective-permute-start(f32[10,32,512]{2,1,0:T(8,128)} %get-tuple-element.41), channel_id=1, source_target_pairs={{0,8},{16,24},{8,0},{24,16},{1,9},{17,25},{9,1},{25,17},{2,10},{18... | collective-permute-start | bytes 1966088 | tf_op jit(solution)/shard_map/ppermute | solution.py:42
  6.5 0.7 %collective-permute-start.5 = (f32[10,32,512]{2,1,0:T(8,128)}, f32[10,32,512]{2,1,0:T(8,128)S(1)}, u32[]{:S(2)}, u32[]{:S(2)}) collective-permute-start(f32[10,32,512]{2,1,0:T(8,128)} %get-tuple-element.42), channel_id=1, source_target_pairs={{8,16},{16,8},{9,17},{17,9},{10,18},{18,10},{11,19},{19,11},{12,20... | collective-permute-start | bytes 1966088 | tf_op jit(solution)/shard_map/ppermute | solution.py:43
  7.2 0.0 copy-done.9
  7.2 3.0 %collective-permute-start.1 = (f32[704,128]{1,0:T(8,128)S(1)}, f32[704,128]{1,0:T(8,128)S(1)}, u32[]{:S(2)}, u32[]{:S(2)}) collective-permute-start(f32[704,128]{1,0:T(8,128)S(1)} %copy-done.9), channel_id=1, source_target_pairs={{1,2},{3,4},{5,6},{2,1},{4,3},{6,5},{9,10},{11,12},{13,14},{10,9},... | collective-permute-start | bytes 1081352 | tf_op jit(solution)/shard_map/ppermute | solution.py:43
  10.3 0.0 copy-done.8
  10.3 1.4 %collective-permute-start = (f32[704,128]{1,0:T(8,128)S(1)}, f32[704,128]{1,0:T(8,128)S(1)}, u32[]{:S(2)}, u32[]{:S(2)}) collective-permute-start(f32[704,128]{1,0:T(8,128)S(1)} %copy-done.8), channel_id=1, source_target_pairs={{0,1},{2,3},{4,5},{6,7},{1,0},{3,2},{5,4},{7,6},{8,9},{10,11},{12,... | collective-permute-start | bytes 1081352 | tf_op jit(solution)/shard_map/ppermute | solution.py:42
  11.7 0.0 copy-done.7
  11.7 0.0 copy-done.6
  11.7 2.2 %rates.1.rates_ref = f32[4576,128]{1,0:T(8,128)S(1)} custom-call(s32[3,128]{1,0:T(4,128)S(1)} %copy-done.6, f32[128]{0:T(128)S(1)} %copy-done.7), custom_call_target="tpu_custom_call" | custom-call | bytes 6291456 | tf_op jit(solution)/shard_map/rates/pallas_call | solution.py:270
  13.9 0.0 copy-done
  13.9 0.0 copy-done.1
  13.9 0.0 copy-done.2
  14.0 0.0 copy-done.4
  14.0 0.0 copy-done.5
  14.0 6.8 %ready_own.1 = (f32[4576,128]{1,0:T(8,128)S(1)}, f32[4576,128]{1,0:T(8,128)S(1)}, f32[4576,128]{1,0:T(8,128)S(1)}, f32[4576,128]{1,0:T(8,128)S(1)}, f32[4576,128...) custom-call(f32[16,32,512]{2,1,0:T(8,128)S(1)} %copy-done, ...), custom_call_target="tpu_custom_call" | custom-call | bytes 18874368 | tf_op jit(solution)/shard_map/ready_own/pallas_call | solution.py:358
  20.8 0.0 collective-permute-done.1.yb_ref
  20.8 7.3 %collective-permute-done.ya_ref = f32[704,128]{1,0:T(8,128)S(1)} collective-permute-done((f32[704,128]{1,0:T(8,128)S(1)}, f32[704,128]{1,0:T(8,128)S(1)}, u32[]{:S(2)}, u32[]{:S(2)}) %collective-permute-start) | collective-permute-done | bytes 360480 | tf_op jit(solution)/shard_map/ppermute | solution.py:42
  28.1 0.2 corners.1
  28.3 0.6 collective-permute-start.2
  28.8 0.7 collective-permute-start.3
  29.5 0.0 collective-permute-done.4.xa_ref
  29.5 0.0 collective-permute-done.5.xb_ref
  29.5 0.0 copy-start.3
  29.5 4.0 %ready_ends.1 = (f32[4576,128]{1,0:T(8,128)S(1)}, f32[4576,128]{1,0:T(8,128)S(1)}, f32[4576,128]{1,0:T(8,128)S(1)}, f32[4576,128]{1,0:T(8,128)S(1)}, f32[4576,12...) custom-call(f32[10,32,512]{2,1,0:T(8,128)S(1)} %collective-permute-d, ...), custom_call_target="tpu_custom_call", output_to_operand_aliasing={{0}: (5, {}), {1}: (6, {}), {2}: (7, {}), {3}: (8, {}), {4}... | custom-call | bytes 9437184 | tf_op jit(solution)/shard_map/ready_ends/pallas_call | solution.py:411
  33.6 0.0 collective-permute-done.2.ca_ref
  33.6 0.0 collective-permute-done.3.cb_ref
  33.6 12.9 %flow.1 = (f32[4576,128]{1,0:T(8,128)S(1)}, f32[4576,128]{1,0:T(8,128)S(1)}, f32[4576,128]{1,0:T(8,128)S(1)}, f32[4576,128]{1,0:T(8,128)S(1)}, f32[4576,128]{1,0...) custom-call(f32[16,32,512]{2,1,0:T(8,128)S(1)} %copy-done.3, ...), custom_call_target="tpu_custom_call", output_to_operand_aliasing={{0}: (10, {}), {1}: (11, {}), {2}: (12, {}), {3}: (13, {}),... | custom-call | tf_op jit(solution)/shard_map/flow/pallas_call | solution.py:595
  46.5 0.6 stage.4
  47.1 0.7 collective-permute-start.6
  47.8 0.0 collective-permute-done.6.inflow_ref
  47.8 0.6 stage.5
  48.4 0.7 collective-permute-start.7
  49.0 0.0 collective-permute-done.7.inflow_ref
  49.1 0.6 stage.6
  49.7 1.3 %collective-permute-start.8 = (f32[128,128]{1,0:T(8,128)S(1)}, f32[128,128]{1,0:T(8,128)S(1)}, u32[]{:S(2)}, u32[]{:S(2)}) collective-permute-start(f32[128,128]{1,0:T(8,128)S(1)} %get-tuple-element.67), channel_id=1, source_target_pairs={{16,24},{17,25},{18,26},{19,27},{20,28},{21,29},{22,30},{23,31}} | collective-permute-start | bytes 196616 | tf_op jit(solution)/shard_map/ppermute | solution.py:689
  51.0 13.8 %collective-permute-done.8.inflow_ref = f32[128,128]{1,0:T(8,128)S(1)} collective-permute-done((f32[128,128]{1,0:T(8,128)S(1)}, f32[128,128]{1,0:T(8,128)S(1)}, u32[]{:S(2)}, u32[]{:S(2)}) %collective-permute-start.8) | collective-permute-done | bytes 65568 | tf_op jit(solution)/shard_map/ppermute | solution.py:689
  64.7 3.7 %stage.7 = (f32[16,32,512]{2,1,0:T(8,128)}, f32[128,128]{1,0:T(8,128)}) custom-call(f32[128,128]{1,0:T(8,128)S(1)} %collective-permute-done.8.inflow_ref, f32[16,640,128]{2,1,0:T(8,128)S(1)} %get-tuple-element.62.prep_ref, f32[16,32,512]{2,1,0:T(8,128)} %get-tuple-element.68.refs_0_), custom_call_target="tpu_custom_call", output_to_operand_aliasing={{0}: (2, {})} | custom-call | tf_op jit(solution)/shard_map/stage/pallas_call | solution.py:658
  (1 shorter events, 0.0 us)
Async XLA Ops:
  0.6 11.1 %copy-start.7 = (f32[128]{0:T(128)S(1)}, f32[128]{0:T(128)}, u32[]{:S(2)}) copy-start(f32[128]{0:T(128)} %rates_ref.1) | copy-start | bytes 1540
  0.6 11.1 %copy-start.6 = (s32[3,128]{1,0:T(4,128)S(1)}, s32[3,128]{1,0:T(4,128)}, u32[]{:S(2)}) copy-start(s32[3,128]{1,0:T(4,128)} %cells_ref.1) | copy-start | bytes 4612
  3.2 4.1 %copy-start.9 = (f32[704,128]{1,0:T(8,128)S(1)}, f32[704,128]{1,0:T(8,128)}, u32[]{:S(2)}) copy-start(f32[704,128]{1,0:T(8,128)} %get-tuple-element.37) | copy-start | bytes 1081348
  3.2 7.1 %copy-start.8 = (f32[704,128]{1,0:T(8,128)S(1)}, f32[704,128]{1,0:T(8,128)}, u32[]{:S(2)}) copy-start(f32[704,128]{1,0:T(8,128)} %get-tuple-element.36._) | copy-start | bytes 1081348
  3.2 10.7 %copy-start = (f32[16,32,512]{2,1,0:T(8,128)S(1)}, f32[16,32,512]{2,1,0:T(8,128)}, u32[]{:S(2)}) copy-start(f32[16,32,512]{2,1,0:T(8,128)} %p_ref.5) | copy-start | bytes 3145732
  3.2 10.7 %copy-start.1 = (s32[16,32,512]{2,1,0:T(8,128)S(1)}, s32[16,32,512]{2,1,0:T(8,128)}, u32[]{:S(2)}) copy-start(s32[16,32,512]{2,1,0:T(8,128)} %rock_ref.5) | copy-start | bytes 3145732
  3.2 10.7 %copy-start.2 = (f32[16,32,512]{2,1,0:T(8,128)S(1)}, f32[16,32,512]{2,1,0:T(8,128)}, u32[]{:S(2)}) copy-start(f32[16,32,512]{2,1,0:T(8,128)} %sat_ref.5) | copy-start | bytes 3145732
  3.2 10.7 %copy-start.4 = (f32[8]{0:T(128)S(1)}, f32[8]{0:T(128)}, u32[]{:S(2)}) copy-start(f32[8]{0:T(128)} %perm_ref.5) | copy-start | bytes 100
  3.2 10.7 %copy-start.5 = (f32[8]{0:T(128)S(1)}, f32[8]{0:T(128)}, u32[]{:S(2)}) copy-start(f32[8]{0:T(128)} %poro_ref.5) | copy-start | bytes 100
  5.8 23.7 %collective-permute-start.4 = (f32[10,32,512]{2,1,0:T(8,128)}, f32[10,32,512]{2,1,0:T(8,128)S(1)}, u32[]{:S(2)}, u32[]{:S(2)}) collective-permute-start(f32[10,32,512]{2,1,0:T(8,128)} %get-tuple-element.41), channel_id=1, source_target_pairs={{0,8},{16,24},{8,0},{24,16},{1,9},{17,25},{9,1},{25,17},{2,10},{18... | collective-permute-start | bytes 1966088 | tf_op jit(solution)/shard_map/ppermute | solution.py:42
  6.5 23.0 %collective-permute-start.5 = (f32[10,32,512]{2,1,0:T(8,128)}, f32[10,32,512]{2,1,0:T(8,128)S(1)}, u32[]{:S(2)}, u32[]{:S(2)}) collective-permute-start(f32[10,32,512]{2,1,0:T(8,128)} %get-tuple-element.42), channel_id=1, source_target_pairs={{8,16},{16,8},{9,17},{17,9},{10,18},{18,10},{11,19},{19,11},{12,20... | collective-permute-start | bytes 1966088 | tf_op jit(solution)/shard_map/ppermute | solution.py:43
  7.2 13.5 %collective-permute-start.1 = (f32[704,128]{1,0:T(8,128)S(1)}, f32[704,128]{1,0:T(8,128)S(1)}, u32[]{:S(2)}, u32[]{:S(2)}) collective-permute-start(f32[704,128]{1,0:T(8,128)S(1)} %copy-done.9), channel_id=1, source_target_pairs={{1,2},{3,4},{5,6},{2,1},{4,3},{6,5},{9,10},{11,12},{13,14},{10,9},... | collective-permute-start | bytes 1081352 | tf_op jit(solution)/shard_map/ppermute | solution.py:43
  10.3 17.8 %collective-permute-start = (f32[704,128]{1,0:T(8,128)S(1)}, f32[704,128]{1,0:T(8,128)S(1)}, u32[]{:S(2)}, u32[]{:S(2)}) collective-permute-start(f32[704,128]{1,0:T(8,128)S(1)} %copy-done.8), channel_id=1, source_target_pairs={{0,1},{2,3},{4,5},{6,7},{1,0},{3,2},{5,4},{7,6},{8,9},{10,11},{12,... | collective-permute-start | bytes 1081352 | tf_op jit(solution)/shard_map/ppermute | solution.py:42
  28.3 5.3 %collective-permute-start.2 = (f32[256,128]{1,0:T(8,128)S(1)}, f32[256,128]{1,0:T(8,128)S(1)}, u32[]{:S(2)}, u32[]{:S(2)}) collective-permute-start(f32[256,128]{1,0:T(8,128)S(1)} %get-tuple-element.39), channel_id=1, source_target_pairs={{0,8},{16,24},{8,0},{24,16},{1,9},{17,25},{9,1},{25,17},{2,10},{18... | collective-permute-start | bytes 393224 | tf_op jit(solution)/shard_map/ppermute | solution.py:42
  28.8 4.7 %collective-permute-start.3 = (f32[256,128]{1,0:T(8,128)S(1)}, f32[256,128]{1,0:T(8,128)S(1)}, u32[]{:S(2)}, u32[]{:S(2)}) collective-permute-start(f32[256,128]{1,0:T(8,128)S(1)} %get-tuple-element.40), channel_id=1, source_target_pairs={{8,16},{16,8},{9,17},{17,9},{10,18},{18,10},{11,19},{19,11},{12,20... | collective-permute-start | bytes 393224 | tf_op jit(solution)/shard_map/ppermute | solution.py:43
  29.5 4.1 %copy-start.3 = (f32[16,32,512]{2,1,0:T(8,128)S(1)}, f32[16,32,512]{2,1,0:T(8,128)}, u32[]{:S(2)}) copy-start(f32[16,32,512]{2,1,0:T(8,128)} %flux_ref.1) | copy-start | bytes 3145732
  47.1 0.7 collective-permute-start.6
  48.4 0.7 collective-permute-start.7
  49.7 15.1 %collective-permute-start.8 = (f32[128,128]{1,0:T(8,128)S(1)}, f32[128,128]{1,0:T(8,128)S(1)}, u32[]{:S(2)}, u32[]{:S(2)}) collective-permute-start(f32[128,128]{1,0:T(8,128)S(1)} %get-tuple-element.67), channel_id=1, source_target_pairs={{16,24},{17,25},{18,26},{19,27},{20,28},{21,29},{22,30},{23,31}} | collective-permute-start | bytes 196616 | tf_op jit(solution)/shard_map/ppermute | solution.py:689

commit v4 on v3

--- a/solution.py
+++ b/solution.py
@@ -18,9 +18,12 @@
 COMPRESS = 0.5
 
 LANES = 128
-UNROLL = 2
+STAGE_UNROLL = 2
+UNROLL = 4
 ENDS_LIMIT = 59 << 20
 SIDES_LIMIT = 62 << 20
+OWN_LIMIT = 5 << 20
+FLOW_LIMIT = 8 << 20
 REACH = PASSES + 1
 PAD = REACH + 1
 HBM = pl.BlockSpec(memory_space=pltpu.MemorySpace.HBM)
@@ -107,34 +110,40 @@
 
 def pack_ends_kernel(p_ref, rock_ref, _, xa_ref, xb_ref, rock, sems):
     nx = p_ref.shape[0]
+    chunks = xa_ref.shape[0]
     even = lax.rem(lax.axis_index("gx"), 2) == 0
+    outs = (xa_ref, xb_ref)
     copies = []
-    for i, (out, high) in enumerate(((xa_ref, even), (xb_ref, jnp.logical_not(even)))):
+    for i, high in enumerate((even, jnp.logical_not(even))):
         layers = pl.ds(jnp.where(high, nx - REACH, 0), REACH)
-        copies.append((
-            pltpu.make_async_copy(p_ref.at[layers], out.at[pl.ds(0, REACH)], sems.at[i, 0]),
-            pltpu.make_async_copy(rock_ref.at[layers], rock.at[i], sems.at[i, 1]),
-        ))
+        for c in range(chunks):
+            lanes = pl.ds(c * LANES, LANES)
+            copies.append((
+                pltpu.make_async_copy(rock_ref.at[layers, :, lanes], rock.at[i, c], sems.at[i, c, 0]),
+                pltpu.make_async_copy(p_ref.at[layers, :, lanes], outs[i].at[c, pl.ds(0, REACH)], sems.at[i, c, 1]),
+            ))
     for pair in copies:
         for copy in pair:
             copy.start()
-    for i, out in enumerate((xa_ref, xb_ref)):
-        copies[i][1].wait()
-        for j in range(REACH):
-            out[REACH + j] = rock[i, j].astype(jnp.float32) + 1.0
-        copies[i][0].wait()
+    for i in range(2):
+        for c in range(chunks):
+            copies[i * chunks + c][0].wait()
+            outs[i][c, pl.ds(REACH, REACH)] = rock[i, c].astype(jnp.float32) + 1.0
+    for pair in copies:
+        pair[1].wait()
 
 
 def pack_ends(pressure, rock_type, after):
     _, ny, nz = pressure.shape
-    end = jax.ShapeDtypeStruct((2 * REACH, ny, nz), jnp.float32)
+    chunks = nz // LANES
+    end = jax.ShapeDtypeStruct((chunks, 2 * REACH, ny, LANES), jnp.float32)
     return pl.pallas_call(
         pack_ends_kernel,
         name="pack_ends",
         out_shape=(end, end),
         in_specs=[HBM] * 2 + [pl.BlockSpec(memory_space=pl.ANY)],
         out_specs=(VMEM,) * 2,
-        scratch_shapes=[pltpu.VMEM((2, REACH, ny, nz), jnp.int32), pltpu.SemaphoreType.DMA((2, 2))],
+        scratch_shapes=[pltpu.VMEM((2, chunks, REACH, ny, LANES), jnp.int32), pltpu.SemaphoreType.DMA((2, chunks, 2))],
         compiler_params=pltpu.CompilerParams(vmem_limit_bytes=ENDS_LIMIT),
     )(pressure, rock_type, after)
 
@@ -206,14 +215,21 @@
 
 def rock_tables(perm_ref, poro_ref):
     lane = lax.broadcasted_iota(jnp.int32, (8, LANES), 1)
-    perm, poro = jnp.zeros((8, LANES), jnp.float32), jnp.zeros((8, LANES), jnp.float32)
+    table = jnp.zeros((8, LANES), jnp.float32)
     for kind in range(perm_ref.shape[0]):
-        perm = jnp.where(lane == kind + 1, perm_ref[kind], perm)
-        poro = jnp.where(lane == kind + 1, poro_ref[kind], poro)
-    return perm, jnp.where(lane == 0, 1.0, COMPRESS * (VOLUME * poro))
-
-
-def rates_kernel(block, cells_ref, rates_ref, out_ref):
+        table = jnp.where(lane == kind + 1, perm_ref[kind], table)
+    return table, [COMPRESS * (VOLUME * poro_ref[kind]) for kind in range(perm_ref.shape[0])]
+
+
+def rock_of(kind, tables):
+    table, stores = tables
+    store = jnp.ones(kind.shape, jnp.float32)
+    for i, value in enumerate(stores):
+        store = jnp.where(kind == i + 1, value, store)
+    return look_up(table, kind), store
+
+
+def fill_rates(block, cells_ref, rates_ref, out_ref):
     (nx, ny, _), (_, layers, pitch) = block, wide_sizes(block)
     rank_x, rank_y = lax.axis_index("gx"), lax.axis_index("gy")
     sub = lax.broadcasted_iota(jnp.int32, (8, LANES), 0)
@@ -264,18 +280,6 @@
     rows = math.prod(wide_sizes(block))
     assert block[0] % 8 == 0 and block[1] % 8 == 0 and block[2] % LANES == 0
     return jax.ShapeDtypeStruct((rows, LANES), jnp.float32)
-
-
-def rates_field(block, well_cells, well_rates):
-    return pl.pallas_call(
-        functools.partial(rates_kernel, block),
-        name="rates",
-        out_shape=wide_shape(block),
-        in_specs=[SMEM] * 2,
-        out_specs=VMEM,
-        cost_estimate=pl.CostEstimate(flops=0, bytes_accessed=6 << 20, transcendentals=0),
-        compiler_params=pltpu.CompilerParams(vmem_limit_bytes=4 << 20),
-    )(well_cells, well_rates)
 
 
 def prepare_layers(block, fields, rates, first, last):
@@ -308,21 +312,22 @@
                 t_s[c] = t_n
         return 0
 
-    lax.fori_loop(first, last, prepare, 0)
-
-
-def ready_own_kernel(block, p_ref, rock_ref, sat_ref, rates_ref, perm_ref, poro_ref, *refs):
-    fields, (frac, slope, p, rock, sat, sems) = refs[:8], refs[8:]
+    lax.fori_loop(first, last, prepare, 0, unroll=2)
+
+
+def ready_own_kernel(block, rock_ref, p_ref, sat_ref, cells_ref, well_ref, perm_ref, poro_ref, *refs):
+    fields, (frac, slope, sat, rates_ref, rock, p, sems) = refs[:8], refs[8:]
+    sources = ((rock_ref, rock), (p_ref, p), (sat_ref, sat))
+    for i, (source, target) in enumerate(sources):
+        fetch(source, target, sems.at[i], True)
+    fill_rates(block, cells_ref, well_ref, rates_ref)
     press, perms, stores = fields[:3]
     (nx, ny, _), (chunks, layers, pitch) = block, wide_sizes(block)
     step = ny // 8
-    fetch(rock_ref, rock, sems.at[0], True)
-    fetch(p_ref, p, sems.at[1], True)
-    fetch(sat_ref, sat, sems.at[2], True)
-    perm_table, store_table = rock_tables(perm_ref, poro_ref)
+    tables = rock_tables(perm_ref, poro_ref)
     p2, rock2, sat2, slope2 = map(flat, (p, rock, sat, slope))
-    fetch(rock_ref, rock, sems.at[0], False)
-    fetch(p_ref, p, sems.at[1], False)
+    for i, (source, target) in enumerate(sources):
+        fetch(source, target, sems.at[i], False)
 
     def look(layer, _):
         for c in range(chunks):
@@ -330,13 +335,12 @@
                 own = pl.ds((c * nx + layer) * ny + k, 8, stride=step)
                 at = pl.ds((c * layers + REACH + layer) * pitch + PAD + k, 8, stride=step)
                 kind = rock2[own, :] + 1
-                perms[at, :], stores[at, :] = look_up(perm_table, kind), look_up(store_table, kind)
+                perms[at, :], stores[at, :] = rock_of(kind, tables)
                 press[at, :] = p2[own, :]
         return 0
 
-    lax.fori_loop(0, nx, look, 0)
+    lax.fori_loop(0, nx, look, 0, unroll=4)
     prepare_layers(block, fields, rates_ref, REACH, REACH + nx)
-    fetch(sat_ref, sat, sems.at[2], False)
 
     def old_fraction(layer, _):
         for c in range(chunks):
@@ -348,10 +352,10 @@
                 slope2[own, :] = 2.0 * MOBILITY * s * (1.0 - s) * (inverse * inverse)
         return 0
 
-    lax.fori_loop(0, nx, old_fraction, 0)
-
-
-def ready_own(pressure, rock_type, saturation, rates, rock_perm, rock_poro):
+    lax.fori_loop(0, nx, old_fraction, 0, unroll=4)
+
+
+def ready_own(pressure, rock_type, saturation, well_cells, well_rates, rock_perm, rock_poro):
     block = pressure.shape
     (nx, ny, _), (chunks, _, pitch) = block, wide_sizes(block)
     own = (chunks, nx, ny, LANES)
@@ -359,32 +363,28 @@
         functools.partial(ready_own_kernel, block),
         name="ready_own",
         out_shape=(wide_shape(block),) * 8
-        + (jax.ShapeDtypeStruct((chunks * nx * pitch, LANES), jnp.float32), jax.ShapeDtypeStruct(own, jnp.float32)),
-        in_specs=[HBM] * 3 + [VMEM] + [SMEM] * 2,
-        out_specs=(VMEM,) * 10,
+        + tuple(jax.ShapeDtypeStruct(shape, jnp.float32) for shape in ((chunks * nx * pitch, LANES), own, own))
+        + (wide_shape(block),),
+        in_specs=[HBM] * 3 + [SMEM] * 4,
+        out_specs=(VMEM,) * 12,
         scratch_shapes=[
-            pltpu.VMEM(own, jnp.float32),
             pltpu.VMEM(own, jnp.int32),
             pltpu.VMEM(own, jnp.float32),
             pltpu.SemaphoreType.DMA((3, chunks)),
         ],
-        cost_estimate=pl.CostEstimate(flops=0, bytes_accessed=18 << 20, transcendentals=0),
-        compiler_params=pltpu.CompilerParams(vmem_limit_bytes=5 << 20),
-    )(pressure, rock_type, saturation, rates, rock_perm, rock_poro)
+        cost_estimate=pl.CostEstimate(flops=0, bytes_accessed=24 << 20, transcendentals=0),
+        compiler_params=pltpu.CompilerParams(vmem_limit_bytes=OWN_LIMIT),
+    )(rock_type, pressure, saturation, well_cells, well_rates, rock_perm, rock_poro)
 
 
 def ready_ends_kernel(block, xa_ref, xb_ref, rates_ref, perm_ref, poro_ref, *refs):
-    fields, (ends_a, ends_b, sems) = refs[8:16], refs[16:]
+    fields = refs[8:16]
     press, perms, stores = fields[:3]
     (nx, ny, _), (chunks, layers, pitch) = block, wide_sizes(block)
     step = ny // 8
     even = lax.rem(lax.axis_index("gx"), 2) == 0
-    fetch(xa_ref, ends_a, sems.at[0], True)
-    fetch(xb_ref, ends_b, sems.at[1], True)
-    perm_table, store_table = rock_tables(perm_ref, poro_ref)
-    fetch(xa_ref, ends_a, sems.at[0], False)
-    fetch(xb_ref, ends_b, sems.at[1], False)
-    a2, b2 = flat(ends_a), flat(ends_b)
+    tables = rock_tables(perm_ref, poro_ref)
+    a2, b2 = flat(xa_ref), flat(xb_ref)
 
     def look(j, _):
         for c in range(chunks):
@@ -396,18 +396,16 @@
                     one, two = (b2, a2) if low else (a2, b2)
                     press[at, :] = jnp.where(even, one[got, :], two[got, :])
                     kind = jnp.where(even, one[kinds_got, :], two[kinds_got, :]).astype(jnp.int32)
-                    perms[at, :], stores[at, :] = look_up(perm_table, kind), look_up(store_table, kind)
-        return 0
-
-    lax.fori_loop(0, REACH, look, 0)
+                    perms[at, :], stores[at, :] = rock_of(kind, tables)
+        return 0
+
+    lax.fori_loop(0, REACH, look, 0, unroll=True)
     prepare_layers(block, fields, rates_ref, 0, REACH + 1)
     prepare_layers(block, fields, rates_ref, REACH + nx - 1, layers - 1)
 
 
 def ready_ends(block, ends, rates, rock_perm, rock_poro, fields):
-    (_, ny, _), (chunks, _, _) = block, wide_sizes(block)
     inputs = (*ends, rates, rock_perm, rock_poro, *fields)
-    end = pltpu.VMEM((chunks, 2 * REACH, ny, LANES), jnp.float32)
     return pl.pallas_call(
         functools.partial(ready_ends_kernel, block),
         name="ready_ends",
@@ -415,17 +413,16 @@
         in_specs=[VMEM] * 3 + [SMEM] * 2 + [VMEM] * len(fields),
         out_specs=(VMEM,) * len(fields),
         input_output_aliases={5 + i: i for i in range(len(fields))},
-        scratch_shapes=[end, end, pltpu.SemaphoreType.DMA((2, chunks))],
         cost_estimate=pl.CostEstimate(flops=0, bytes_accessed=9 << 20, transcendentals=0),
         compiler_params=pltpu.CompilerParams(vmem_limit_bytes=4 << 20),
     )(*inputs)
 
 
 def flow_kernel(
-    block, flux_ref, sat_ref, ya_ref, yb_ref, ca_ref, cb_ref, rates_ref, slope_ref, perm_ref, poro_ref, *refs
+    block, flux_ref, sat, ya_ref, yb_ref, ca_ref, cb_ref, rates_ref, slope_ref, perm_ref, poro_ref, *refs
 ):
     press, perms, stores, trans_x, trans_y, trans_z, scale, drive, frac = refs[9:18]
-    press_ref, prep_ref, inlet_ref, other, flux, sat, leave, sems = refs[18:]
+    press_ref, prep_ref, inlet_ref, other, leave, flux, sems = refs[18:]
     (nx, ny, _), (chunks, layers, pitch) = block, wide_sizes(block)
     depth, step = layers * pitch, ny // 8
     tiles = (ny + 2 * PASSES) // 8
@@ -435,8 +432,7 @@
     tx2, ty2, tz2, scale2, drive2 = trans_x, trans_y, trans_z, scale, drive
     flux2, sat2, slope2, leave2 = map(flat, (flux, sat, slope_ref, leave))
     fetch(flux_ref, flux, sems.at[0], True)
-    fetch(sat_ref, sat, sems.at[1], True)
-    perm_table, store_table = rock_tables(perm_ref, poro_ref)
+    tables = rock_tables(perm_ref, poro_ref)
     lane = lax.broadcasted_iota(jnp.int32, (8, LANES), 1)
 
     for c in range(chunks):
@@ -450,7 +446,7 @@
                 press2[low, :], press2[high, :] = jnp.where(even_y, b, a), jnp.where(even_y, a, b)
                 a, b = (ref[pl.ds(start + REACH * nx, 8), :].astype(jnp.int32) for ref in (ya_ref, yb_ref))
                 for where, kind in ((low, jnp.where(even_y, b, a)), (high, jnp.where(even_y, a, b))):
-                    perms2[where, :], stores2[where, :] = look_up(perm_table, kind), look_up(store_table, kind)
+                    perms2[where, :], stores2[where, :] = rock_of(kind, tables)
         start = c * side_rows + 2 * REACH * nx
         a, b = fraction(ya_ref[pl.ds(start, nx), :]), fraction(yb_ref[pl.ds(start, nx), :])
         at = c * nx * pitch
@@ -465,7 +461,7 @@
             a, b = (ref[pl.ds(start, both), :].astype(jnp.int32) for ref in (ca_ref, cb_ref))
             kinds = (jnp.where(even_x, b, a), jnp.where(even_x, a, b))
             for (layer, value), kind in zip(ends, kinds):
-                for ref, new in ((press2, value), (perms2, look_up(perm_table, kind)), (stores2, look_up(store_table, kind))):
+                for ref, new in zip((press2, perms2, stores2), (value, *rock_of(kind, tables))):
                     at = c * depth + layer * pitch + PAD
                     ref[pl.ds(at - PASSES, PASSES), :] = new[:PASSES]
                     ref[pl.ds(at + ny, PASSES), :] = new[PASSES:]
@@ -543,7 +539,6 @@
     lax.fori_loop(0, nx, gather, 0)
     send_out(True)
     fetch(flux_ref, flux, sems.at[0], False)
-    fetch(sat_ref, sat, sems.at[1], False)
     for c in range(chunks):
         inlet_ref[pl.ds(c * ny, ny), :] = flux[c, 0]
 
@@ -581,50 +576,54 @@
             south = north
         return 0
 
-    lax.fori_loop(0, nx, fluxes, 0)
+    lax.fori_loop(0, nx, fluxes, 0, unroll=2)
     send_out(False)
 
 
-def flow(base_flux, saturation, sides, ends_corner, rates, made, rock_perm, rock_poro):
-    nx, ny, nz = base_flux.shape
+def flow(block, base_flux, saturation, sides, ends_corner, rates, made, rock_perm, rock_poro):
+    nx, ny, nz = block
     chunks = nz // LANES
     *fields, slope = made
     own = pltpu.VMEM((chunks, nx, ny, LANES), jnp.float32)
     inputs = (base_flux, saturation, *sides, *ends_corner, rates, slope, rock_perm, rock_poro, *fields)
     first = len(inputs) - len(fields)
     return pl.pallas_call(
-        functools.partial(flow_kernel, base_flux.shape),
+        functools.partial(flow_kernel, block),
         name="flow",
         out_shape=tuple(jax.ShapeDtypeStruct(f.shape, f.dtype) for f in fields) + (
-            jax.ShapeDtypeStruct(base_flux.shape, jnp.float32),
+            jax.ShapeDtypeStruct(block, jnp.float32),
             jax.ShapeDtypeStruct((nx, 5 * chunks * ny, LANES), jnp.float32),
             jax.ShapeDtypeStruct((chunks * ny, LANES), jnp.float32),
         ),
-        in_specs=[HBM] * 2 + [VMEM] * 6 + [SMEM] * 2 + [VMEM] * len(fields),
+        in_specs=[HBM] + [VMEM] * 7 + [SMEM] * 2 + [VMEM] * len(fields),
         out_specs=(VMEM,) * len(fields) + (HBM, VMEM, VMEM),
         input_output_aliases={first + i: i for i in range(len(fields))},
-        scratch_shapes=[pltpu.VMEM(wide_shape(base_flux.shape).shape, jnp.float32), own, own, own, pltpu.SemaphoreType.DMA((3, chunks))],
-        compiler_params=pltpu.CompilerParams(vmem_limit_bytes=8 << 20),
+        scratch_shapes=[pltpu.VMEM(wide_shape(block).shape, jnp.float32), own, own, pltpu.SemaphoreType.DMA((3, chunks))],
+        compiler_params=pltpu.CompilerParams(vmem_limit_bytes=FLOW_LIMIT),
     )(*inputs)[-3:]
 
 
-def stage_kernel(stage, inflow_ref, prep_ref, *refs):
-    sat_ref, out_ref, sat, out_sems = refs[-4:]
+def stage_kernel(stage, last, inflow_ref, prep_ref, *refs):
     nx, rows, _ = prep_ref.shape
     plane = rows // 5
+    if last:
+        held_ref, out_ref, sat, sems = refs
+    else:
+        sat, out_ref = refs[-2:]
     chunks, _, ny, _ = sat.shape
-
-    @pl.when(lax.axis_index("gx") == stage)
+    mine = lax.axis_index("gx") == stage
+
+    def send(layer):
+        return [
+            pltpu.make_async_copy(sat.at[c, layer], out_ref.at[layer, :, pl.ds(c * LANES, LANES)], sems.at[layer, c])
+            for c in range(chunks)
+        ]
+
+    @pl.when(mine)
     def _():
-        def send(layer):
-            return [
-                pltpu.make_async_copy(sat.at[c, layer], sat_ref.at[layer, :, pl.ds(c * LANES, LANES)], out_sems.at[layer, c])
-                for c in range(chunks)
-            ]
-
         def advance(layer, incoming):
-            first, gain, through, volume, held = (prep_ref[layer, pl.ds(i * plane, plane), :] for i in range(5))
-            known = held + incoming
+            first, gain, through, volume, base = (prep_ref[layer, pl.ds(i * plane, plane), :] for i in range(5))
+            known = base + incoming
             water = jnp.clip(first + gain * incoming, 0.0, 1.0)
             for _ in range(NEWTON - 1):
                 square = water * water
@@ -636,38 +635,54 @@
                 water = jnp.clip(top / bottom, 0.0, 1.0)
             for c in range(chunks):
                 sat[c, layer] = water[c * ny : (c + 1) * ny]
-            for copy in send(layer):
-                copy.start()
+            if last:
+                for copy in send(layer):
+                    copy.start()
             square = water * water
             return (through * square) / (1.5 * square + (0.5 - water))
 
-        out_ref[...] = lax.fori_loop(0, nx, advance, inflow_ref[...])
-
-        def finish(layer, _):
-            for copy in send(layer):
+        outflow = lax.fori_loop(0, nx, advance, inflow_ref[...], unroll=STAGE_UNROLL)
+        if not last:
+            out_ref[...] = outflow
+        else:
+            def finish(layer, _):
+                for copy in send(layer):
+                    copy.wait()
+                return 0
+
+            lax.fori_loop(0, nx, finish, 0)
+
+    if last:
+        @pl.when(jnp.logical_not(mine))
+        def _():
+            copies = [
+                pltpu.make_async_copy(held_ref.at[c], out_ref.at[:, :, pl.ds(c * LANES, LANES)], sems.at[0, c])
+                for c in range(chunks)
+            ]
+            for copy in copies:
+                copy.start()
+            for copy in copies:
                 copy.wait()
-            return 0
-
-        lax.fori_loop(0, nx, finish, 0)
-
-
-def run_stage(stage, inflow, prep, shape, saturation):
-    nx, ny, nz = shape
+
+
+def run_stage(stage, last, inflow, prep, block, held):
+    nx, ny, nz = block
     chunks = nz // LANES
-    block = jax.ShapeDtypeStruct(shape, jnp.float32)
+    own = (chunks, nx, ny, LANES)
     return pl.pallas_call(
-        functools.partial(stage_kernel, stage),
+        functools.partial(stage_kernel, stage, last),
         name="stage",
-        out_shape=(block, jax.ShapeDtypeStruct(inflow.shape, jnp.float32)),
-        in_specs=[VMEM, VMEM] + [HBM] * len(saturation),
-        out_specs=(HBM, VMEM),
-        input_output_aliases={2: 0} if saturation else {},
-        scratch_shapes=[
-            pltpu.VMEM((chunks, nx, ny, LANES), jnp.float32),
-            pltpu.SemaphoreType.DMA((nx, chunks)),
-        ],
-        compiler_params=pltpu.CompilerParams(vmem_limit_bytes=12 << 20),
-    )(inflow, prep, *saturation)
+        out_shape=(
+            jax.ShapeDtypeStruct(block, jnp.float32)
+            if last
+            else (jax.ShapeDtypeStruct(own, jnp.float32), jax.ShapeDtypeStruct(inflow.shape, jnp.float32))
+        ),
+        in_specs=[VMEM] * (2 + len(held)),
+        out_specs=HBM if last else (VMEM, VMEM),
+        input_output_aliases={2: 0} if held and not last else {},
+        scratch_shapes=[pltpu.VMEM(own, jnp.float32), pltpu.SemaphoreType.DMA((nx, chunks))] if last else [],
+        compiler_params=pltpu.CompilerParams(vmem_limit_bytes=4 << 20),
+    )(inflow, prep, *held)
 
 
 def step(rock_type, rock_perm, rock_poro, base_flux, initial_pressure, old_saturation, well_cells, well_rates):
@@ -675,19 +690,20 @@
     sides = pack_sides(initial_pressure, rock_type, old_saturation)
     sides_got = swap(*sides, "gy")
     ends = swap(*pack_ends(initial_pressure, rock_type, sides[0]), "gx")
-    rates = rates_field(rock_type.shape, well_cells, well_rates)
-    *fields, frac, slope = ready_own(initial_pressure, rock_type, old_saturation, rates, rock_perm, rock_poro)
+    block = rock_type.shape
+    *fields, frac, slope, water, rates = ready_own(initial_pressure, rock_type, old_saturation, well_cells, well_rates, rock_perm, rock_poro)
     ends_corner = swap(*corners(*sides_got, nx, slope), "gx")
-    fields = ready_ends(rock_type.shape, ends, rates, rock_perm, rock_poro, fields)
+    fields = ready_ends(block, ends, rates, rock_perm, rock_poro, fields)
     made = (*fields, frac, slope)
-    pressure, prep, inflow = flow(base_flux, old_saturation, sides_got, ends_corner, rates, made, rock_perm, rock_poro)
-    saturation = ()
+    pressure, prep, inflow = flow(block, base_flux, water, sides_got, ends_corner, rates, made, rock_perm, rock_poro)
+    swept = ()
     count = lax.axis_size("gx")
-    for stage in range(count):
-        *saturation, outflow = run_stage(stage, inflow, prep, rock_type.shape, saturation)
-        if stage < count - 1:
-            inflow = lax.ppermute(outflow, "gx", [(stage, stage + 1)])
-    return pressure, saturation[0]
+    assert count > 1
+    for stage in range(count - 1):
+        *swept, outflow = run_stage(stage, False, inflow, prep, block, swept)
+        inflow = lax.ppermute(outflow, "gx", [(stage, stage + 1)])
+    saturation = run_stage(count - 1, True, inflow, prep, block, swept)
+    return pressure, saturation
 
 
 def solution(mesh):

time: 68.8 us -> 62.6 us (0.910)
  Pallas kernels: 36.6 us -> 27.9 us
  waiting for transfers between devices: 21.1 us -> 23.8 us
    pallas_call x6 -> x5, Pallas kernels: 20.6 us -> 14 us  [the longest x1 11 us: flow(): pl.pallas_call(functools.partial(flow_kernel, block), name='flow', out_sh...]
    ppermute x3, waiting for transfers between devices: 7.3 us -> 9.86 us  [swap(): got_a = lax.ppermute(value_a, axis, pairs_a)]
    pallas_call x1, Pallas kernels: 4.02 us -> 2.4 us  [ready_ends(): pl.pallas_call(functools.partial(ready_ends_kernel, block), name='ready_e...]
    pallas_call x1, Pallas kernels: 6.81 us -> 6.06 us  [ready_own(): pl.pallas_call(functools.partial(ready_own_kernel, block), name='ready_ow...]
  transfers between devices with their start and end apart: 9 -> 9, of which waited for: 2 -> 3; matrix products, arithmetic and copies ran while one was open for 0% -> 0% of each run, Pallas kernels for 19% -> 14%
where the time goes in v4:
time: 62.6 us; the launch traced here: 62.4 us
  Pallas kernels  27.9 us (45%)
  waiting for transfers between devices  23.8 us (38%)
  starting transfers between devices  9.72 us (16%)
  between operations  0.91 us (1%)
    ppermute x3, waiting for transfers between devices, step(): inflow = lax.ppermute(outflow, 'gx', [(stage, stage + 1)])  13.3 us
    pallas_call x1, Pallas kernels, flow(): pl.pallas_call(functools.partial(flow_kernel, block), name='flow', out_sh...  11 us
    ppermute x3, waiting for transfers between devices, swap(): got_a = lax.ppermute(value_a, axis, pairs_a)  9.86 us
    pallas_call x1, Pallas kernels, ready_own(): pl.pallas_call(functools.partial(ready_own_kernel, block), name='ready_ow...  6.06 us
    ppermute x3, starting transfers between devices, swap(): got_b = lax.ppermute(value_b, axis, pairs_b)  4.38 us
    pallas_call x4, Pallas kernels, run_stage(): pl.pallas_call(functools.partial(stage_kernel, stage, last), name='stage'...  3.01 us
    pallas_call x1, Pallas kernels, pack_ends(): pl.pallas_call(pack_ends_kernel, name='pack_ends', out_shape=(end, end),...  2.74 us
    ppermute x3, starting transfers between devices, swap(): got_a = lax.ppermute(value_a, axis, pairs_a)  2.72 us
  transfers between devices with their start and end apart: 9, of which 3 were waited for; matrix products, arithmetic and copies ran while one was open for 0% of the time, Pallas kernels for 14%

profile of v4, /device:TPU:11, one launch (start us, length us, event | category | flops | bytes accessed | tf_op | source)
XLA Modules:
  0.0 62.4 jit_solution(13524702784596269423)
XLA Ops:
  0.6 0.0 copy-start
  0.6 0.0 copy-start.5
  0.7 0.0 copy-start.4
  0.7 0.0 copy-start.7
  0.7 0.0 copy-start.6
  0.7 2.6 %pack_sides.1 = (f32[704,128]{1,0:T(8,128)}, f32[704,128]{1,0:T(8,128)}) custom-call(f32[16,32,512]{2,1,0:T(8,128)} %p_ref.5, s32[16,32,512]{2,1,0:T(8,128)} %rock_ref.5, f32[16,32,512]{2,1,0:T(8,128)} %sat_ref.3), custom_call_target="tpu_custom_call" | custom-call | tf_op jit(solution)/shard_map/pack_sides/pallas_call | solution.py:95
  3.3 0.0 copy-start.8
  3.3 0.0 copy-start.1
  3.3 0.0 copy-start.2
  3.3 2.7 %pack_ends.1 = (f32[4,10,32,128]{3,2,1,0:T(8,128)}, f32[4,10,32,128]{3,2,1,0:T(8,128)}) custom-call(f32[16,32,512]{2,1,0:T(8,128)} %p_ref.5, s32[16,32,512]{2,1,0:T(8,128)} %rock_ref.5, f32[704,128]{1,0:T(8,128)} %get-tuple-element.38._), custom_call_target="tpu_custom_call" | custom-call | tf_op jit(solution)/shard_map/pack_ends/pallas_call | solution.py:140
  6.0 0.7 %collective-permute-start.4 = (f32[4,10,32,128]{3,2,1,0:T(8,128)}, f32[4,10,32,128]{3,2,1,0:T(8,128)S(1)}, u32[]{:S(2)}, u32[]{:S(2)}) collective-permute-start(f32[4,10,32,128]{3,2,1,0:T(8,128)} %get-tuple-element.44), channel_id=1, source_target_pairs={{0,8},{16,24},{8,0},{24,16},{1,9},{17,25},{9,1},{25,17},{2,10},{18... | collective-permute-start | bytes 1966088 | tf_op jit(solution)/shard_map/ppermute | solution.py:45
  6.8 0.7 %collective-permute-start.5 = (f32[4,10,32,128]{3,2,1,0:T(8,128)}, f32[4,10,32,128]{3,2,1,0:T(8,128)S(1)}, u32[]{:S(2)}, u32[]{:S(2)}) collective-permute-start(f32[4,10,32,128]{3,2,1,0:T(8,128)} %get-tuple-element.45), channel_id=1, source_target_pairs={{8,16},{16,8},{9,17},{17,9},{10,18},{18,10},{11,19},{19,11},{12,20... | collective-permute-start | bytes 1966088 | tf_op jit(solution)/shard_map/ppermute | solution.py:46
  7.5 3.0 %collective-permute-start.1 = (f32[704,128]{1,0:T(8,128)}, f32[704,128]{1,0:T(8,128)S(1)}, u32[]{:S(2)}, u32[]{:S(2)}) collective-permute-start(f32[704,128]{1,0:T(8,128)} %get-tuple-element.39), channel_id=1, source_target_pairs={{1,2},{3,4},{5,6},{2,1},{4,3},{6,5},{9,10},{11,12},{13,14},{10,9},... | collective-permute-start | bytes 1081352 | tf_op jit(solution)/shard_map/ppermute | solution.py:46
  10.5 0.0 copy-done.8
  10.5 1.4 %collective-permute-start = (f32[704,128]{1,0:T(8,128)S(1)}, f32[704,128]{1,0:T(8,128)S(1)}, u32[]{:S(2)}, u32[]{:S(2)}) collective-permute-start(f32[704,128]{1,0:T(8,128)S(1)} %copy-done.8), channel_id=1, source_target_pairs={{0,1},{2,3},{4,5},{6,7},{1,0},{3,2},{5,4},{7,6},{8,9},{10,11},{12,... | collective-permute-start | bytes 1081352 | tf_op jit(solution)/shard_map/ppermute | solution.py:45
  12.0 0.0 copy-done
  12.0 0.0 copy-done.5
  12.0 0.0 copy-done.4
  12.0 0.0 copy-done.7
  12.0 0.0 copy-done.6
  12.0 0.0 copy-done.1
  12.0 0.0 copy-done.2
  12.0 6.1 %ready_own.1 = (f32[4576,128]{1,0:T(8,128)S(1)}, f32[4576,128]{1,0:T(8,128)S(1)}, f32[4576,128]{1,0:T(8,128)S(1)}, f32[4576,128]{1,0:T(8,128)S(1)}, f32[4576,128...) custom-call(s32[16,32,512]{2,1,0:T(8,128)S(1)} %copy-done, ...), custom_call_target="tpu_custom_call" | custom-call | bytes 25165824 | tf_op jit(solution)/shard_map/ready_own/pallas_call | solution.py:362
  18.1 0.6 collective-permute-done.1.yb_ref
  18.7 9.9 %collective-permute-done.ya_ref = f32[704,128]{1,0:T(8,128)S(1)} collective-permute-done((f32[704,128]{1,0:T(8,128)S(1)}, f32[704,128]{1,0:T(8,128)S(1)}, u32[]{:S(2)}, u32[]{:S(2)}) %collective-permute-start) | collective-permute-done | bytes 360480 | tf_op jit(solution)/shard_map/ppermute | solution.py:45
  28.6 0.2 corners.1
  28.7 0.6 collective-permute-start.2
  29.3 0.7 %collective-permute-start.3 = (f32[256,128]{1,0:T(8,128)S(1)}, f32[256,128]{1,0:T(8,128)S(1)}, u32[]{:S(2)}, u32[]{:S(2)}) collective-permute-start(f32[256,128]{1,0:T(8,128)S(1)} %get-tuple-element.42), channel_id=1, source_target_pairs={{8,16},{16,8},{9,17},{17,9},{10,18},{18,10},{11,19},{19,11},{12,20... | collective-permute-start | bytes 393224 | tf_op jit(solution)/shard_map/ppermute | solution.py:46
  30.0 0.0 collective-permute-done.4.xa_ref
  30.0 0.0 collective-permute-done.5.xb_ref
  30.0 0.0 copy-start.3
  30.0 2.4 %ready_ends.1 = (f32[4576,128]{1,0:T(8,128)S(1)}, f32[4576,128]{1,0:T(8,128)S(1)}, f32[4576,128]{1,0:T(8,128)S(1)}, f32[4576,128]{1,0:T(8,128)S(1)}, f32[4576,12...) custom-call(f32[4,10,32,128]{3,2,1,0:T(8,128)S(1)} %collective-permu, ...), custom_call_target="tpu_custom_call", output_to_operand_aliasing={{0}: (5, {}), {1}: (6, {}), {2}: (7, {}), {3}: (8, {}), {4}... | custom-call | bytes 9437184 | tf_op jit(solution)/shard_map/ready_ends/pallas_call | solution.py:409
  32.4 0.0 collective-permute-done.2.ca_ref
  32.4 0.0 collective-permute-done.3.cb_ref
  32.4 0.0 copy-done.3
  32.4 11.0 %flow.1 = (f32[4576,128]{1,0:T(8,128)S(1)}, f32[4576,128]{1,0:T(8,128)S(1)}, f32[4576,128]{1,0:T(8,128)S(1)}, f32[4576,128]{1,0:T(8,128)S(1)}, f32[4576,128]{1,0...) custom-call(f32[16,32,512]{2,1,0:T(8,128)S(1)} %copy-done.3, ...), custom_call_target="tpu_custom_call", output_to_operand_aliasing={{0}: (10, {}), {1}: (11, {}), {2}: (12, {}), {3}: (13, {}),... | custom-call | tf_op jit(solution)/shard_map/flow/pallas_call | solution.py:590
  43.4 0.7 %collective-permute-start.6 = (f32[128,128]{1,0:T(8,128)S(1)}, f32[128,128]{1,0:T(8,128)S(1)}, u32[]{:S(2)}, u32[]{:S(2)}) collective-permute-start(f32[128,128]{1,0:T(8,128)S(1)} %get-tuple-element.66), channel_id=1, source_target_pairs={{0,8},{1,9},{2,10},{3,11},{4,12},{5,13},{6,14},{7,15}} | collective-permute-start | bytes 196616 | tf_op jit(solution)/shard_map/ppermute | solution.py:704
  44.1 0.0 collective-permute-done.6.inflow_ref
  44.1 0.7 %collective-permute-start.7 = (f32[128,128]{1,0:T(8,128)S(1)}, f32[128,128]{1,0:T(8,128)S(1)}, u32[]{:S(2)}, u32[]{:S(2)}) collective-permute-start(f32[128,128]{1,0:T(8,128)S(1)} %get-tuple-element.68), channel_id=1, source_target_pairs={{8,16},{9,17},{10,18},{11,19},{12,20},{13,21},{14,22},{15,23}} | collective-permute-start | bytes 196616 | tf_op jit(solution)/shard_map/ppermute | solution.py:704
  44.8 0.0 collective-permute-done.7.inflow_ref
  44.8 1.3 %collective-permute-start.8 = (f32[128,128]{1,0:T(8,128)S(1)}, f32[128,128]{1,0:T(8,128)S(1)}, u32[]{:S(2)}, u32[]{:S(2)}) collective-permute-start(f32[128,128]{1,0:T(8,128)S(1)} %get-tuple-element.70), channel_id=1, source_target_pairs={{16,24},{17,25},{18,26},{19,27},{20,28},{21,29},{22,30},{23,31}} | collective-permute-start | bytes 196616 | tf_op jit(solution)/shard_map/ppermute | solution.py:704
  46.1 13.3 %collective-permute-done.8.inflow_ref = f32[128,128]{1,0:T(8,128)S(1)} collective-permute-done((f32[128,128]{1,0:T(8,128)S(1)}, f32[128,128]{1,0:T(8,128)S(1)}, u32[]{:S(2)}, u32[]{:S(2)}) %collective-permute-start.8) | collective-permute-done | bytes 65568 | tf_op jit(solution)/shard_map/ppermute | solution.py:704
  59.4 3.0 %stage.7 = f32[16,32,512]{2,1,0:T(8,128)} custom-call(f32[128,128]{1,0:T(8,128)S(1)} %collective-permute-done.8.inflow_ref, f32[16,640,128]{2,1,0:T(8,128)S(1)} %get-tuple-element.65.prep_ref, f32[4,16,32,128]{3,2,1,0:T(8,128)S(1)} %get-tuple-element.71.refs_0_), custom_call_target="tpu_custom_call" | custom-call | tf_op jit(solution)/shard_map/stage/pallas_call | solution.py:672
  (3 shorter events, 0.1 us)
Async XLA Ops:
  0.6 11.3 %copy-start = (s32[16,32,512]{2,1,0:T(8,128)S(1)}, s32[16,32,512]{2,1,0:T(8,128)}, u32[]{:S(2)}) copy-start(s32[16,32,512]{2,1,0:T(8,128)} %rock_ref.5) | copy-start | bytes 3145732
  0.6 11.3 %copy-start.5 = (f32[8]{0:T(128)S(1)}, f32[8]{0:T(128)}, u32[]{:S(2)}) copy-start(f32[8]{0:T(128)} %poro_ref.5) | copy-start | bytes 100
  0.7 11.3 %copy-start.4 = (f32[8]{0:T(128)S(1)}, f32[8]{0:T(128)}, u32[]{:S(2)}) copy-start(f32[8]{0:T(128)} %perm_ref.5) | copy-start | bytes 100
  0.7 11.3 %copy-start.7 = (f32[128]{0:T(128)S(1)}, f32[128]{0:T(128)}, u32[]{:S(2)}) copy-start(f32[128]{0:T(128)} %well_ref.1) | copy-start | bytes 1540
  0.7 11.3 %copy-start.6 = (s32[3,128]{1,0:T(4,128)S(1)}, s32[3,128]{1,0:T(4,128)}, u32[]{:S(2)}) copy-start(s32[3,128]{1,0:T(4,128)} %cells_ref.1) | copy-start | bytes 4612
  3.3 7.3 %copy-start.8 = (f32[704,128]{1,0:T(8,128)S(1)}, f32[704,128]{1,0:T(8,128)}, u32[]{:S(2)}) copy-start(f32[704,128]{1,0:T(8,128)} %get-tuple-element.38._) | copy-start | bytes 1081348
  3.3 8.7 %copy-start.1 = (f32[16,32,512]{2,1,0:T(8,128)S(1)}, f32[16,32,512]{2,1,0:T(8,128)}, u32[]{:S(2)}) copy-start(f32[16,32,512]{2,1,0:T(8,128)} %p_ref.5) | copy-start | bytes 3145732
  3.3 8.7 %copy-start.2 = (f32[16,32,512]{2,1,0:T(8,128)S(1)}, f32[16,32,512]{2,1,0:T(8,128)}, u32[]{:S(2)}) copy-start(f32[16,32,512]{2,1,0:T(8,128)} %sat_ref.3) | copy-start | bytes 3145732
  6.0 23.9 %collective-permute-start.4 = (f32[4,10,32,128]{3,2,1,0:T(8,128)}, f32[4,10,32,128]{3,2,1,0:T(8,128)S(1)}, u32[]{:S(2)}, u32[]{:S(2)}) collective-permute-start(f32[4,10,32,128]{3,2,1,0:T(8,128)} %get-tuple-element.44), channel_id=1, source_target_pairs={{0,8},{16,24},{8,0},{24,16},{1,9},{17,25},{9,1},{25,17},{2,10},{18... | collective-permute-start | bytes 1966088 | tf_op jit(solution)/shard_map/ppermute | solution.py:45
  6.8 23.2 %collective-permute-start.5 = (f32[4,10,32,128]{3,2,1,0:T(8,128)}, f32[4,10,32,128]{3,2,1,0:T(8,128)S(1)}, u32[]{:S(2)}, u32[]{:S(2)}) collective-permute-start(f32[4,10,32,128]{3,2,1,0:T(8,128)} %get-tuple-element.45), channel_id=1, source_target_pairs={{8,16},{16,8},{9,17},{17,9},{10,18},{18,10},{11,19},{19,11},{12,20... | collective-permute-start | bytes 1966088 | tf_op jit(solution)/shard_map/ppermute | solution.py:46
  7.5 11.2 %collective-permute-start.1 = (f32[704,128]{1,0:T(8,128)}, f32[704,128]{1,0:T(8,128)S(1)}, u32[]{:S(2)}, u32[]{:S(2)}) collective-permute-start(f32[704,128]{1,0:T(8,128)} %get-tuple-element.39), channel_id=1, source_target_pairs={{1,2},{3,4},{5,6},{2,1},{4,3},{6,5},{9,10},{11,12},{13,14},{10,9},... | collective-permute-start | bytes 1081352 | tf_op jit(solution)/shard_map/ppermute | solution.py:46
  10.5 18.0 %collective-permute-start = (f32[704,128]{1,0:T(8,128)S(1)}, f32[704,128]{1,0:T(8,128)S(1)}, u32[]{:S(2)}, u32[]{:S(2)}) collective-permute-start(f32[704,128]{1,0:T(8,128)S(1)} %copy-done.8), channel_id=1, source_target_pairs={{0,1},{2,3},{4,5},{6,7},{1,0},{3,2},{5,4},{7,6},{8,9},{10,11},{12,... | collective-permute-start | bytes 1081352 | tf_op jit(solution)/shard_map/ppermute | solution.py:45
  28.7 3.7 %collective-permute-start.2 = (f32[256,128]{1,0:T(8,128)S(1)}, f32[256,128]{1,0:T(8,128)S(1)}, u32[]{:S(2)}, u32[]{:S(2)}) collective-permute-start(f32[256,128]{1,0:T(8,128)S(1)} %get-tuple-element.41), channel_id=1, source_target_pairs={{0,8},{16,24},{8,0},{24,16},{1,9},{17,25},{9,1},{25,17},{2,10},{18... | collective-permute-start | bytes 393224 | tf_op jit(solution)/shard_map/ppermute | solution.py:45
  29.3 3.1 %collective-permute-start.3 = (f32[256,128]{1,0:T(8,128)S(1)}, f32[256,128]{1,0:T(8,128)S(1)}, u32[]{:S(2)}, u32[]{:S(2)}) collective-permute-start(f32[256,128]{1,0:T(8,128)S(1)} %get-tuple-element.42), channel_id=1, source_target_pairs={{8,16},{16,8},{9,17},{17,9},{10,18},{18,10},{11,19},{19,11},{12,20... | collective-permute-start | bytes 393224 | tf_op jit(solution)/shard_map/ppermute | solution.py:46
  30.0 2.4 %copy-start.3 = (f32[16,32,512]{2,1,0:T(8,128)S(1)}, f32[16,32,512]{2,1,0:T(8,128)}, u32[]{:S(2)}) copy-start(f32[16,32,512]{2,1,0:T(8,128)} %flux_ref.1) | copy-start | bytes 3145732
  43.4 0.7 %collective-permute-start.6 = (f32[128,128]{1,0:T(8,128)S(1)}, f32[128,128]{1,0:T(8,128)S(1)}, u32[]{:S(2)}, u32[]{:S(2)}) collective-permute-start(f32[128,128]{1,0:T(8,128)S(1)} %get-tuple-element.66), channel_id=1, source_target_pairs={{0,8},{1,9},{2,10},{3,11},{4,12},{5,13},{6,14},{7,15}} | collective-permute-start | bytes 196616 | tf_op jit(solution)/shard_map/ppermute | solution.py:704
  44.1 0.7 %collective-permute-start.7 = (f32[128,128]{1,0:T(8,128)S(1)}, f32[128,128]{1,0:T(8,128)S(1)}, u32[]{:S(2)}, u32[]{:S(2)}) collective-permute-start(f32[128,128]{1,0:T(8,128)S(1)} %get-tuple-element.68), channel_id=1, source_target_pairs={{8,16},{9,17},{10,18},{11,19},{12,20},{13,21},{14,22},{15,23}} | collective-permute-start | bytes 196616 | tf_op jit(solution)/shard_map/ppermute | solution.py:704
  44.8 14.6 %collective-permute-start.8 = (f32[128,128]{1,0:T(8,128)S(1)}, f32[128,128]{1,0:T(8,128)S(1)}, u32[]{:S(2)}, u32[]{:S(2)}) collective-permute-start(f32[128,128]{1,0:T(8,128)S(1)} %get-tuple-element.70), channel_id=1, source_target_pairs={{16,24},{17,25},{18,26},{19,27},{20,28},{21,29},{22,30},{23,31}} | collective-permute-start | bytes 196616 | tf_op jit(solution)/shard_map/ppermute | solution.py:704

commit v5 on v4

--- a/solution.py
+++ b/solution.py
@@ -315,6 +315,45 @@
     lax.fori_loop(first, last, prepare, 0, unroll=2)
 
 
+def edge_groups(block):
+    nx = block[0]
+    inside, outside = [], []
+    for group in range((nx + 2 * REACH - 2) // 8):
+        low, high = 1 + group * 8, 8 + group * 8
+        (inside if low > REACH and high < REACH + nx - 1 else outside).append(group)
+    return inside, outside
+
+
+def complete_rows(block, fields, rates, group):
+    press, perms, stores, trans_x, trans_y, trans_z, scale, drive = fields
+    chunks, layers, pitch = wide_sizes(block)
+    lane = lax.broadcasted_iota(jnp.int32, (8, LANES), 1)
+    for first in (PAD - PASSES, PAD + block[1] - 1):
+        def rows(k, by, c):
+            return pl.ds((c * layers + 1 + group * 8 + by) * pitch + first + k, 8, stride=pitch)
+
+        perm = {k: [perms[rows(k, 0, c), :] for c in range(chunks)] for k in range(-1, PASSES + 2)}
+        t_s = [transmit(perm[-1][c], perm[0][c]) for c in range(chunks)]
+        for c in range(chunks):
+            trans_y[rows(-1, 0, c), :] = t_s[c]
+        for k in range(PASSES + 1):
+            deep = deeper(perm[k])
+            t_z = [transmit(perm[k][c], deep[c]) for c in range(chunks)]
+            t_z[-1] = jnp.where(lane == LANES - 1, 0.0, t_z[-1])
+            above = shallower(t_z)
+            for c in range(chunks):
+                at = rows(k, 0, c)
+                t_x = transmit(perm[k][c], perms[rows(k, 1, c), :])
+                t_w = transmit(perm[k][c], perms[rows(k, -1, c), :])
+                t_n = transmit(perm[k][c], perm[k + 1][c])
+                trans_x[at, :], trans_y[at, :], trans_z[at, :] = t_x, t_n, t_z[c]
+                store = stores[at, :]
+                factor = OMEGA / (store + ((t_x + t_w) + (t_n + t_s[c]) + (t_z[c] + above[c])))
+                scale[at, :] = factor
+                drive[at, :] = factor * (store * press[at, :] + rates[at, :])
+                t_s[c] = t_n
+
+
 def ready_own_kernel(block, rock_ref, p_ref, sat_ref, cells_ref, well_ref, perm_ref, poro_ref, *refs):
     fields, (frac, slope, sat, rates_ref, rock, p, sems) = refs[:8], refs[8:]
     sources = ((rock_ref, rock), (p_ref, p), (sat_ref, sat))
@@ -377,8 +416,9 @@
     )(rock_type, pressure, saturation, well_cells, well_rates, rock_perm, rock_poro)
 
 
-def ready_ends_kernel(block, xa_ref, xb_ref, rates_ref, perm_ref, poro_ref, *refs):
+def ready_ends_kernel(block, xa_ref, xb_ref, ya_ref, yb_ref, rates_ref, perm_ref, poro_ref, *refs):
     fields = refs[8:16]
+    even_y = lax.rem(lax.axis_index("gy"), 2) == 0
     press, perms, stores = fields[:3]
     (nx, ny, _), (chunks, layers, pitch) = block, wide_sizes(block)
     step = ny // 8
@@ -402,17 +442,31 @@
     lax.fori_loop(0, REACH, look, 0, unroll=True)
     prepare_layers(block, fields, rates_ref, 0, REACH + 1)
     prepare_layers(block, fields, rates_ref, REACH + nx - 1, layers - 1)
-
-
-def ready_ends(block, ends, rates, rock_perm, rock_poro, fields):
-    inputs = (*ends, rates, rock_perm, rock_poro, *fields)
+    for c in range(chunks):
+        for j in range(REACH):
+            for half in range(nx // 8):
+                start = (c * (2 * REACH + 1) + j) * nx + half * 8
+                at = (c * layers + REACH + half * 8) * pitch + j
+                low = pl.ds(at + PAD - REACH, 8, stride=pitch)
+                high = pl.ds(at + PAD + ny, 8, stride=pitch)
+                a, b = ya_ref[pl.ds(start, 8), :], yb_ref[pl.ds(start, 8), :]
+                press[low, :], press[high, :] = jnp.where(even_y, b, a), jnp.where(even_y, a, b)
+                a, b = (ref[pl.ds(start + REACH * nx, 8), :].astype(jnp.int32) for ref in (ya_ref, yb_ref))
+                for where, kind in ((low, jnp.where(even_y, b, a)), (high, jnp.where(even_y, a, b))):
+                    perms[where, :], stores[where, :] = rock_of(kind, tables)
+    for group in edge_groups(block)[0]:
+        complete_rows(block, fields, rates_ref, group)
+
+
+def ready_ends(block, ends, sides, rates, rock_perm, rock_poro, fields):
+    inputs = (*ends, *sides, rates, rock_perm, rock_poro, *fields)
     return pl.pallas_call(
         functools.partial(ready_ends_kernel, block),
         name="ready_ends",
         out_shape=tuple(jax.ShapeDtypeStruct(f.shape, f.dtype) for f in fields),
-        in_specs=[VMEM] * 3 + [SMEM] * 2 + [VMEM] * len(fields),
+        in_specs=[VMEM] * 5 + [SMEM] * 2 + [VMEM] * len(fields),
         out_specs=(VMEM,) * len(fields),
-        input_output_aliases={5 + i: i for i in range(len(fields))},
+        input_output_aliases={7 + i: i for i in range(len(fields))},
         cost_estimate=pl.CostEstimate(flops=0, bytes_accessed=9 << 20, transcendentals=0),
         compiler_params=pltpu.CompilerParams(vmem_limit_bytes=4 << 20),
     )(*inputs)
@@ -436,17 +490,6 @@
     lane = lax.broadcasted_iota(jnp.int32, (8, LANES), 1)
 
     for c in range(chunks):
-        for j in range(REACH):
-            for half in range(nx // 8):
-                start = c * side_rows + j * nx + half * 8
-                at = c * depth + (REACH + half * 8) * pitch + j
-                low = pl.ds(at + PAD - REACH, 8, stride=pitch)
-                high = pl.ds(at + PAD + ny, 8, stride=pitch)
-                a, b = ya_ref[pl.ds(start, 8), :], yb_ref[pl.ds(start, 8), :]
-                press2[low, :], press2[high, :] = jnp.where(even_y, b, a), jnp.where(even_y, a, b)
-                a, b = (ref[pl.ds(start + REACH * nx, 8), :].astype(jnp.int32) for ref in (ya_ref, yb_ref))
-                for where, kind in ((low, jnp.where(even_y, b, a)), (high, jnp.where(even_y, a, b))):
-                    perms2[where, :], stores2[where, :] = rock_of(kind, tables)
         start = c * side_rows + 2 * REACH * nx
         a, b = fraction(ya_ref[pl.ds(start, nx), :]), fraction(yb_ref[pl.ds(start, nx), :])
         at = c * nx * pitch
@@ -466,34 +509,8 @@
                     ref[pl.ds(at - PASSES, PASSES), :] = new[:PASSES]
                     ref[pl.ds(at + ny, PASSES), :] = new[PASSES:]
 
-    def complete(group, _):
-        for first in (PAD - PASSES, PAD + ny - 1):
-            def rows(k, by, c):
-                return pl.ds(c * depth + (1 + group * 8 + by) * pitch + first + k, 8, stride=pitch)
-
-            perm = {k: [perms2[rows(k, 0, c), :] for c in range(chunks)] for k in range(-1, PASSES + 2)}
-            t_s = [transmit(perm[-1][c], perm[0][c]) for c in range(chunks)]
-            for c in range(chunks):
-                ty2[rows(-1, 0, c), :] = t_s[c]
-            for k in range(PASSES + 1):
-                deep = deeper(perm[k])
-                t_z = [transmit(perm[k][c], deep[c]) for c in range(chunks)]
-                t_z[-1] = jnp.where(lane == LANES - 1, 0.0, t_z[-1])
-                above = shallower(t_z)
-                for c in range(chunks):
-                    at = rows(k, 0, c)
-                    t_x = transmit(perm[k][c], perms2[rows(k, 1, c), :])
-                    t_w = transmit(perm[k][c], perms2[rows(k, -1, c), :])
-                    t_n = transmit(perm[k][c], perm[k + 1][c])
-                    tx2[at, :], ty2[at, :], tz2[at, :] = t_x, t_n, t_z[c]
-                    store = stores2[at, :]
-                    factor = OMEGA / (store + ((t_x + t_w) + (t_n + t_s[c]) + (t_z[c] + above[c])))
-                    scale2[at, :] = factor
-                    drive2[at, :] = factor * (store * press2[at, :] + rates2[at, :])
-                    t_s[c] = t_n
-        return 0
-
-    lax.fori_loop(0, (layers - 2) // 8, complete, 0)
+    for group in edge_groups(block)[1]:
+        complete_rows(block, (press, perms, stores, trans_x, trans_y, trans_z, scale, drive), rates_ref, group)
 
     def relax(source, target, number):
         def one(layer, _):
@@ -613,9 +630,11 @@
     chunks, _, ny, _ = sat.shape
     mine = lax.axis_index("gx") == stage
 
-    def send(layer):
+    def send(first, count, slot):
         return [
-            pltpu.make_async_copy(sat.at[c, layer], out_ref.at[layer, :, pl.ds(c * LANES, LANES)], sems.at[layer, c])
+            pltpu.make_async_copy(
+                sat.at[c, pl.ds(first, count)], out_ref.at[pl.ds(first, count), :, pl.ds(c * LANES, LANES)], sems.at[slot, c]
+            )
             for c in range(chunks)
         ]
 
@@ -635,22 +654,22 @@
                 water = jnp.clip(top / bottom, 0.0, 1.0)
             for c in range(chunks):
                 sat[c, layer] = water[c * ny : (c + 1) * ny]
-            if last:
-                for copy in send(layer):
-                    copy.start()
             square = water * water
             return (through * square) / (1.5 * square + (0.5 - water))
 
-        outflow = lax.fori_loop(0, nx, advance, inflow_ref[...], unroll=STAGE_UNROLL)
+        outflow, parts, done = inflow_ref[...], [], 0
+        for slot, count in enumerate((nx // 2, nx // 4, nx - nx // 2 - nx // 4) if last else (nx,)):
+            outflow = lax.fori_loop(done, done + count, advance, outflow, unroll=STAGE_UNROLL)
+            if last:
+                parts.append(send(done, count, slot))
+                for copy in parts[-1]:
+                    copy.start()
+            done += count
         if not last:
             out_ref[...] = outflow
-        else:
-            def finish(layer, _):
-                for copy in send(layer):
-                    copy.wait()
-                return 0
-
-            lax.fori_loop(0, nx, finish, 0)
+        for part in parts:
+            for copy in part:
+                copy.wait()
 
     if last:
         @pl.when(jnp.logical_not(mine))
@@ -680,7 +699,7 @@
         in_specs=[VMEM] * (2 + len(held)),
         out_specs=HBM if last else (VMEM, VMEM),
         input_output_aliases={2: 0} if held and not last else {},
-        scratch_shapes=[pltpu.VMEM(own, jnp.float32), pltpu.SemaphoreType.DMA((nx, chunks))] if last else [],
+        scratch_shapes=[pltpu.VMEM(own, jnp.float32), pltpu.SemaphoreType.DMA((3, chunks))] if last else [],
         compiler_params=pltpu.CompilerParams(vmem_limit_bytes=4 << 20),
     )(inflow, prep, *held)
 
@@ -693,7 +712,7 @@
     block = rock_type.shape
     *fields, frac, slope, water, rates = ready_own(initial_pressure, rock_type, old_saturation, well_cells, well_rates, rock_perm, rock_poro)
     ends_corner = swap(*corners(*sides_got, nx, slope), "gx")
-    fields = ready_ends(block, ends, rates, rock_perm, rock_poro, fields)
+    fields = ready_ends(block, ends, sides_got, rates, rock_perm, rock_poro, fields)
     made = (*fields, frac, slope)
     pressure, prep, inflow = flow(block, base_flux, water, sides_got, ends_corner, rates, made, rock_perm, rock_poro)
     swept = ()

time: 62.6 us -> 61.5 us (0.982)
    pallas_call x1, Pallas kernels: 11 us -> 10.3 us  [flow(): pl.pallas_call(functools.partial(flow_kernel, block), name='flow', out_sh...]
  transfers between devices with their start and end apart: 9 -> 9, of which waited for: 3 -> 3; matrix products, arithmetic and copies ran while one was open for 0% -> 0% of each run, Pallas kernels for 14% -> 15%
where the time goes in v5:
time: 61.5 us; the launch traced here: 61.2 us
  Pallas kernels  27.3 us (44%)
  waiting for transfers between devices  23.2 us (38%)
  starting transfers between devices  9.72 us (16%)
  between operations  0.91 us (1%)
    ppermute x3, waiting for transfers between devices, step(): inflow = lax.ppermute(outflow, 'gx', [(stage, stage + 1)])  12.7 us
    pallas_call x1, Pallas kernels, flow(): pl.pallas_call(functools.partial(flow_kernel, block), name='flow', out_sh...  10.3 us
    ppermute x3, waiting for transfers between devices, swap(): got_a = lax.ppermute(value_a, axis, pairs_a)  9.86 us
    pallas_call x1, Pallas kernels, ready_own(): pl.pallas_call(functools.partial(ready_own_kernel, block), name='ready_ow...  6.06 us
    ppermute x3, starting transfers between devices, swap(): got_b = lax.ppermute(value_b, axis, pairs_b)  4.38 us
    pallas_call x1, Pallas kernels, ready_ends(): pl.pallas_call(functools.partial(ready_ends_kernel, block), name='ready_e...  2.94 us
    pallas_call x1, Pallas kernels, pack_ends(): pl.pallas_call(pack_ends_kernel, name='pack_ends', out_shape=(end, end),...  2.74 us
    ppermute x3, starting transfers between devices, swap(): got_a = lax.ppermute(value_a, axis, pairs_a)  2.72 us
  transfers between devices with their start and end apart: 9, of which 3 were waited for; matrix products, arithmetic and copies ran while one was open for 0% of the time, Pallas kernels for 15%

profile of v5, /device:TPU:11, one launch (start us, length us, event | category | flops | bytes accessed | tf_op | source)
XLA Modules:
  0.0 61.2 jit_solution(4463355536862059649)
XLA Ops:
  0.6 0.0 copy-start
  0.6 0.0 copy-start.5
  0.7 0.0 copy-start.4
  0.7 0.0 copy-start.7
  0.7 0.0 copy-start.6
  0.7 2.6 %pack_sides.1 = (f32[704,128]{1,0:T(8,128)}, f32[704,128]{1,0:T(8,128)}) custom-call(f32[16,32,512]{2,1,0:T(8,128)} %p_ref.5, s32[16,32,512]{2,1,0:T(8,128)} %rock_ref.5, f32[16,32,512]{2,1,0:T(8,128)} %sat_ref.3), custom_call_target="tpu_custom_call" | custom-call | tf_op jit(solution)/shard_map/pack_sides/pallas_call | solution.py:95
  3.3 0.0 copy-start.8
  3.3 0.0 copy-start.1
  3.3 0.0 copy-start.2
  3.3 2.7 %pack_ends.1 = (f32[4,10,32,128]{3,2,1,0:T(8,128)}, f32[4,10,32,128]{3,2,1,0:T(8,128)}) custom-call(f32[16,32,512]{2,1,0:T(8,128)} %p_ref.5, s32[16,32,512]{2,1,0:T(8,128)} %rock_ref.5, f32[704,128]{1,0:T(8,128)} %get-tuple-element.38._), custom_call_target="tpu_custom_call" | custom-call | tf_op jit(solution)/shard_map/pack_ends/pallas_call | solution.py:140
  6.0 0.7 %collective-permute-start.4 = (f32[4,10,32,128]{3,2,1,0:T(8,128)}, f32[4,10,32,128]{3,2,1,0:T(8,128)S(1)}, u32[]{:S(2)}, u32[]{:S(2)}) collective-permute-start(f32[4,10,32,128]{3,2,1,0:T(8,128)} %get-tuple-element.44), channel_id=1, source_target_pairs={{0,8},{16,24},{8,0},{24,16},{1,9},{17,25},{9,1},{25,17},{2,10},{18... | collective-permute-start | bytes 1966088 | tf_op jit(solution)/shard_map/ppermute | solution.py:45
  6.8 0.7 %collective-permute-start.5 = (f32[4,10,32,128]{3,2,1,0:T(8,128)}, f32[4,10,32,128]{3,2,1,0:T(8,128)S(1)}, u32[]{:S(2)}, u32[]{:S(2)}) collective-permute-start(f32[4,10,32,128]{3,2,1,0:T(8,128)} %get-tuple-element.45), channel_id=1, source_target_pairs={{8,16},{16,8},{9,17},{17,9},{10,18},{18,10},{11,19},{19,11},{12,20... | collective-permute-start | bytes 1966088 | tf_op jit(solution)/shard_map/ppermute | solution.py:46
  7.5 3.0 %collective-permute-start.1 = (f32[704,128]{1,0:T(8,128)}, f32[704,128]{1,0:T(8,128)S(1)}, u32[]{:S(2)}, u32[]{:S(2)}) collective-permute-start(f32[704,128]{1,0:T(8,128)} %get-tuple-element.39), channel_id=1, source_target_pairs={{1,2},{3,4},{5,6},{2,1},{4,3},{6,5},{9,10},{11,12},{13,14},{10,9},... | collective-permute-start | bytes 1081352 | tf_op jit(solution)/shard_map/ppermute | solution.py:46
  10.5 0.0 copy-done.8
  10.5 1.4 %collective-permute-start = (f32[704,128]{1,0:T(8,128)S(1)}, f32[704,128]{1,0:T(8,128)S(1)}, u32[]{:S(2)}, u32[]{:S(2)}) collective-permute-start(f32[704,128]{1,0:T(8,128)S(1)} %copy-done.8), channel_id=1, source_target_pairs={{0,1},{2,3},{4,5},{6,7},{1,0},{3,2},{5,4},{7,6},{8,9},{10,11},{12,... | collective-permute-start | bytes 1081352 | tf_op jit(solution)/shard_map/ppermute | solution.py:45
  12.0 0.0 copy-done
  12.0 0.0 copy-done.5
  12.0 0.0 copy-done.4
  12.0 0.0 copy-done.7
  12.0 0.0 copy-done.6
  12.0 0.0 copy-done.1
  12.0 0.0 copy-done.2
  12.0 6.1 %ready_own.1 = (f32[4576,128]{1,0:T(8,128)S(1)}, f32[4576,128]{1,0:T(8,128)S(1)}, f32[4576,128]{1,0:T(8,128)S(1)}, f32[4576,128]{1,0:T(8,128)S(1)}, f32[4576,128...) custom-call(s32[16,32,512]{2,1,0:T(8,128)S(1)} %copy-done, ...), custom_call_target="tpu_custom_call" | custom-call | bytes 25165824 | tf_op jit(solution)/shard_map/ready_own/pallas_call | solution.py:401
  18.1 0.6 %collective-permute-done.1.yb_ref = f32[704,128]{1,0:T(8,128)S(1)} collective-permute-done((f32[704,128]{1,0:T(8,128)}, f32[704,128]{1,0:T(8,128)S(1)}, u32[]{:S(2)}, u32[]{:S(2)}) %collective-permute-start.1) | collective-permute-done | bytes 360480 | tf_op jit(solution)/shard_map/ppermute | solution.py:46
  18.7 9.9 %collective-permute-done.ya_ref = f32[704,128]{1,0:T(8,128)S(1)} collective-permute-done((f32[704,128]{1,0:T(8,128)S(1)}, f32[704,128]{1,0:T(8,128)S(1)}, u32[]{:S(2)}, u32[]{:S(2)}) %collective-permute-start) | collective-permute-done | bytes 360480 | tf_op jit(solution)/shard_map/ppermute | solution.py:45
  28.6 0.2 corners.1
  28.7 0.6 collective-permute-start.2
  29.3 0.7 %collective-permute-start.3 = (f32[256,128]{1,0:T(8,128)S(1)}, f32[256,128]{1,0:T(8,128)S(1)}, u32[]{:S(2)}, u32[]{:S(2)}) collective-permute-start(f32[256,128]{1,0:T(8,128)S(1)} %get-tuple-element.42), channel_id=1, source_target_pairs={{8,16},{16,8},{9,17},{17,9},{10,18},{18,10},{11,19},{19,11},{12,20... | collective-permute-start | bytes 393224 | tf_op jit(solution)/shard_map/ppermute | solution.py:46
  30.0 0.0 collective-permute-done.4.xa_ref
  30.0 0.0 collective-permute-done.5.xb_ref
  30.0 0.0 copy-start.3
  30.0 2.9 %ready_ends.1 = (f32[4576,128]{1,0:T(8,128)S(1)}, f32[4576,128]{1,0:T(8,128)S(1)}, f32[4576,128]{1,0:T(8,128)S(1)}, f32[4576,128]{1,0:T(8,128)S(1)}, f32[4576,12...) custom-call(f32[4,10,32,128]{3,2,1,0:T(8,128)S(1)} %collective-permu, ...), custom_call_target="tpu_custom_call", output_to_operand_aliasing={{0}: (7, {}), {1}: (8, {}), {2}: (9, {}), {3}: (10, {}), {4... | custom-call | bytes 9437184 | tf_op jit(solution)/shard_map/ready_ends/pallas_call | solution.py:463
  32.9 0.0 collective-permute-done.2.ca_ref
  32.9 0.0 collective-permute-done.3.cb_ref
  33.0 0.0 copy-done.3
  33.0 10.3 %flow.1 = (f32[4576,128]{1,0:T(8,128)S(1)}, f32[4576,128]{1,0:T(8,128)S(1)}, f32[4576,128]{1,0:T(8,128)S(1)}, f32[4576,128]{1,0:T(8,128)S(1)}, f32[4576,128]{1,0...) custom-call(f32[16,32,512]{2,1,0:T(8,128)S(1)} %copy-done.3, ...), custom_call_target="tpu_custom_call", output_to_operand_aliasing={{0}: (10, {}), {1}: (11, {}), {2}: (12, {}), {3}: (13, {}),... | custom-call | tf_op jit(solution)/shard_map/flow/pallas_call | solution.py:607
  43.3 0.7 %collective-permute-start.6 = (f32[128,128]{1,0:T(8,128)S(1)}, f32[128,128]{1,0:T(8,128)S(1)}, u32[]{:S(2)}, u32[]{:S(2)}) collective-permute-start(f32[128,128]{1,0:T(8,128)S(1)} %get-tuple-element.66), channel_id=1, source_target_pairs={{0,8},{1,9},{2,10},{3,11},{4,12},{5,13},{6,14},{7,15}} | collective-permute-start | bytes 196616 | tf_op jit(solution)/shard_map/ppermute | solution.py:723
  43.9 0.0 collective-permute-done.6.inflow_ref
  44.0 0.7 %collective-permute-start.7 = (f32[128,128]{1,0:T(8,128)S(1)}, f32[128,128]{1,0:T(8,128)S(1)}, u32[]{:S(2)}, u32[]{:S(2)}) collective-permute-start(f32[128,128]{1,0:T(8,128)S(1)} %get-tuple-element.68), channel_id=1, source_target_pairs={{8,16},{9,17},{10,18},{11,19},{12,20},{13,21},{14,22},{15,23}} | collective-permute-start | bytes 196616 | tf_op jit(solution)/shard_map/ppermute | solution.py:723
  44.6 0.0 collective-permute-done.7.inflow_ref
  44.7 1.3 %collective-permute-start.8 = (f32[128,128]{1,0:T(8,128)S(1)}, f32[128,128]{1,0:T(8,128)S(1)}, u32[]{:S(2)}, u32[]{:S(2)}) collective-permute-start(f32[128,128]{1,0:T(8,128)S(1)} %get-tuple-element.70), channel_id=1, source_target_pairs={{16,24},{17,25},{18,26},{19,27},{20,28},{21,29},{22,30},{23,31}} | collective-permute-start | bytes 196616 | tf_op jit(solution)/shard_map/ppermute | solution.py:723
  46.0 12.7 %collective-permute-done.8.inflow_ref = f32[128,128]{1,0:T(8,128)S(1)} collective-permute-done((f32[128,128]{1,0:T(8,128)S(1)}, f32[128,128]{1,0:T(8,128)S(1)}, u32[]{:S(2)}, u32[]{:S(2)}) %collective-permute-start.8) | collective-permute-done | bytes 65568 | tf_op jit(solution)/shard_map/ppermute | solution.py:723
  58.7 2.5 %stage.7 = f32[16,32,512]{2,1,0:T(8,128)} custom-call(f32[128,128]{1,0:T(8,128)S(1)} %collective-permute-done.8.inflow_ref, f32[16,640,128]{2,1,0:T(8,128)S(1)} %get-tuple-element.65.prep_ref, f32[4,16,32,128]{3,2,1,0:T(8,128)S(1)} %get-tuple-element.71.refs_0_), custom_call_target="tpu_custom_call" | custom-call | tf_op jit(solution)/shard_map/stage/pallas_call | solution.py:691
  (3 shorter events, 0.1 us)
Async XLA Ops:
  0.6 11.3 %copy-start = (s32[16,32,512]{2,1,0:T(8,128)S(1)}, s32[16,32,512]{2,1,0:T(8,128)}, u32[]{:S(2)}) copy-start(s32[16,32,512]{2,1,0:T(8,128)} %rock_ref.5) | copy-start | bytes 3145732
  0.6 11.3 %copy-start.5 = (f32[8]{0:T(128)S(1)}, f32[8]{0:T(128)}, u32[]{:S(2)}) copy-start(f32[8]{0:T(128)} %poro_ref.5) | copy-start | bytes 100
  0.7 11.3 %copy-start.4 = (f32[8]{0:T(128)S(1)}, f32[8]{0:T(128)}, u32[]{:S(2)}) copy-start(f32[8]{0:T(128)} %perm_ref.5) | copy-start | bytes 100
  0.7 11.3 %copy-start.7 = (f32[128]{0:T(128)S(1)}, f32[128]{0:T(128)}, u32[]{:S(2)}) copy-start(f32[128]{0:T(128)} %well_ref.1) | copy-start | bytes 1540
  0.7 11.3 %copy-start.6 = (s32[3,128]{1,0:T(4,128)S(1)}, s32[3,128]{1,0:T(4,128)}, u32[]{:S(2)}) copy-start(s32[3,128]{1,0:T(4,128)} %cells_ref.1) | copy-start | bytes 4612
  3.3 7.3 %copy-start.8 = (f32[704,128]{1,0:T(8,128)S(1)}, f32[704,128]{1,0:T(8,128)}, u32[]{:S(2)}) copy-start(f32[704,128]{1,0:T(8,128)} %get-tuple-element.38._) | copy-start | bytes 1081348
  3.3 8.7 %copy-start.1 = (f32[16,32,512]{2,1,0:T(8,128)S(1)}, f32[16,32,512]{2,1,0:T(8,128)}, u32[]{:S(2)}) copy-start(f32[16,32,512]{2,1,0:T(8,128)} %p_ref.5) | copy-start | bytes 3145732
  3.3 8.7 %copy-start.2 = (f32[16,32,512]{2,1,0:T(8,128)S(1)}, f32[16,32,512]{2,1,0:T(8,128)}, u32[]{:S(2)}) copy-start(f32[16,32,512]{2,1,0:T(8,128)} %sat_ref.3) | copy-start | bytes 3145732
  6.0 23.9 %collective-permute-start.4 = (f32[4,10,32,128]{3,2,1,0:T(8,128)}, f32[4,10,32,128]{3,2,1,0:T(8,128)S(1)}, u32[]{:S(2)}, u32[]{:S(2)}) collective-permute-start(f32[4,10,32,128]{3,2,1,0:T(8,128)} %get-tuple-element.44), channel_id=1, source_target_pairs={{0,8},{16,24},{8,0},{24,16},{1,9},{17,25},{9,1},{25,17},{2,10},{18... | collective-permute-start | bytes 1966088 | tf_op jit(solution)/shard_map/ppermute | solution.py:45
  6.8 23.2 %collective-permute-start.5 = (f32[4,10,32,128]{3,2,1,0:T(8,128)}, f32[4,10,32,128]{3,2,1,0:T(8,128)S(1)}, u32[]{:S(2)}, u32[]{:S(2)}) collective-permute-start(f32[4,10,32,128]{3,2,1,0:T(8,128)} %get-tuple-element.45), channel_id=1, source_target_pairs={{8,16},{16,8},{9,17},{17,9},{10,18},{18,10},{11,19},{19,11},{12,20... | collective-permute-start | bytes 1966088 | tf_op jit(solution)/shard_map/ppermute | solution.py:46
  7.5 11.2 %collective-permute-start.1 = (f32[704,128]{1,0:T(8,128)}, f32[704,128]{1,0:T(8,128)S(1)}, u32[]{:S(2)}, u32[]{:S(2)}) collective-permute-start(f32[704,128]{1,0:T(8,128)} %get-tuple-element.39), channel_id=1, source_target_pairs={{1,2},{3,4},{5,6},{2,1},{4,3},{6,5},{9,10},{11,12},{13,14},{10,9},... | collective-permute-start | bytes 1081352 | tf_op jit(solution)/shard_map/ppermute | solution.py:46
  10.5 18.0 %collective-permute-start = (f32[704,128]{1,0:T(8,128)S(1)}, f32[704,128]{1,0:T(8,128)S(1)}, u32[]{:S(2)}, u32[]{:S(2)}) collective-permute-start(f32[704,128]{1,0:T(8,128)S(1)} %copy-done.8), channel_id=1, source_target_pairs={{0,1},{2,3},{4,5},{6,7},{1,0},{3,2},{5,4},{7,6},{8,9},{10,11},{12,... | collective-permute-start | bytes 1081352 | tf_op jit(solution)/shard_map/ppermute | solution.py:45
  28.7 4.2 %collective-permute-start.2 = (f32[256,128]{1,0:T(8,128)S(1)}, f32[256,128]{1,0:T(8,128)S(1)}, u32[]{:S(2)}, u32[]{:S(2)}) collective-permute-start(f32[256,128]{1,0:T(8,128)S(1)} %get-tuple-element.41), channel_id=1, source_target_pairs={{0,8},{16,24},{8,0},{24,16},{1,9},{17,25},{9,1},{25,17},{2,10},{18... | collective-permute-start | bytes 393224 | tf_op jit(solution)/shard_map/ppermute | solution.py:45
  29.3 3.7 %collective-permute-start.3 = (f32[256,128]{1,0:T(8,128)S(1)}, f32[256,128]{1,0:T(8,128)S(1)}, u32[]{:S(2)}, u32[]{:S(2)}) collective-permute-start(f32[256,128]{1,0:T(8,128)S(1)} %get-tuple-element.42), channel_id=1, source_target_pairs={{8,16},{16,8},{9,17},{17,9},{10,18},{18,10},{11,19},{19,11},{12,20... | collective-permute-start | bytes 393224 | tf_op jit(solution)/shard_map/ppermute | solution.py:46
  30.0 3.0 %copy-start.3 = (f32[16,32,512]{2,1,0:T(8,128)S(1)}, f32[16,32,512]{2,1,0:T(8,128)}, u32[]{:S(2)}) copy-start(f32[16,32,512]{2,1,0:T(8,128)} %flux_ref.1) | copy-start | bytes 3145732
  43.3 0.7 %collective-permute-start.6 = (f32[128,128]{1,0:T(8,128)S(1)}, f32[128,128]{1,0:T(8,128)S(1)}, u32[]{:S(2)}, u32[]{:S(2)}) collective-permute-start(f32[128,128]{1,0:T(8,128)S(1)} %get-tuple-element.66), channel_id=1, source_target_pairs={{0,8},{1,9},{2,10},{3,11},{4,12},{5,13},{6,14},{7,15}} | collective-permute-start | bytes 196616 | tf_op jit(solution)/shard_map/ppermute | solution.py:723
  44.0 0.7 %collective-permute-start.7 = (f32[128,128]{1,0:T(8,128)S(1)}, f32[128,128]{1,0:T(8,128)S(1)}, u32[]{:S(2)}, u32[]{:S(2)}) collective-permute-start(f32[128,128]{1,0:T(8,128)S(1)} %get-tuple-element.68), channel_id=1, source_target_pairs={{8,16},{9,17},{10,18},{11,19},{12,20},{13,21},{14,22},{15,23}} | collective-permute-start | bytes 196616 | tf_op jit(solution)/shard_map/ppermute | solution.py:723
  44.7 14.0 %collective-permute-start.8 = (f32[128,128]{1,0:T(8,128)S(1)}, f32[128,128]{1,0:T(8,128)S(1)}, u32[]{:S(2)}, u32[]{:S(2)}) collective-permute-start(f32[128,128]{1,0:T(8,128)S(1)} %get-tuple-element.70), channel_id=1, source_target_pairs={{16,24},{17,25},{18,26},{19,27},{20,28},{21,29},{22,30},{23,31}} | collective-permute-start | bytes 196616 | tf_op jit(solution)/shard_map/ppermute | solution.py:723

commit v6 on v5

--- a/solution.py
+++ b/solution.py
@@ -20,8 +20,8 @@
 LANES = 128
 STAGE_UNROLL = 2
 UNROLL = 4
-ENDS_LIMIT = 59 << 20
-SIDES_LIMIT = 62 << 20
+ENDS_LIMIT = 4 << 20
+SIDES_LIMIT = 6 << 20
 OWN_LIMIT = 5 << 20
 FLOW_LIMIT = 8 << 20
 REACH = PASSES + 1
@@ -706,6 +706,10 @@
 
 def step(rock_type, rock_perm, rock_poro, base_flux, initial_pressure, old_saturation, well_cells, well_rates):
     nx = rock_type.shape[0]
+    initial_pressure, rock_type, old_saturation, base_flux = (
+        pltpu.with_memory_space_constraint(f, pltpu.MemorySpace.HBM)
+        for f in (initial_pressure, rock_type, old_saturation, base_flux)
+    )
     sides = pack_sides(initial_pressure, rock_type, old_saturation)
     sides_got = swap(*sides, "gy")
     ends = swap(*pack_ends(initial_pressure, rock_type, sides[0]), "gx")

time: 61.5 us -> 59.1 us (0.961)
  the two profiles are of different devices: /device:TPU:11 before, /device:TPU:7 now
where the time goes in v6:
time: 59.1 us; the launch traced here: 58.7 us
  Pallas kernels  24.9 us (42%)
  waiting for transfers between devices  24.5 us (41%)
  starting transfers between devices  8.48 us (14%)
  between operations  0.86 us (1%)
    ppermute x3, waiting for transfers between devices, step(): inflow = lax.ppermute(outflow, 'gx', [(stage, stage + 1)])  12.7 us
    pallas_call x1, Pallas kernels, flow(): pl.pallas_call(functools.partial(flow_kernel, block), name='flow', out_sh...  10.1 us
    ppermute x3, waiting for transfers between devices, swap(): got_a = lax.ppermute(value_a, axis, pairs_a)  9.86 us
    pallas_call x1, Pallas kernels, ready_own(): pl.pallas_call(functools.partial(ready_own_kernel, block), name='ready_ow...  5.82 us
    ppermute x3, starting transfers between devices, swap(): got_b = lax.ppermute(value_b, axis, pairs_b)  4.49 us
    pallas_call x1, Pallas kernels, ready_ends(): pl.pallas_call(functools.partial(ready_ends_kernel, block), name='ready_e...  2.95 us
    ppermute x3, starting transfers between devices, step(): inflow = lax.ppermute(outflow, 'gx', [(stage, stage + 1)])  2.62 us
    pallas_call x4, Pallas kernels, run_stage(): pl.pallas_call(functools.partial(stage_kernel, stage, last), name='stage'...  2.56 us
  transfers between devices with their start and end apart: 9, of which 3 were waited for; matrix products, arithmetic and copies ran while one was open for 0% of the time, Pallas kernels for 15%

profile of v6, /device:TPU:7, one launch (start us, length us, event | category | flops | bytes accessed | tf_op | source)
XLA Modules:
  0.0 58.7 jit_solution(7532153520951099746)
XLA Ops:
  0.6 0.0 copy-start.1
  0.6 0.0 copy-start
  0.7 0.0 copy-start.3
  0.7 0.0 copy-start.2
  0.7 1.7 %pack_sides.1 = (f32[704,128]{1,0:T(8,128)S(1)}, f32[704,128]{1,0:T(8,128)S(1)}) custom-call(f32[16,32,512]{2,1,0:T(8,128)} %p_ref.5, s32[16,32,512]{2,1,0:T(8,128)} %rock_ref.5, f32[16,32,512]{2,1,0:T(8,128)} %sat_ref.3), custom_call_target="tpu_custom_call" | custom-call | tf_op jit(solution)/shard_map/pack_sides/pallas_call | solution.py:95
  2.4 1.5 %pack_ends.1 = (f32[4,10,32,128]{3,2,1,0:T(8,128)S(1)}, f32[4,10,32,128]{3,2,1,0:T(8,128)S(1)}) custom-call(f32[16,32,512]{2,1,0:T(8,128)} %p_ref.5, s32[16,32,512]{2,1,0:T(8,128)} %rock_ref.5, f32[704,128]{1,0:T(8,128)S(1)} %get-tuple-element.38._), custom_call_target="tpu_custom_call" | custom-call | tf_op jit(solution)/shard_map/pack_ends/pallas_call | solution.py:140
  4.0 0.7 %collective-permute-start.4 = (f32[4,10,32,128]{3,2,1,0:T(8,128)S(1)}, f32[4,10,32,128]{3,2,1,0:T(8,128)S(1)}, u32[]{:S(2)}, u32[]{:S(2)}) collective-permute-start(f32[4,10,32,128]{3,2,1,0:T(8,128)S(1)} %get-tuple-element.44), channel_id=1, source_target_pairs={{0,8},{16,24},{8,0},{24,16},{1,9},{17,25},{9,1},{25,17},{2,10},{18... | collective-permute-start | bytes 1966088 | tf_op jit(solution)/shard_map/ppermute | solution.py:45
  4.7 0.7 %collective-permute-start.5 = (f32[4,10,32,128]{3,2,1,0:T(8,128)S(1)}, f32[4,10,32,128]{3,2,1,0:T(8,128)S(1)}, u32[]{:S(2)}, u32[]{:S(2)}) collective-permute-start(f32[4,10,32,128]{3,2,1,0:T(8,128)S(1)} %get-tuple-element.45), channel_id=1, source_target_pairs={{8,16},{16,8},{9,17},{17,9},{10,18},{18,10},{11,19},{19,11},{12,20... | collective-permute-start | bytes 1966088 | tf_op jit(solution)/shard_map/ppermute | solution.py:46
  5.4 3.1 %collective-permute-start.1 = (f32[704,128]{1,0:T(8,128)S(1)}, f32[704,128]{1,0:T(8,128)S(1)}, u32[]{:S(2)}, u32[]{:S(2)}) collective-permute-start(f32[704,128]{1,0:T(8,128)S(1)} %get-tuple-element.39), channel_id=1, source_target_pairs={{1,2},{3,4},{5,6},{2,1},{4,3},{6,5},{9,10},{11,12},{13,14},{10,9},... | collective-permute-start | bytes 1081352 | tf_op jit(solution)/shard_map/ppermute | solution.py:46
  8.5 0.1 collective-permute-start
  8.6 0.0 copy-done.1
  8.6 0.0 copy-done
  8.6 0.0 copy-done.3
  8.7 0.0 copy-done.2
  8.7 5.8 %ready_own.1 = (f32[4576,128]{1,0:T(8,128)S(1)}, f32[4576,128]{1,0:T(8,128)S(1)}, f32[4576,128]{1,0:T(8,128)S(1)}, f32[4576,128]{1,0:T(8,128)S(1)}, f32[4576,128...) custom-call(s32[16,32,512]{2,1,0:T(8,128)} %rock_ref.5, ...), custom_call_target="tpu_custom_call" | custom-call | bytes 25165824 | tf_op jit(solution)/shard_map/ready_own/pallas_call | solution.py:401
  14.5 1.9 %collective-permute-done.1.yb_ref = f32[704,128]{1,0:T(8,128)S(1)} collective-permute-done((f32[704,128]{1,0:T(8,128)S(1)}, f32[704,128]{1,0:T(8,128)S(1)}, u32[]{:S(2)}, u32[]{:S(2)}) %collective-permute-start.1) | collective-permute-done | bytes 360480 | tf_op jit(solution)/shard_map/ppermute | solution.py:46
  16.4 9.9 %collective-permute-done.ya_ref = f32[704,128]{1,0:T(8,128)S(1)} collective-permute-done((f32[704,128]{1,0:T(8,128)S(1)}, f32[704,128]{1,0:T(8,128)S(1)}, u32[]{:S(2)}, u32[]{:S(2)}) %collective-permute-start) | collective-permute-done | bytes 360480 | tf_op jit(solution)/shard_map/ppermute | solution.py:45
  26.2 0.2 corners.1
  26.4 0.6 collective-permute-start.2
  27.0 0.7 %collective-permute-start.3 = (f32[256,128]{1,0:T(8,128)S(1)}, f32[256,128]{1,0:T(8,128)S(1)}, u32[]{:S(2)}, u32[]{:S(2)}) collective-permute-start(f32[256,128]{1,0:T(8,128)S(1)} %get-tuple-element.42), channel_id=1, source_target_pairs={{8,16},{16,8},{9,17},{17,9},{10,18},{18,10},{11,19},{19,11},{12,20... | collective-permute-start | bytes 393224 | tf_op jit(solution)/shard_map/ppermute | solution.py:46
  27.6 0.0 collective-permute-done.4.xa_ref
  27.7 0.0 collective-permute-done.5.xb_ref
  27.7 2.9 %ready_ends.1 = (f32[4576,128]{1,0:T(8,128)S(1)}, f32[4576,128]{1,0:T(8,128)S(1)}, f32[4576,128]{1,0:T(8,128)S(1)}, f32[4576,128]{1,0:T(8,128)S(1)}, f32[4576,12...) custom-call(f32[4,10,32,128]{3,2,1,0:T(8,128)S(1)} %collective-permu, ...), custom_call_target="tpu_custom_call", output_to_operand_aliasing={{0}: (7, {}), {1}: (8, {}), {2}: (9, {}), {3}: (10, {}), {4... | custom-call | bytes 9437184 | tf_op jit(solution)/shard_map/ready_ends/pallas_call | solution.py:463
  30.6 0.0 collective-permute-done.2.ca_ref
  30.6 0.0 collective-permute-done.3.cb_ref
  30.6 10.1 %flow.1 = (f32[4576,128]{1,0:T(8,128)S(1)}, f32[4576,128]{1,0:T(8,128)S(1)}, f32[4576,128]{1,0:T(8,128)S(1)}, f32[4576,128]{1,0:T(8,128)S(1)}, f32[4576,128]{1,0...) custom-call(f32[16,32,512]{2,1,0:T(8,128)} %flux_ref.1, ...), custom_call_target="tpu_custom_call", output_to_operand_aliasing={{0}: (10, {}), {1}: (11, {}), {2}: (12, {}), {3}: (13, {}),... | custom-call | tf_op jit(solution)/shard_map/flow/pallas_call | solution.py:607
  40.8 0.7 %collective-permute-start.6 = (f32[128,128]{1,0:T(8,128)S(1)}, f32[128,128]{1,0:T(8,128)S(1)}, u32[]{:S(2)}, u32[]{:S(2)}) collective-permute-start(f32[128,128]{1,0:T(8,128)S(1)} %get-tuple-element.66), channel_id=1, source_target_pairs={{0,8},{1,9},{2,10},{3,11},{4,12},{5,13},{6,14},{7,15}} | collective-permute-start | bytes 196616 | tf_op jit(solution)/shard_map/ppermute | solution.py:727
  41.5 0.0 collective-permute-done.6.inflow_ref
  41.5 0.7 %collective-permute-start.7 = (f32[128,128]{1,0:T(8,128)S(1)}, f32[128,128]{1,0:T(8,128)S(1)}, u32[]{:S(2)}, u32[]{:S(2)}) collective-permute-start(f32[128,128]{1,0:T(8,128)S(1)} %get-tuple-element.68), channel_id=1, source_target_pairs={{8,16},{9,17},{10,18},{11,19},{12,20},{13,21},{14,22},{15,23}} | collective-permute-start | bytes 196616 | tf_op jit(solution)/shard_map/ppermute | solution.py:727
  42.2 0.0 collective-permute-done.7.inflow_ref
  42.2 1.3 %collective-permute-start.8 = (f32[128,128]{1,0:T(8,128)S(1)}, f32[128,128]{1,0:T(8,128)S(1)}, u32[]{:S(2)}, u32[]{:S(2)}) collective-permute-start(f32[128,128]{1,0:T(8,128)S(1)} %get-tuple-element.70), channel_id=1, source_target_pairs={{16,24},{17,25},{18,26},{19,27},{20,28},{21,29},{22,30},{23,31}} | collective-permute-start | bytes 196616 | tf_op jit(solution)/shard_map/ppermute | solution.py:727
  43.5 12.7 %collective-permute-done.8.inflow_ref = f32[128,128]{1,0:T(8,128)S(1)} collective-permute-done((f32[128,128]{1,0:T(8,128)S(1)}, f32[128,128]{1,0:T(8,128)S(1)}, u32[]{:S(2)}, u32[]{:S(2)}) %collective-permute-start.8) | collective-permute-done | bytes 65568 | tf_op jit(solution)/shard_map/ppermute | solution.py:727
  56.2 2.5 %stage.7 = f32[16,32,512]{2,1,0:T(8,128)} custom-call(f32[128,128]{1,0:T(8,128)S(1)} %collective-permute-done.8.inflow_ref, f32[16,640,128]{2,1,0:T(8,128)S(1)} %get-tuple-element.65.prep_ref, f32[4,16,32,128]{3,2,1,0:T(8,128)S(1)} %get-tuple-element.71.refs_0_), custom_call_target="tpu_custom_call" | custom-call | tf_op jit(solution)/shard_map/stage/pallas_call | solution.py:691
  (3 shorter events, 0.1 us)
Async XLA Ops:
  0.6 8.0 %copy-start.1 = (f32[8]{0:T(128)S(1)}, f32[8]{0:T(128)}, u32[]{:S(2)}) copy-start(f32[8]{0:T(128)} %poro_ref.5) | copy-start | bytes 100
  0.6 8.0 %copy-start = (f32[8]{0:T(128)S(1)}, f32[8]{0:T(128)}, u32[]{:S(2)}) copy-start(f32[8]{0:T(128)} %perm_ref.5) | copy-start | bytes 100
  0.7 8.0 %copy-start.3 = (f32[128]{0:T(128)S(1)}, f32[128]{0:T(128)}, u32[]{:S(2)}) copy-start(f32[128]{0:T(128)} %well_ref.1) | copy-start | bytes 1540
  0.7 8.0 %copy-start.2 = (s32[3,128]{1,0:T(4,128)S(1)}, s32[3,128]{1,0:T(4,128)}, u32[]{:S(2)}) copy-start(s32[3,128]{1,0:T(4,128)} %cells_ref.1) | copy-start | bytes 4612
  4.0 23.7 %collective-permute-start.4 = (f32[4,10,32,128]{3,2,1,0:T(8,128)S(1)}, f32[4,10,32,128]{3,2,1,0:T(8,128)S(1)}, u32[]{:S(2)}, u32[]{:S(2)}) collective-permute-start(f32[4,10,32,128]{3,2,1,0:T(8,128)S(1)} %get-tuple-element.44), channel_id=1, source_target_pairs={{0,8},{16,24},{8,0},{24,16},{1,9},{17,25},{9,1},{25,17},{2,10},{18... | collective-permute-start | bytes 1966088 | tf_op jit(solution)/shard_map/ppermute | solution.py:45
  4.7 23.0 %collective-permute-start.5 = (f32[4,10,32,128]{3,2,1,0:T(8,128)S(1)}, f32[4,10,32,128]{3,2,1,0:T(8,128)S(1)}, u32[]{:S(2)}, u32[]{:S(2)}) collective-permute-start(f32[4,10,32,128]{3,2,1,0:T(8,128)S(1)} %get-tuple-element.45), channel_id=1, source_target_pairs={{8,16},{16,8},{9,17},{17,9},{10,18},{18,10},{11,19},{19,11},{12,20... | collective-permute-start | bytes 1966088 | tf_op jit(solution)/shard_map/ppermute | solution.py:46
  5.4 11.0 %collective-permute-start.1 = (f32[704,128]{1,0:T(8,128)S(1)}, f32[704,128]{1,0:T(8,128)S(1)}, u32[]{:S(2)}, u32[]{:S(2)}) collective-permute-start(f32[704,128]{1,0:T(8,128)S(1)} %get-tuple-element.39), channel_id=1, source_target_pairs={{1,2},{3,4},{5,6},{2,1},{4,3},{6,5},{9,10},{11,12},{13,14},{10,9},... | collective-permute-start | bytes 1081352 | tf_op jit(solution)/shard_map/ppermute | solution.py:46
  8.5 17.7 %collective-permute-start = (f32[704,128]{1,0:T(8,128)S(1)}, f32[704,128]{1,0:T(8,128)S(1)}, u32[]{:S(2)}, u32[]{:S(2)}) collective-permute-start(f32[704,128]{1,0:T(8,128)S(1)} %get-tuple-element.38._), channel_id=1, source_target_pairs={{0,1},{2,3},{4,5},{6,7},{1,0},{3,2},{5,4},{7,6},{8,9},{10,11},{12,... | collective-permute-start | bytes 1081352 | tf_op jit(solution)/shard_map/ppermute | solution.py:45
  26.4 4.2 %collective-permute-start.2 = (f32[256,128]{1,0:T(8,128)S(1)}, f32[256,128]{1,0:T(8,128)S(1)}, u32[]{:S(2)}, u32[]{:S(2)}) collective-permute-start(f32[256,128]{1,0:T(8,128)S(1)} %get-tuple-element.41), channel_id=1, source_target_pairs={{0,8},{16,24},{8,0},{24,16},{1,9},{17,25},{9,1},{25,17},{2,10},{18... | collective-permute-start | bytes 393224 | tf_op jit(solution)/shard_map/ppermute | solution.py:45
  27.0 3.7 %collective-permute-start.3 = (f32[256,128]{1,0:T(8,128)S(1)}, f32[256,128]{1,0:T(8,128)S(1)}, u32[]{:S(2)}, u32[]{:S(2)}) collective-permute-start(f32[256,128]{1,0:T(8,128)S(1)} %get-tuple-element.42), channel_id=1, source_target_pairs={{8,16},{16,8},{9,17},{17,9},{10,18},{18,10},{11,19},{19,11},{12,20... | collective-permute-start | bytes 393224 | tf_op jit(solution)/shard_map/ppermute | solution.py:46
  40.8 0.7 %collective-permute-start.6 = (f32[128,128]{1,0:T(8,128)S(1)}, f32[128,128]{1,0:T(8,128)S(1)}, u32[]{:S(2)}, u32[]{:S(2)}) collective-permute-start(f32[128,128]{1,0:T(8,128)S(1)} %get-tuple-element.66), channel_id=1, source_target_pairs={{0,8},{1,9},{2,10},{3,11},{4,12},{5,13},{6,14},{7,15}} | collective-permute-start | bytes 196616 | tf_op jit(solution)/shard_map/ppermute | solution.py:727
  41.5 0.7 %collective-permute-start.7 = (f32[128,128]{1,0:T(8,128)S(1)}, f32[128,128]{1,0:T(8,128)S(1)}, u32[]{:S(2)}, u32[]{:S(2)}) collective-permute-start(f32[128,128]{1,0:T(8,128)S(1)} %get-tuple-element.68), channel_id=1, source_target_pairs={{8,16},{9,17},{10,18},{11,19},{12,20},{13,21},{14,22},{15,23}} | collective-permute-start | bytes 196616 | tf_op jit(solution)/shard_map/ppermute | solution.py:727
  42.2 14.0 %collective-permute-start.8 = (f32[128,128]{1,0:T(8,128)S(1)}, f32[128,128]{1,0:T(8,128)S(1)}, u32[]{:S(2)}, u32[]{:S(2)}) collective-permute-start(f32[128,128]{1,0:T(8,128)S(1)} %get-tuple-element.70), channel_id=1, source_target_pairs={{16,24},{17,25},{18,26},{19,27},{20,28},{21,29},{22,30},{23,31}} | collective-permute-start | bytes 196616 | tf_op jit(solution)/shard_map/ppermute | solution.py:727
